TPU v7x, 512 devices: a whole 4x8x8 slice. The times are simulated.
512 devices in a mesh: scen: 8 (over x, y_hi), grid: 64 (over y_lo, z, core).
Axes of the slice: x: 4, y: 8 (y_hi: 2, y_lo: 4; y = y_hi * 4 + y_lo), z: 8, core: 2. Of those that a mesh axis runs over, the one named last changes fastest.
Arguments:
- forward_states: float32 [8, 4, 64, 256, 512], P('scen', None, 'grid'), may hold values from -6 to 6
- kappa: float32 [64, 256, 512], P('grid'), may hold values from 0.02 to 0.08
- courant: float32 [64, 256, 512], P('grid'), may hold values from 0.1 to 0.45
- direction: float32 [64, 256, 512], P('grid'), may hold values from -6 to 6
- obs_index: int32 [8, 262144], P('scen', 'grid'), may hold values from 0 to 131071
- obs_weight: float32 [8, 262144], P('scen', 'grid'), may hold values from 0.5 to 4
Outputs:
- hess_vec: float32 [64, 256, 512], P('grid', 'scen')
Inputs may be any that keep to these rules, and one draw needn't show every extreme that they name: `obs_index`: an index names a cell of the slab of 1 x 256 x 512 cells that belongs to its block of 4096 observations.
All inputs are finite; a program needn't handle non-finite values.
Results may differ from a plain program's by a relative error of at most 0.00002.
Values sent between devices are 32-bit elements; how exact they have to be, the bound alone decides.
No kernel may reach another device: no remote copies, remote signals or barrier semaphores. Data moves between devices by JAX's collectives and lax.ppermute only.
A program may use at most 64 MiB of HBM per device.

v0:
```python
import jax
import jax.numpy as jnp
from jax import lax
from jax.sharding import PartitionSpec as P

source_gain = 0.2
prior_gain = 0.5
prior_reach = 0.1


def padded_2(block, sides, width):
    for axis, dim in sides:
        count = lax.axis_size(axis)
        forward = [(i, i + 1) for i in range(count - 1)]
        backward = [(target, source) for source, target in forward]
        low = lax.ppermute(
            lax.slice_in_dim(block, block.shape[dim] - width, None, axis=dim), axis, forward
        )
        high = lax.ppermute(lax.slice_in_dim(block, 0, width, axis=dim), axis, backward)
        block = jnp.concatenate([low, block, high], axis=dim)
    return block


def laplace(padded):
    inner = padded[..., 1:-1, :, :]
    widths = [(0, 0)] * (inner.ndim - 2) + [(1, 1), (1, 1)]
    side = jnp.pad(inner, widths)
    total = padded[..., 2:, :, :] + padded[..., :-2, :, :]
    total = total + side[..., 2:, 1:-1] + side[..., :-2, 1:-1]
    total = total + side[..., 1:-1, 2:] + side[..., 1:-1, :-2]
    return total - 6.0 * inner


def local(forward_states, kappa, courant, direction, obs_index, obs_weight):
    states = forward_states[0]
    steps = states.shape[0]
    stacked = jnp.concatenate([direction[None], states], 0)
    padded_all = padded_2(stacked, (("grid", 1),), 1)
    leading = padded_all.shape[0] - steps
    lap_states = laplace(padded_all[leading:])
    tangent = source_gain * direction * lap_states[0]
    for step in range(1, steps):
        padded = padded_2(tangent, (("grid", 0),), 1)
        tangent = (
            tangent
            + kappa * laplace(padded)
            - courant * (tangent - padded[:-2])
            + source_gain * direction * lap_states[step]
        )
    cells = tangent.size
    index = obs_index[0]
    values = tangent.reshape(-1)[index] * obs_weight[0]
    adjoint = jnp.zeros((cells,), jnp.float32).at[index].add(values).reshape(tangent.shape)
    terms = [source_gain * lap_states[steps - 1] * adjoint]
    for step in range(steps - 2, -1, -1):
        paired = padded_2(jnp.stack([kappa * adjoint, courant * adjoint]), (("grid", 1),), 1)
        weighted = paired[0]
        carried = paired[1]
        adjoint = adjoint + laplace(weighted) - (courant * adjoint - carried[2:])
        terms.append(source_gain * lap_states[step] * adjoint)
    partial_value = terms[0]
    for term in terms[1:]:
        partial_value = partial_value + term
    reduced = lax.psum_scatter(partial_value, "scen", scatter_dimension=1, tiled=True)
    rows_share = direction.shape[1] // lax.axis_size("scen")
    prior = prior_gain * (direction - prior_reach * laplace(padded_all[0]))
    prior_share = lax.dynamic_slice_in_dim(
        prior, lax.axis_index("scen") * rows_share, rows_share, 1
    )
    return reduced + prior_share


def solution(mesh):
    return jax.shard_map(
        local,
        mesh=mesh,
        in_specs=(
            P("scen", None, "grid", None, None),
            P("grid", None, None),
            P("grid", None, None),
            P("grid", None, None),
            P("scen", "grid"),
            P("scen", "grid"),
        ),
        out_specs=P("grid", "scen", None),
        check_vma=False,
    )
```

profile of v0, /device:TPU:6, one launch (start us, length us, event | category | flops | bytes accessed | tf_op | source)
XLA Modules:
  0.0 308.9 jit_solution(8494432370517738724)
XLA Ops:
  6.5 0.0 reduce-scatter.2.cloned.1.call-start
  6.5 0.0 copy-start.4
  6.5 2.1 pad_maximum_fusion
  8.7 0.0 copy-start.3
  8.7 0.0 copy-start
  8.7 0.0 copy-start.1
  8.7 1.4 collective-permute-start
  10.1 3.2 %collective-permute-start.1 = (f32[5,1,256,512]{3,2,1,0:T(8,128)S(1)}, f32[5,1,256,512]{3,2,1,0:T(8,128)S(1)}, u32[]{:S(2)}, u32[]{:S(2)}) collective-permute-start(f32[5,1,256,512]{3,2,1,0:T(8,128)S(1)} %pad_maximum_fusion), channel_id=1, source_target_pairs={{0,1},{1,2},{2,3},{3,4},{4,5},{5,6},{6,7},{7,8},{8,9},{9,10},{10,1... | collective-permute-start | bytes 7864328 | tf_op jit(solution)/shard_map/ppermute | solution.py:16
  13.4 2.3 collective-permute-done
  15.6 2.1 collective-permute-done.1
  17.7 0.0 copy-done.4
  17.7 1.5 fusion.4
  19.2 0.0 copy-done.3
  19.3 0.1 fusion.65
  19.4 1.3 collective-permute-start.2
  20.7 28.6 %collective-permute-start.3 = (f32[1,256,512]{2,1,0:T(8,128)S(1)}, f32[1,256,512]{2,1,0:T(8,128)S(1)}, u32[]{:S(2)}, u32[]{:S(2)}) collective-permute-start(f32[1,256,512]{2,1,0:T(8,128)S(1)} %fusion.65), channel_id=1, source_target_pairs={{0,1},{1,2},{2,3},{3,4},{4,5},{5,6},{6,7},{7,8},{8,9},{9,10},{10,1... | collective-permute-start | bytes 1572872 | tf_op jit(solution)/shard_map/ppermute | solution.py:16
  49.3 0.0 collective-permute-done.2
  49.3 1.5 collective-permute-done.3
  50.8 0.0 copy-done
  50.8 0.0 copy-done.1
  50.8 1.9 fusion.57
  52.7 1.4 collective-permute-start.4
  54.1 9.6 %collective-permute-start.5 = (f32[1,256,512]{2,1,0:T(8,128)S(1)}, f32[1,256,512]{2,1,0:T(8,128)S(1)}, u32[]{:S(2)}, u32[]{:S(2)}) collective-permute-start(f32[1,256,512]{2,1,0:T(8,128)S(1)} %get-tuple-element.10), channel_id=1, source_target_pairs={{0,1},{1,2},{2,3},{3,4},{4,5},{5,6},{6,7},{7,8},{8,9},{9,10},{10,1... | collective-permute-start | bytes 1572872 | tf_op jit(solution)/shard_map/ppermute | solution.py:16
  63.7 0.0 collective-permute-done.4
  63.8 1.5 collective-permute-done.5
  65.2 0.6 fusion.22
  65.9 1.3 collective-permute-start.6
  67.2 9.6 %collective-permute-start.7 = (f32[1,256,512]{2,1,0:T(8,128)S(1)}, f32[1,256,512]{2,1,0:T(8,128)S(1)}, u32[]{:S(2)}, u32[]{:S(2)}) collective-permute-start(f32[1,256,512]{2,1,0:T(8,128)S(1)} %fusion.22), channel_id=1, source_target_pairs={{0,1},{1,2},{2,3},{3,4},{4,5},{5,6},{6,7},{7,8},{8,9},{9,10},{10,1... | collective-permute-start | bytes 1572872 | tf_op jit(solution)/shard_map/ppermute | solution.py:16
  76.8 0.0 copy-done.6
  76.8 0.0 collective-permute-done.6
  76.9 1.4 collective-permute-done.7
  78.3 0.6 fusion.32
  78.9 0.1 copy.7
  79.1 0.0 copy-start.5
  79.1 23.0 %gather_fusion = f32[4096]{0:T(1024)S(1)} fusion(f32[131072]{0:T(1024)S(1)} %bitcast.77, s32[4096]{0:T(1024)S(1)} %broadcast_clamp_fusion), kind=kCustom, calls=%fused_computation | custom fusion | bytes 49152 | tf_op jit(solution)/shard_map/gather | solution.py:52
  102.1 0.0 copy-done.5
  102.1 22.7 %scatter_custom_fusion = f32[131072]{0:T(1024)} fusion(s32[4096]{0:T(1024)S(1)} %bitcast.88, f32[4096]{0:T(1024)S(1)} %mul.197, f32[]{:T(128)} %constant.11.clone.1), kind=kCustom, calls=%fused_computation.116 | custom fusion | flops 4096 | bytes 524292 | tf_op jit(solution)/shard_map/scatter-add | solution.py:53
  124.8 1.1 reshape.223
  126.0 1.2 fusion.77
  127.2 0.1 pad_maximum_fusion.1
  127.2 0.0 copy-start.2
  127.3 1.4 collective-permute-start.8
  128.7 9.7 %collective-permute-start.9 = (f32[2,1,256,512]{3,2,1,0:T(8,128)S(1)}, f32[2,1,256,512]{3,2,1,0:T(8,128)S(1)}, u32[]{:S(2)}, u32[]{:S(2)}) collective-permute-start(f32[2,1,256,512]{3,2,1,0:T(8,128)S(1)} %pad_maximum_fusion.1), channel_id=1, source_target_pairs={{0,1},{1,2},{2,3},{3,4},{4,5},{5,6},{6,7},{7,8},{8,9},{9,10},{10,1... | collective-permute-start | bytes 3145736 | tf_op jit(solution)/shard_map/ppermute | solution.py:16
  138.4 0.1 collective-permute-done.8
  138.5 2.1 collective-permute-done.9
  140.6 0.6 fusion.75
  141.2 0.0 copy-done.2
  141.2 0.1 mul.205
  141.3 0.1 pad_maximum_fusion.2
  141.4 1.3 collective-permute-start.10
  142.7 14.5 %collective-permute-start.11 = (f32[2,1,256,512]{3,2,1,0:T(8,128)S(1)}, f32[2,1,256,512]{3,2,1,0:T(8,128)S(1)}, u32[]{:S(2)}, u32[]{:S(2)}) collective-permute-start(f32[2,1,256,512]{3,2,1,0:T(8,128)S(1)} %pad_maximum_fusion.2), channel_id=1, source_target_pairs={{0,1},{1,2},{2,3},{3,4},{4,5},{5,6},{6,7},{7,8},{8,9},{9,10},{10,1... | collective-permute-start | bytes 3145736 | tf_op jit(solution)/shard_map/ppermute | solution.py:16
  157.2 0.1 collective-permute-done.10
  157.4 2.1 collective-permute-done.11
  159.4 0.6 fusion.73
  160.0 0.1 mul.210
  160.1 0.1 pad_maximum_fusion.3
  160.2 1.3 collective-permute-start.12
  161.5 14.5 %collective-permute-start.13 = (f32[2,1,256,512]{3,2,1,0:T(8,128)S(1)}, f32[2,1,256,512]{3,2,1,0:T(8,128)S(1)}, u32[]{:S(2)}, u32[]{:S(2)}) collective-permute-start(f32[2,1,256,512]{3,2,1,0:T(8,128)S(1)} %pad_maximum_fusion.3), channel_id=1, source_target_pairs={{0,1},{1,2},{2,3},{3,4},{4,5},{5,6},{6,7},{7,8},{8,9},{9,10},{10,1... | collective-permute-start | bytes 3145736 | tf_op jit(solution)/shard_map/ppermute | solution.py:16
  176.0 0.1 collective-permute-done.12
  176.2 2.1 collective-permute-done.13
  178.2 1.7 fusion.55
  179.9 0.0 reduce-scatter.2.cloned.1.call-update
  180.0 120.5 %reduce-scatter.2.cloned.1.call-done = f32[1,32,512]{2,1,0:T(8,128)} async-done(((f32[1,256,512]{2,1,0:T(8,128)}), f32[1,32,512]{2,1,0:T(8,128)}) %reduce-scatter.2.cloned.1.call-update) | async-done | bytes 65552 | tf_op jit(solution)/shard_map/reduce_scatter | solution.py:64
  300.4 1.6 fusion.72
  (4 shorter events, 0.0 us)
Async XLA Ops:
  6.5 293.9 %reduce-scatter.2.cloned.1.call-start = ((), (), s32[]{:S(2)}) async-start(), calls=%async_computation.1 | async-start | bytes 589824 | tf_op jit(solution)/shard_map/reduce_scatter | solution.py:64
  6.5 11.2 %copy-start.4 = (f32[1,4,1,256,512]{4,3,2,1,0:T(8,128)S(1)}, f32[1,4,1,256,512]{4,3,2,1,0:T(8,128)}, u32[]{:S(2)}) copy-start(f32[1,4,1,256,512]{4,3,2,1,0:T(8,128)} %param.6) | copy-start | bytes 6291460
  8.7 10.6 %copy-start.3 = (f32[1,256,512]{2,1,0:T(8,128)S(1)}, f32[1,256,512]{2,1,0:T(8,128)}, u32[]{:S(2)}) copy-start(f32[1,256,512]{2,1,0:T(8,128)} %param.9) | copy-start | bytes 1572868
  8.7 42.1 %copy-start = (f32[1,256,512]{2,1,0:T(8,128)S(1)}, f32[1,256,512]{2,1,0:T(8,128)}, u32[]{:S(2)}) copy-start(f32[1,256,512]{2,1,0:T(8,128)} %param.8) | copy-start | bytes 1572868
  8.7 42.1 %copy-start.1 = (f32[1,256,512]{2,1,0:T(8,128)S(1)}, f32[1,256,512]{2,1,0:T(8,128)}, u32[]{:S(2)}) copy-start(f32[1,256,512]{2,1,0:T(8,128)} %param.7) | copy-start | bytes 1572868
  8.7 6.9 %collective-permute-start = (f32[5,1,256,512]{3,2,1,0:T(8,128)S(1)}, f32[5,1,256,512]{3,2,1,0:T(8,128)S(1)}, u32[]{:S(2)}, u32[]{:S(2)}) collective-permute-start(f32[5,1,256,512]{3,2,1,0:T(8,128)S(1)} %pad_maximum_fusion), channel_id=1, source_target_pairs={{1,0},{2,1},{3,2},{4,3},{5,4},{6,5},{7,6},{8,7},{9,8},{10,9},{11,1... | collective-permute-start | bytes 7864328 | tf_op jit(solution)/shard_map/ppermute | solution.py:19
  10.1 7.6 %collective-permute-start.1 = (f32[5,1,256,512]{3,2,1,0:T(8,128)S(1)}, f32[5,1,256,512]{3,2,1,0:T(8,128)S(1)}, u32[]{:S(2)}, u32[]{:S(2)}) collective-permute-start(f32[5,1,256,512]{3,2,1,0:T(8,128)S(1)} %pad_maximum_fusion), channel_id=1, source_target_pairs={{0,1},{1,2},{2,3},{3,4},{4,5},{5,6},{6,7},{7,8},{8,9},{9,10},{10,1... | collective-permute-start | bytes 7864328 | tf_op jit(solution)/shard_map/ppermute | solution.py:16
  19.4 29.9 %collective-permute-start.2 = (f32[1,256,512]{2,1,0:T(8,128)S(1)}, f32[1,256,512]{2,1,0:T(8,128)S(1)}, u32[]{:S(2)}, u32[]{:S(2)}) collective-permute-start(f32[1,256,512]{2,1,0:T(8,128)S(1)} %fusion.65), channel_id=1, source_target_pairs={{1,0},{2,1},{3,2},{4,3},{5,4},{6,5},{7,6},{8,7},{9,8},{10,9},{11,1... | collective-permute-start | bytes 1572872 | tf_op jit(solution)/shard_map/ppermute | solution.py:19
  20.7 30.1 %collective-permute-start.3 = (f32[1,256,512]{2,1,0:T(8,128)S(1)}, f32[1,256,512]{2,1,0:T(8,128)S(1)}, u32[]{:S(2)}, u32[]{:S(2)}) collective-permute-start(f32[1,256,512]{2,1,0:T(8,128)S(1)} %fusion.65), channel_id=1, source_target_pairs={{0,1},{1,2},{2,3},{3,4},{4,5},{5,6},{6,7},{7,8},{8,9},{9,10},{10,1... | collective-permute-start | bytes 1572872 | tf_op jit(solution)/shard_map/ppermute | solution.py:16
  52.7 24.1 %copy-start.6 = (s32[1,4096]{1,0:T(1,128)S(1)}, s32[1,4096]{1,0:T(1,128)}, u32[]{:S(2)}) copy-start(s32[1,4096]{1,0:T(1,128)} %param.10) | copy-start | bytes 49156
  52.7 11.1 %collective-permute-start.4 = (f32[1,256,512]{2,1,0:T(8,128)S(1)}, f32[1,256,512]{2,1,0:T(8,128)S(1)}, u32[]{:S(2)}, u32[]{:S(2)}) collective-permute-start(f32[1,256,512]{2,1,0:T(8,128)S(1)} %get-tuple-element.10), channel_id=1, source_target_pairs={{1,0},{2,1},{3,2},{4,3},{5,4},{6,5},{7,6},{8,7},{9,8},{10,9},{11,1... | collective-permute-start | bytes 1572872 | tf_op jit(solution)/shard_map/ppermute | solution.py:19
  54.1 11.1 %collective-permute-start.5 = (f32[1,256,512]{2,1,0:T(8,128)S(1)}, f32[1,256,512]{2,1,0:T(8,128)S(1)}, u32[]{:S(2)}, u32[]{:S(2)}) collective-permute-start(f32[1,256,512]{2,1,0:T(8,128)S(1)} %get-tuple-element.10), channel_id=1, source_target_pairs={{0,1},{1,2},{2,3},{3,4},{4,5},{5,6},{6,7},{7,8},{8,9},{9,10},{10,1... | collective-permute-start | bytes 1572872 | tf_op jit(solution)/shard_map/ppermute | solution.py:16
  65.9 11.0 %collective-permute-start.6 = (f32[1,256,512]{2,1,0:T(8,128)S(1)}, f32[1,256,512]{2,1,0:T(8,128)S(1)}, u32[]{:S(2)}, u32[]{:S(2)}) collective-permute-start(f32[1,256,512]{2,1,0:T(8,128)S(1)} %fusion.22), channel_id=1, source_target_pairs={{1,0},{2,1},{3,2},{4,3},{5,4},{6,5},{7,6},{8,7},{9,8},{10,9},{11,1... | collective-permute-start | bytes 1572872 | tf_op jit(solution)/shard_map/ppermute | solution.py:19
  67.2 11.1 %collective-permute-start.7 = (f32[1,256,512]{2,1,0:T(8,128)S(1)}, f32[1,256,512]{2,1,0:T(8,128)S(1)}, u32[]{:S(2)}, u32[]{:S(2)}) collective-permute-start(f32[1,256,512]{2,1,0:T(8,128)S(1)} %fusion.22), channel_id=1, source_target_pairs={{0,1},{1,2},{2,3},{3,4},{4,5},{5,6},{6,7},{7,8},{8,9},{9,10},{10,1... | collective-permute-start | bytes 1572872 | tf_op jit(solution)/shard_map/ppermute | solution.py:16
  79.1 23.1 %copy-start.5 = (f32[1,4096]{1,0:T(1,128)S(1)}, f32[1,4096]{1,0:T(1,128)}, u32[]{:S(2)}) copy-start(f32[1,4096]{1,0:T(1,128)} %param.11) | copy-start | bytes 49156
  127.2 13.9 %copy-start.2 = (f32[1,256,512]{2,1,0:T(8,128)S(1)}, f32[1,256,512]{2,1,0:T(8,128)}, u32[]{:S(2)}) copy-start(f32[1,256,512]{2,1,0:T(8,128)} %param.7) | copy-start | bytes 1572868
  127.3 11.3 %collective-permute-start.8 = (f32[2,1,256,512]{3,2,1,0:T(8,128)S(1)}, f32[2,1,256,512]{3,2,1,0:T(8,128)S(1)}, u32[]{:S(2)}, u32[]{:S(2)}) collective-permute-start(f32[2,1,256,512]{3,2,1,0:T(8,128)S(1)} %pad_maximum_fusion.1), channel_id=1, source_target_pairs={{1,0},{2,1},{3,2},{4,3},{5,4},{6,5},{7,6},{8,7},{9,8},{10,9},{11,1... | collective-permute-start | bytes 3145736 | tf_op jit(solution)/shard_map/ppermute | solution.py:19
  128.7 11.9 %collective-permute-start.9 = (f32[2,1,256,512]{3,2,1,0:T(8,128)S(1)}, f32[2,1,256,512]{3,2,1,0:T(8,128)S(1)}, u32[]{:S(2)}, u32[]{:S(2)}) collective-permute-start(f32[2,1,256,512]{3,2,1,0:T(8,128)S(1)} %pad_maximum_fusion.1), channel_id=1, source_target_pairs={{0,1},{1,2},{2,3},{3,4},{4,5},{5,6},{6,7},{7,8},{8,9},{9,10},{10,1... | collective-permute-start | bytes 3145736 | tf_op jit(solution)/shard_map/ppermute | solution.py:16
  141.4 16.0 %collective-permute-start.10 = (f32[2,1,256,512]{3,2,1,0:T(8,128)S(1)}, f32[2,1,256,512]{3,2,1,0:T(8,128)S(1)}, u32[]{:S(2)}, u32[]{:S(2)}) collective-permute-start(f32[2,1,256,512]{3,2,1,0:T(8,128)S(1)} %pad_maximum_fusion.2), channel_id=1, source_target_pairs={{1,0},{2,1},{3,2},{4,3},{5,4},{6,5},{7,6},{8,7},{9,8},{10,9},{11,1... | collective-permute-start | bytes 3145736 | tf_op jit(solution)/shard_map/ppermute | solution.py:19
  142.7 16.7 %collective-permute-start.11 = (f32[2,1,256,512]{3,2,1,0:T(8,128)S(1)}, f32[2,1,256,512]{3,2,1,0:T(8,128)S(1)}, u32[]{:S(2)}, u32[]{:S(2)}) collective-permute-start(f32[2,1,256,512]{3,2,1,0:T(8,128)S(1)} %pad_maximum_fusion.2), channel_id=1, source_target_pairs={{0,1},{1,2},{2,3},{3,4},{4,5},{5,6},{6,7},{7,8},{8,9},{9,10},{10,1... | collective-permute-start | bytes 3145736 | tf_op jit(solution)/shard_map/ppermute | solution.py:16
  160.2 16.0 %collective-permute-start.12 = (f32[2,1,256,512]{3,2,1,0:T(8,128)S(1)}, f32[2,1,256,512]{3,2,1,0:T(8,128)S(1)}, u32[]{:S(2)}, u32[]{:S(2)}) collective-permute-start(f32[2,1,256,512]{3,2,1,0:T(8,128)S(1)} %pad_maximum_fusion.3), channel_id=1, source_target_pairs={{1,0},{2,1},{3,2},{4,3},{5,4},{6,5},{7,6},{8,7},{9,8},{10,9},{11,1... | collective-permute-start | bytes 3145736 | tf_op jit(solution)/shard_map/ppermute | solution.py:19
  161.5 16.7 %collective-permute-start.13 = (f32[2,1,256,512]{3,2,1,0:T(8,128)S(1)}, f32[2,1,256,512]{3,2,1,0:T(8,128)S(1)}, u32[]{:S(2)}, u32[]{:S(2)}) collective-permute-start(f32[2,1,256,512]{3,2,1,0:T(8,128)S(1)} %pad_maximum_fusion.3), channel_id=1, source_target_pairs={{0,1},{1,2},{2,3},{3,4},{4,5},{5,6},{6,7},{7,8},{8,9},{9,10},{10,1... | collective-permute-start | bytes 3145736 | tf_op jit(solution)/shard_map/ppermute | solution.py:16
Sparse Core Ops, SparseCore 0:
  180.1 120.2 reduce-scatter.1
where the time goes:
time: 310 us; the launch traced here: 309 us
  waiting for transfers between devices  136 us (44%)
  starting transfers between devices  99.3 us (32%)
  other arithmetic  35.8 us (12%)
  local copies, waits for them, and re-layouts  24.3 us (8%)
  between operations  13.7 us (4%)
    reduce_scatter x1, waiting for transfers between devices, local(): lax.psum_scatter(partial_value, 'scen', scatter_dimension=1, tiled=True)  120 us
    ppermute x7, starting transfers between devices, padded_2(): lax.ppermute(lax.slice_in_dim(block, block.shape[dim] - width, None, axis...  89.8 us
    gather x1, local copies, waits for them, and re-layouts, local(): values = tangent.reshape(-1)[index] * obs_weight[0]  23 us
    scatter-add x1, other arithmetic, local(): jnp.zeros((cells,), jnp.float32).at[index].add(values)  22.7 us
    ppermute x7, waiting for transfers between devices, padded_2(): lax.ppermute(lax.slice_in_dim(block, block.shape[dim] - width, None, axis...  12.6 us
    ppermute x7, starting transfers between devices, padded_2(): lax.ppermute(lax.slice_in_dim(block, 0, width, axis=dim), axis, backward)  9.43 us
  transfers between devices with their start and end apart: 15, of which 12 were waited for; matrix products, arithmetic and copies ran while one was open for 0% of the time, Pallas kernels for 0%

commit v1 on v0

v1 whole, which is shorter than its diff:
```python
import jax
import jax.numpy as jnp
from jax import lax
from jax.experimental import pallas as pl
from jax.experimental.pallas import tpu as pltpu
from jax.sharding import PartitionSpec as P

source_gain = 0.2
prior_gain = 0.5
prior_reach = 0.1


def weight_kernel(index_ref, weight_ref, field_ref):
    rows, columns = field_ref.shape
    chunk = index_ref.shape[1]

    @pl.when(pl.program_id(0) == 0)
    def _():
        field_ref[...] = jnp.zeros_like(field_ref)

    index = index_ref[...]
    row = index // columns
    column = index - row * columns
    left = weight_ref[...]
    row_hit = lax.broadcasted_iota(jnp.int32, (rows, chunk), 0) == row
    column_hit = lax.broadcasted_iota(jnp.int32, (columns, chunk), 0) == column
    column_one = jnp.where(column_hit, 1.0, 0.0).astype(jnp.bfloat16)
    for _ in range(3):
        part = left.astype(jnp.bfloat16).astype(jnp.float32)
        left = left - part
        row_part = jnp.where(row_hit, part, 0.0).astype(jnp.bfloat16)
        field_ref[...] += lax.dot_general(
            row_part, column_one, (((1,), (1,)), ((), ())), preferred_element_type=jnp.float32
        )


def weight_field(index, weight, rows, columns):
    count = index.shape[1]
    chunk = 1024
    return pl.pallas_call(
        weight_kernel,
        grid=(count // chunk,),
        in_specs=[pl.BlockSpec((1, chunk), lambda i: (0, i))] * 2,
        out_specs=pl.BlockSpec((rows, columns), lambda i: (0, 0)),
        out_shape=jax.ShapeDtypeStruct((rows, columns), jnp.float32),
        compiler_params=pltpu.CompilerParams(vmem_limit_bytes=24 << 20),
        cost_estimate=pl.CostEstimate(
            flops=6 * rows * columns * count, bytes_accessed=4 * rows * columns, transcendentals=0
        ),
        name="weight_field",
    )(index, weight)


def side_sum(field):
    wide = jnp.pad(field, [(0, 0)] * (field.ndim - 2) + [(1, 1), (1, 1)])
    total = wide[..., 2:, 1:-1] + wide[..., :-2, 1:-1]
    return total + wide[..., 1:-1, 2:] + wide[..., 1:-1, :-2] - 6.0 * field


def local(forward_states, kappa, courant, direction, obs_index, obs_weight):
    states = forward_states[0, :, 0]
    kappa, courant, direction = kappa[0], courant[0], direction[0]
    steps, rows, columns = states.shape
    slabs = lax.axis_size("grid")
    scens = lax.axis_size("scen")
    even = lax.axis_index("grid") % 2 == 0
    mine = lax.axis_index("scen")

    near = [(g, g ^ 1) for g in range(slabs)]
    far = [(g, g - 1 if g % 2 == 0 else g + 1) for g in range(slabs)]
    far = [(g, h) for g, h in far if 0 <= h < slabs]

    def swap(far_field, near_field):
        return lax.ppermute(far_field, "grid", far), lax.ppermute(near_field, "grid", near)

    fars, nears = [], lax.ppermute(states, "grid", near)
    for step in range(steps):
        fars.append(lax.ppermute(states[step], "grid", far))
    laps = [fars[k] + nears[k] + side_sum(states[k]) for k in range(steps)]

    weights = weight_field(obs_index, obs_weight, rows, columns)

    tangent = source_gain * direction * laps[0]
    for step in range(1, steps):
        over, beside = swap(tangent, tangent)
        below = jnp.where(even, over, beside)
        tangent = (
            tangent
            + kappa * (over + beside + side_sum(tangent))
            - courant * (tangent - below)
            + source_gain * direction * laps[step]
        )

    adjoint = tangent * weights
    partial_value = source_gain * laps[steps - 1] * adjoint
    for step in range(steps - 2, -1, -1):
        weighted = kappa * adjoint
        carried = courant * adjoint
        both = weighted + carried
        over, beside = swap(
            jnp.where(even, both, weighted), jnp.where(even, weighted, both)
        )
        adjoint = adjoint + (over + beside + side_sum(weighted)) - carried
        partial_value = partial_value + source_gain * laps[step] * adjoint

    share = rows // scens
    block = 2 * share
    blocks = scens // 2
    place, half = mine // 2, mine % 2
    arrived = []
    for hop in (2, 1, 3):
        piece = lax.dynamic_slice_in_dim(
            partial_value, ((place + hop) % blocks) * block, block, 0
        )
        ring = [(s, (s // 2 + hop) % blocks * 2 + s % 2) for s in range(scens)]
        arrived.append(lax.ppermute(piece, "scen", ring))
    total = lax.dynamic_slice_in_dim(partial_value, place * block, block, 0)
    for piece in arrived:
        total = total + piece
    other = lax.dynamic_slice_in_dim(total, (1 - half) * share, share, 0)
    kept = lax.dynamic_slice_in_dim(total, half * share, share, 0)
    across = lax.ppermute(other, "scen", [(s, s ^ 1) for s in range(scens)])

    own = lax.dynamic_slice_in_dim(direction, mine * share, share, 0)
    over, beside = swap(own, own)
    tall = jnp.pad(direction, ((1, 1), (0, 0)))
    tall = lax.dynamic_slice_in_dim(tall, mine * share, share + 2, 0)
    lap = over + beside + side_sum(tall)[1:-1]
    prior = prior_gain * (own - prior_reach * lap)
    return (kept + across + prior)[None]


def solution(mesh):
    return jax.shard_map(
        local,
        mesh=mesh,
        in_specs=(
            P("scen", None, "grid", None, None),
            P("grid", None, None),
            P("grid", None, None),
            P("grid", None, None),
            P("scen", "grid"),
            P("scen", "grid"),
        ),
        out_specs=P("grid", "scen", None),
        check_vma=False,
    )
```

time: 310 us -> 152 us (0.49)
  the two profiles are of different devices: /device:TPU:6 before, /device:TPU:40 now
where the time goes in v1:
time: 152 us; the launch traced here: 151 us
  starting transfers between devices  86.6 us (57%)
  waiting for transfers between devices  38 us (25%)
  other arithmetic  16.9 us (11%)
  Pallas kernels  4.3 us (3%)
  local copies, waits for them, and re-layouts  4.28 us (3%)
    ppermute x7, starting transfers between devices, swap(): lax.ppermute(far_field, 'grid', far)  39.4 us
    ppermute x7, waiting for transfers between devices, swap(): lax.ppermute(far_field, 'grid', far)  23.5 us
    ppermute x4, starting transfers between devices, local(): fars.append(lax.ppermute(states[step], 'grid', far))  17.7 us
    ppermute x7, starting transfers between devices, swap(): lax.ppermute(near_field, 'grid', near)  13.4 us
    ppermute x3, starting transfers between devices, local(): arrived.append(lax.ppermute(piece, 'scen', ring))  12 us
    ppermute x1, waiting for transfers between devices, local(): across = lax.ppermute(other, 'scen', [(s, s ^ 1) for s in range(scens)])  9.55 us
    add x2, other arithmetic, local(): tangent + kappa * (over + beside + side_sum(tangent))  6.16 us
    ppermute x4, waiting for transfers between devices, local(): fars.append(lax.ppermute(states[step], 'grid', far))  4.93 us
  transfers between devices with their start and end apart: 23, of which 8 were waited for; matrix products, arithmetic and copies ran while one was open for 7% of the time, Pallas kernels for 3%

profile of v1, /device:TPU:40, one launch (start us, length us, event | category | flops | bytes accessed | tf_op | source)
XLA Modules:
  0.0 150.6 jit_solution(13182997259481979249)
XLA Ops:
  0.0 2.0 %collective-permute-start.1 = (f32[4,256,512]{2,1,0:T(8,128)}, f32[4,256,512]{2,1,0:T(8,128)S(1)}, u32[]{:S(2)}, u32[]{:S(2)}) collective-permute-start(f32[4,256,512]{2,1,0:T(8,128)} %bitcast.96), channel_id=1, source_target_pairs={{0,1},{1,0},{2,3},{3,2},{4,5},{5,4},{6,7},{7,6},{8,9},{9,8},{10,11... | collective-permute-start | bytes 6291464 | tf_op jit(solution)/shard_map/ppermute | solution.py:76
  2.0 2.5 %slice_bitcast_fusion.7 = (f32[256,512]{1,0:T(8,128)}, f32[256,512]{1,0:T(8,128)S(1)}, f32[256,512]{1,0:T(8,128)S(1)}, f32[256,512]{1,0:T(8,128)S(1)}) fusion(f32[1,4,1,256,512]{4,3,2,1,0:T(8,128)} %param.6), kind=kLoop, calls=%fused_computation.137 | loop fusion | bytes 4194304 | tf_op jit(solution)/shard_map/squeeze | solution.py:78
  4.5 12.0 %collective-permute-start.2 = (f32[256,512]{1,0:T(8,128)S(1)}, f32[256,512]{1,0:T(8,128)S(1)}, u32[]{:S(2)}, u32[]{:S(2)}) collective-permute-start(f32[256,512]{1,0:T(8,128)S(1)} %get-tuple-element.22), channel_id=1, source_target_pairs={{1,2},{2,1},{3,4},{4,3},{5,6},{6,5},{7,8},{8,7},{9,10},{10,9},{11,... | collective-permute-start | bytes 1572872 | tf_op jit(solution)/shard_map/ppermute | solution.py:78
  16.5 1.9 %collective-permute-start.5 = (f32[256,512]{1,0:T(8,128)S(1)}, f32[256,512]{1,0:T(8,128)}, u32[]{:S(2)}, u32[]{:S(2)}) collective-permute-start(f32[256,512]{1,0:T(8,128)S(1)} %get-tuple-element.24), channel_id=1, source_target_pairs={{1,2},{2,1},{3,4},{4,3},{5,6},{6,5},{7,8},{8,7},{9,10},{10,9},{11,... | collective-permute-start | bytes 1572872 | tf_op jit(solution)/shard_map/ppermute | solution.py:78
  18.4 4.9 %collective-permute-done.2 = f32[256,512]{1,0:T(8,128)S(1)} collective-permute-done((f32[256,512]{1,0:T(8,128)S(1)}, f32[256,512]{1,0:T(8,128)S(1)}, u32[]{:S(2)}, u32[]{:S(2)}) %collective-permute-start.2) | collective-permute-done | bytes 524320 | tf_op jit(solution)/shard_map/ppermute | solution.py:78
  23.3 0.0 collective-permute-done.1
  23.4 1.4 multiply_multiply_fusion
  24.8 0.0 copy-done.8
  24.8 5.7 %collective-permute-start.3 = (f32[256,512]{1,0:T(8,128)S(1)}, f32[256,512]{1,0:T(8,128)}, u32[]{:S(2)}, u32[]{:S(2)}) collective-permute-start(f32[256,512]{1,0:T(8,128)S(1)} %get-tuple-element.19), channel_id=1, source_target_pairs={{1,2},{2,1},{3,4},{4,3},{5,6},{6,5},{7,8},{8,7},{9,10},{10,9},{11,... | collective-permute-start | bytes 1572872 | tf_op jit(solution)/shard_map/ppermute | solution.py:74
  30.6 1.9 %collective-permute-start.4 = (f32[256,512]{1,0:T(8,128)S(1)}, f32[256,512]{1,0:T(8,128)}, u32[]{:S(2)}, u32[]{:S(2)}) collective-permute-start(f32[256,512]{1,0:T(8,128)S(1)} %get-tuple-element.19), channel_id=1, source_target_pairs={{0,1},{1,0},{2,3},{3,2},{4,5},{5,4},{6,7},{7,6},{8,9},{9,8},{10,11... | collective-permute-start | bytes 1572872 | tf_op jit(solution)/shard_map/ppermute | solution.py:74
  32.5 1.9 %collective-permute-start.8 = (f32[256,512]{1,0:T(8,128)S(1)}, f32[256,512]{1,0:T(8,128)}, u32[]{:S(2)}, u32[]{:S(2)}) collective-permute-start(f32[256,512]{1,0:T(8,128)S(1)} %get-tuple-element.23), channel_id=1, source_target_pairs={{1,2},{2,1},{3,4},{4,3},{5,6},{6,5},{7,8},{8,7},{9,10},{10,9},{11,... | collective-permute-start | bytes 1572872 | tf_op jit(solution)/shard_map/ppermute | solution.py:78
  34.5 0.0 collective-permute-done.5
  34.5 3.1 %collective-permute-done.3 = f32[256,512]{1,0:T(8,128)} collective-permute-done((f32[256,512]{1,0:T(8,128)S(1)}, f32[256,512]{1,0:T(8,128)}, u32[]{:S(2)}, u32[]{:S(2)}) %collective-permute-start.3) | collective-permute-done | bytes 524320 | tf_op jit(solution)/shard_map/ppermute | solution.py:74
  37.5 0.0 collective-permute-done.4
  37.5 3.3 %fusion.18 = (f32[256,512]{1,0:T(8,128)S(1)}, f32[256,512]{1,0:T(8,128)}) fusion(f32[256,512]{1,0:T(8,128)S(1)} %get-tuple-element.19, f32[1,256,512]{2,1,0:T(8,128)S(1)} %copy-done.2, f32[1,256,512]{2,1,0:T(8,128)S(1)} %copy-done.4, f32[256,512]{1,0:T(8,128)} %collective-permute-done.3, f32[256,512]{1,0:T(8,128)} %collective-permute-done.4, pred[]{:T(512)S(6)} %eq.9, ...), kind=kLoop, calls=%fused_computation.64 | loop fusion | flops 3014656 | bytes 5767169 | tf_op jit(solution)/shard_map/add | solution.py:88
  40.9 5.7 %collective-permute-start.6 = (f32[256,512]{1,0:T(8,128)S(1)}, f32[256,512]{1,0:T(8,128)S(1)}, u32[]{:S(2)}, u32[]{:S(2)}) collective-permute-start(f32[256,512]{1,0:T(8,128)S(1)} %get-tuple-element.17), channel_id=1, source_target_pairs={{1,2},{2,1},{3,4},{4,3},{5,6},{6,5},{7,8},{8,7},{9,10},{10,9},{11,... | collective-permute-start | bytes 1572872 | tf_op jit(solution)/shard_map/ppermute | solution.py:74
  46.6 1.9 %collective-permute-start.7 = (f32[256,512]{1,0:T(8,128)S(1)}, f32[256,512]{1,0:T(8,128)S(1)}, u32[]{:S(2)}, u32[]{:S(2)}) collective-permute-start(f32[256,512]{1,0:T(8,128)S(1)} %get-tuple-element.17), channel_id=1, source_target_pairs={{0,1},{1,0},{2,3},{3,2},{4,5},{5,4},{6,7},{7,6},{8,9},{9,8},{10,11... | collective-permute-start | bytes 1572872 | tf_op jit(solution)/shard_map/ppermute | solution.py:74
  48.5 0.0 copy-start
  48.5 0.0 copy-start.1
  48.6 1.9 %collective-permute-start = (f32[256,512]{1,0:T(8,128)S(1)}, f32[256,512]{1,0:T(8,128)S(1)}, u32[]{:S(2)}, u32[]{:S(2)}) collective-permute-start(f32[256,512]{1,0:T(8,128)S(1)} %copy-done.10), channel_id=1, source_target_pairs={{1,2},{2,1},{3,4},{4,3},{5,6},{6,5},{7,8},{8,7},{9,10},{10,9},{11,... | collective-permute-start | bytes 1572872 | tf_op jit(solution)/shard_map/ppermute | solution.py:78
  50.5 0.0 collective-permute-done.8
  50.5 2.9 %collective-permute-done.6 = f32[256,512]{1,0:T(8,128)S(1)} collective-permute-done((f32[256,512]{1,0:T(8,128)S(1)}, f32[256,512]{1,0:T(8,128)S(1)}, u32[]{:S(2)}, u32[]{:S(2)}) %collective-permute-start.6) | collective-permute-done | bytes 524320 | tf_op jit(solution)/shard_map/ppermute | solution.py:74
  53.4 0.0 collective-permute-done.7
  53.5 2.9 %fusion.32 = (f32[256,512]{1,0:T(8,128)S(1)}, f32[256,512]{1,0:T(8,128)}) fusion(f32[256,512]{1,0:T(8,128)S(1)} %get-tuple-element.17, f32[1,256,512]{2,1,0:T(8,128)S(1)} %copy-done.2, f32[1,256,512]{2,1,0:T(8,128)S(1)} %copy-done.4, f32[256,512]{1,0:T(8,128)S(1)} %collective-permute-done.6, f32[256,512]{1,0:T(8,128)S(1)} %collective-permute-done.7, ...), kind=kLoop, calls=%fused_computation.78 | loop fusion | flops 3014656 | bytes 5767169 | tf_op jit(solution)/shard_map/add | solution.py:88
  56.3 1.9 %collective-permute-start.10 = (f32[256,512]{1,0:T(8,128)S(1)}, f32[256,512]{1,0:T(8,128)S(1)}, u32[]{:S(2)}, u32[]{:S(2)}) collective-permute-start(f32[256,512]{1,0:T(8,128)S(1)} %get-tuple-element.15), channel_id=1, source_target_pairs={{0,1},{1,0},{2,3},{3,2},{4,5},{5,4},{6,7},{7,6},{8,9},{9,8},{10,11... | collective-permute-start | bytes 1572872 | tf_op jit(solution)/shard_map/ppermute | solution.py:74
  58.2 5.7 %collective-permute-start.9 = (f32[256,512]{1,0:T(8,128)S(1)}, f32[256,512]{1,0:T(8,128)S(1)}, u32[]{:S(2)}, u32[]{:S(2)}) collective-permute-start(f32[256,512]{1,0:T(8,128)S(1)} %get-tuple-element.15), channel_id=1, source_target_pairs={{1,2},{2,1},{3,4},{4,3},{5,6},{6,5},{7,8},{8,7},{9,10},{10,9},{11,... | collective-permute-start | bytes 1572872 | tf_op jit(solution)/shard_map/ppermute | solution.py:74
  64.0 4.3 %weight_field.1 = f32[256,512]{1,0:T(8,128)S(1)} custom-call(s32[1,4096]{1,0:T(1,128)S(1)} %copy-done, f32[1,4096]{1,0:T(1,128)S(1)} %copy-done.1), custom_call_target="tpu_custom_call" | custom-call | flops 3221225472 | bytes 524288 | tf_op jit(solution)/shard_map/weight_field/pallas_call | solution.py:40
  68.3 0.0 collective-permute-done
  68.3 0.0 collective-permute-done.10
  68.3 2.5 %collective-permute-done.9 = f32[256,512]{1,0:T(8,128)S(1)} collective-permute-done((f32[256,512]{1,0:T(8,128)S(1)}, f32[256,512]{1,0:T(8,128)S(1)}, u32[]{:S(2)}, u32[]{:S(2)}) %collective-permute-start.9) | collective-permute-done | bytes 524320 | tf_op jit(solution)/shard_map/ppermute | solution.py:74
  70.8 1.8 %add_select_fusion.4 = (f32[256,512]{1,0:T(8,128)S(1)}, f32[256,512]{1,0:T(8,128)S(1)}, f32[256,512]{1,0:T(8,128)S(1)}, f32[256,512]{1,0:T(8,128)}) fusion(pred[]{:T(512)S(6)} %eq.9, f32[1,256,512]{2,1,0:T(8,128)S(1)} %copy-done.2, f32[1,256,512]{2,1,0:T(8,128)S(1)} %copy-done.4, f32[256,512]{1,0:T(8,128)S(1)} %weight_field.1, ...), kind=kLoop, calls=%fused_computation.44 | loop fusion | flops 3670016 | bytes 7340033 | tf_op jit(solution)/shard_map/jit(_where)/select_n | solution.py:101
  72.7 0.2 add_select_fusion.5
  72.8 5.7 %collective-permute-start.11 = (f32[256,512]{1,0:T(8,128)S(1)}, f32[256,512]{1,0:T(8,128)S(1)}, u32[]{:S(2)}, u32[]{:S(2)}) collective-permute-start(f32[256,512]{1,0:T(8,128)S(1)} %add_select_fusion.5), channel_id=1, source_target_pairs={{1,2},{2,1},{3,4},{4,3},{5,6},{6,5},{7,8},{8,7},{9,10},{10,9},{11,... | collective-permute-start | bytes 1572872 | tf_op jit(solution)/shard_map/ppermute | solution.py:74
  78.6 1.9 %collective-permute-start.12 = (f32[256,512]{1,0:T(8,128)S(1)}, f32[256,512]{1,0:T(8,128)S(1)}, u32[]{:S(2)}, u32[]{:S(2)}) collective-permute-start(f32[256,512]{1,0:T(8,128)S(1)} %get-tuple-element.11), channel_id=1, source_target_pairs={{0,1},{1,0},{2,3},{3,2},{4,5},{5,4},{6,7},{7,6},{8,9},{9,8},{10,11... | collective-permute-start | bytes 1572872 | tf_op jit(solution)/shard_map/ppermute | solution.py:74
  80.5 4.9 %collective-permute-done.11 = f32[256,512]{1,0:T(8,128)S(1)} collective-permute-done((f32[256,512]{1,0:T(8,128)S(1)}, f32[256,512]{1,0:T(8,128)S(1)}, u32[]{:S(2)}, u32[]{:S(2)}) %collective-permute-start.11) | collective-permute-done | bytes 524320 | tf_op jit(solution)/shard_map/ppermute | solution.py:74
  85.4 0.0 collective-permute-done.12
  85.4 0.6 add_select_fusion.2
  86.0 0.2 add_select_fusion.3
  86.2 5.7 %collective-permute-start.13 = (f32[256,512]{1,0:T(8,128)S(1)}, f32[256,512]{1,0:T(8,128)S(1)}, u32[]{:S(2)}, u32[]{:S(2)}) collective-permute-start(f32[256,512]{1,0:T(8,128)S(1)} %add_select_fusion.3), channel_id=1, source_target_pairs={{1,2},{2,1},{3,4},{4,3},{5,6},{6,5},{7,8},{8,7},{9,10},{10,9},{11,... | collective-permute-start | bytes 1572872 | tf_op jit(solution)/shard_map/ppermute | solution.py:74
  91.9 1.9 %collective-permute-start.14 = (f32[256,512]{1,0:T(8,128)S(1)}, f32[256,512]{1,0:T(8,128)S(1)}, u32[]{:S(2)}, u32[]{:S(2)}) collective-permute-start(f32[256,512]{1,0:T(8,128)S(1)} %get-tuple-element.8), channel_id=1, source_target_pairs={{0,1},{1,0},{2,3},{3,2},{4,5},{5,4},{6,7},{7,6},{8,9},{9,8},{10,11... | collective-permute-start | bytes 1572872 | tf_op jit(solution)/shard_map/ppermute | solution.py:74
  93.8 4.9 %collective-permute-done.13 = f32[256,512]{1,0:T(8,128)S(1)} collective-permute-done((f32[256,512]{1,0:T(8,128)S(1)}, f32[256,512]{1,0:T(8,128)S(1)}, u32[]{:S(2)}, u32[]{:S(2)}) %collective-permute-start.13) | collective-permute-done | bytes 524320 | tf_op jit(solution)/shard_map/ppermute | solution.py:74
  98.8 0.0 collective-permute-done.14
  98.8 1.4 add_select_fusion
  100.1 0.8 copy-done.5
  100.9 1.0 add_select_fusion.1
  101.9 5.7 %collective-permute-start.15 = (f32[256,512]{1,0:T(8,128)}, f32[256,512]{1,0:T(8,128)}, u32[]{:S(2)}, u32[]{:S(2)}) collective-permute-start(f32[256,512]{1,0:T(8,128)} %add_select_fusion.1), channel_id=1, source_target_pairs={{1,2},{2,1},{3,4},{4,3},{5,6},{6,5},{7,8},{8,7},{9,10},{10,9},{11,... | collective-permute-start | bytes 1572872 | tf_op jit(solution)/shard_map/ppermute | solution.py:74
  107.6 1.9 %collective-permute-start.16 = (f32[256,512]{1,0:T(8,128)}, f32[256,512]{1,0:T(8,128)}, u32[]{:S(2)}, u32[]{:S(2)}) collective-permute-start(f32[256,512]{1,0:T(8,128)} %get-tuple-element.5), channel_id=1, source_target_pairs={{0,1},{1,0},{2,3},{3,2},{4,5},{5,4},{6,7},{7,6},{8,9},{9,8},{10,11... | collective-permute-start | bytes 1572872 | tf_op jit(solution)/shard_map/ppermute | solution.py:74
  109.6 5.2 %collective-permute-done.15 = f32[256,512]{1,0:T(8,128)} collective-permute-done((f32[256,512]{1,0:T(8,128)}, f32[256,512]{1,0:T(8,128)}, u32[]{:S(2)}, u32[]{:S(2)}) %collective-permute-start.15) | collective-permute-done | bytes 524320 | tf_op jit(solution)/shard_map/ppermute | solution.py:74
  114.8 0.0 collective-permute-done.16
  114.8 2.7 %fusion.70 = f32[256,512]{1,0:T(8,128)S(1)} fusion(f32[256,512]{1,0:T(8,128)} %copy-done.5, f32[256,512]{1,0:T(8,128)S(1)} %get-tuple-element.6, f32[256,512]{1,0:T(8,128)} %collective-permute-done.15, f32[256,512]{1,0:T(8,128)} %collective-permute-done.16, f32[256,512]{1,0:T(8,128)} %get-tuple-element.20, f32[256,512]{1,0:T(8,128)S(1)} %copy-done.6, ...), kind=kLoop, calls=%fused_computation.116 | loop fusion | flops 2752512 | bytes 6291456 | tf_op jit(solution)/shard_map/add | solution.py:104
  117.5 0.8 copy-done.7
  118.3 4.9 %collective-permute-start.17 = (f32[64,512]{1,0:T(8,128)S(1)}, f32[64,512]{1,0:T(8,128)S(1)}, u32[]{:S(2)}, u32[]{:S(2)}) collective-permute-start(f32[64,512]{1,0:T(8,128)S(1)} %get-tuple-element.25), channel_id=1, source_target_pairs={{0,256},{64,320},{128,384},{192,448},{256,0},{320,64},{384,128},{4... | collective-permute-start | bytes 393224 | tf_op jit(solution)/shard_map/ppermute | solution.py:116
  123.2 2.5 %collective-permute-start.18 = (f32[64,512]{1,0:T(8,128)S(1)}, f32[64,512]{1,0:T(8,128)S(1)}, u32[]{:S(2)}, u32[]{:S(2)}) collective-permute-start(f32[64,512]{1,0:T(8,128)S(1)} %get-tuple-element.27), channel_id=1, source_target_pairs={{0,128},{64,192},{128,256},{192,320},{256,384},{320,448},{384,0},{... | collective-permute-start | bytes 393224 | tf_op jit(solution)/shard_map/ppermute | solution.py:116
  125.8 4.6 %collective-permute-start.19 = (f32[64,512]{1,0:T(8,128)S(1)}, f32[64,512]{1,0:T(8,128)S(1)}, u32[]{:S(2)}, u32[]{:S(2)}) collective-permute-start(f32[64,512]{1,0:T(8,128)S(1)} %get-tuple-element.26), channel_id=1, source_target_pairs={{0,384},{64,448},{128,0},{192,64},{256,128},{320,192},{384,256},{4... | collective-permute-start | bytes 393224 | tf_op jit(solution)/shard_map/ppermute | solution.py:116
  130.3 4.9 %collective-permute-start.21 = (f32[32,512]{1,0:T(8,128)S(1)}, f32[32,512]{1,0:T(8,128)S(1)}, u32[]{:S(2)}, u32[]{:S(2)}) collective-permute-start(f32[32,512]{1,0:T(8,128)S(1)} %dynamic-slice_bitcast_fusion), channel_id=1, source_target_pairs={{1,2},{2,1},{3,4},{4,3},{5,6},{6,5},{7,8},{8,7},{9,10},{10,9},{11,... | collective-permute-start | bytes 196616 | tf_op jit(solution)/shard_map/ppermute | solution.py:74
  135.2 1.9 %collective-permute-start.22 = (f32[32,512]{1,0:T(8,128)S(1)}, f32[32,512]{1,0:T(8,128)S(1)}, u32[]{:S(2)}, u32[]{:S(2)}) collective-permute-start(f32[32,512]{1,0:T(8,128)S(1)} %dynamic-slice_bitcast_fusion), channel_id=1, source_target_pairs={{0,1},{1,0},{2,3},{3,2},{4,5},{5,4},{6,7},{7,6},{8,9},{9,8},{10,11... | collective-permute-start | bytes 196616 | tf_op jit(solution)/shard_map/ppermute | solution.py:74
  137.2 0.0 collective-permute-done.18
  137.3 0.9 add_add_fusion
  138.2 2.0 %collective-permute-start.20 = (f32[32,512]{1,0:T(8,128)S(1)}, f32[32,512]{1,0:T(8,128)S(1)}, u32[]{:S(2)}, u32[]{:S(2)}) collective-permute-start(f32[32,512]{1,0:T(8,128)S(1)} %constant_dynamic-slice_fusion), channel_id=1, source_target_pairs={{0,64},{64,0},{128,192},{192,128},{256,320},{320,256},{384,448},{4... | collective-permute-start | bytes 196616 | tf_op jit(solution)/shard_map/ppermute | solution.py:122
  140.3 0.1 pad_slice_fusion.43
  140.4 0.0 collective-permute-done.21
  140.4 0.0 collective-permute-done.22
  140.4 9.5 %collective-permute-done.20 = f32[32,512]{1,0:T(8,128)S(1)} collective-permute-done((f32[32,512]{1,0:T(8,128)S(1)}, f32[32,512]{1,0:T(8,128)S(1)}, u32[]{:S(2)}, u32[]{:S(2)}) %collective-permute-start.20) | collective-permute-done | bytes 65568 | tf_op jit(solution)/shard_map/ppermute | solution.py:122
  149.9 0.7 fusion.82
  (23 shorter events, 0.1 us)
Async XLA Ops:
  0.0 23.3 %copy-start.3 = (f32[1,256,512]{2,1,0:T(8,128)S(1)}, f32[1,256,512]{2,1,0:T(8,128)}, u32[]{:S(2)}) copy-start(f32[1,256,512]{2,1,0:T(8,128)} %param.9) | copy-start | bytes 1572868
  0.0 23.3 %collective-permute-start.1 = (f32[4,256,512]{2,1,0:T(8,128)}, f32[4,256,512]{2,1,0:T(8,128)S(1)}, u32[]{:S(2)}, u32[]{:S(2)}) collective-permute-start(f32[4,256,512]{2,1,0:T(8,128)} %bitcast.96), channel_id=1, source_target_pairs={{0,1},{1,0},{2,3},{3,2},{4,5},{5,4},{6,7},{7,6},{8,9},{9,8},{10,11... | collective-permute-start | bytes 6291464 | tf_op jit(solution)/shard_map/ppermute | solution.py:76
  4.5 33.0 %copy-start.2 = (f32[1,256,512]{2,1,0:T(8,128)S(1)}, f32[1,256,512]{2,1,0:T(8,128)}, u32[]{:S(2)}) copy-start(f32[1,256,512]{2,1,0:T(8,128)} %param.8) | copy-start | bytes 1572868
  4.5 33.0 %copy-start.4 = (f32[1,256,512]{2,1,0:T(8,128)S(1)}, f32[1,256,512]{2,1,0:T(8,128)}, u32[]{:S(2)}) copy-start(f32[1,256,512]{2,1,0:T(8,128)} %param.7) | copy-start | bytes 1572868
  4.5 18.8 %collective-permute-start.2 = (f32[256,512]{1,0:T(8,128)S(1)}, f32[256,512]{1,0:T(8,128)S(1)}, u32[]{:S(2)}, u32[]{:S(2)}) collective-permute-start(f32[256,512]{1,0:T(8,128)S(1)} %get-tuple-element.22), channel_id=1, source_target_pairs={{1,2},{2,1},{3,4},{4,3},{5,6},{6,5},{7,8},{8,7},{9,10},{10,9},{11,... | collective-permute-start | bytes 1572872 | tf_op jit(solution)/shard_map/ppermute | solution.py:78
  16.5 18.0 %collective-permute-start.5 = (f32[256,512]{1,0:T(8,128)S(1)}, f32[256,512]{1,0:T(8,128)}, u32[]{:S(2)}, u32[]{:S(2)}) collective-permute-start(f32[256,512]{1,0:T(8,128)S(1)} %get-tuple-element.24), channel_id=1, source_target_pairs={{1,2},{2,1},{3,4},{4,3},{5,6},{6,5},{7,8},{8,7},{9,10},{10,9},{11,... | collective-permute-start | bytes 1572872 | tf_op jit(solution)/shard_map/ppermute | solution.py:78
  23.3 1.5 copy-start.8
  24.8 12.7 %collective-permute-start.3 = (f32[256,512]{1,0:T(8,128)S(1)}, f32[256,512]{1,0:T(8,128)}, u32[]{:S(2)}, u32[]{:S(2)}) collective-permute-start(f32[256,512]{1,0:T(8,128)S(1)} %get-tuple-element.19), channel_id=1, source_target_pairs={{1,2},{2,1},{3,4},{4,3},{5,6},{6,5},{7,8},{8,7},{9,10},{10,9},{11,... | collective-permute-start | bytes 1572872 | tf_op jit(solution)/shard_map/ppermute | solution.py:74
  30.6 7.0 %collective-permute-start.4 = (f32[256,512]{1,0:T(8,128)S(1)}, f32[256,512]{1,0:T(8,128)}, u32[]{:S(2)}, u32[]{:S(2)}) collective-permute-start(f32[256,512]{1,0:T(8,128)S(1)} %get-tuple-element.19), channel_id=1, source_target_pairs={{0,1},{1,0},{2,3},{3,2},{4,5},{5,4},{6,7},{7,6},{8,9},{9,8},{10,11... | collective-permute-start | bytes 1572872 | tf_op jit(solution)/shard_map/ppermute | solution.py:74
  32.5 18.0 %collective-permute-start.8 = (f32[256,512]{1,0:T(8,128)S(1)}, f32[256,512]{1,0:T(8,128)}, u32[]{:S(2)}, u32[]{:S(2)}) collective-permute-start(f32[256,512]{1,0:T(8,128)S(1)} %get-tuple-element.23), channel_id=1, source_target_pairs={{1,2},{2,1},{3,4},{4,3},{5,6},{6,5},{7,8},{8,7},{9,10},{10,9},{11,... | collective-permute-start | bytes 1572872 | tf_op jit(solution)/shard_map/ppermute | solution.py:78
  34.4 14.1 %copy-start.10 = (f32[256,512]{1,0:T(8,128)S(1)}, f32[256,512]{1,0:T(8,128)}, u32[]{:S(2)}) copy-start(f32[256,512]{1,0:T(8,128)} %get-tuple-element.21) | copy-start | bytes 1572868
  34.5 19.0 %copy-start.9 = (f32[4,256,512]{2,1,0:T(8,128)S(1)}, f32[4,256,512]{2,1,0:T(8,128)}, u32[]{:S(2)}) copy-start(f32[4,256,512]{2,1,0:T(8,128)} %copy-done.8) | copy-start | bytes 6291460
  40.9 12.6 %collective-permute-start.6 = (f32[256,512]{1,0:T(8,128)S(1)}, f32[256,512]{1,0:T(8,128)S(1)}, u32[]{:S(2)}, u32[]{:S(2)}) collective-permute-start(f32[256,512]{1,0:T(8,128)S(1)} %get-tuple-element.17), channel_id=1, source_target_pairs={{1,2},{2,1},{3,4},{4,3},{5,6},{6,5},{7,8},{8,7},{9,10},{10,9},{11,... | collective-permute-start | bytes 1572872 | tf_op jit(solution)/shard_map/ppermute | solution.py:74
  46.6 6.9 %collective-permute-start.7 = (f32[256,512]{1,0:T(8,128)S(1)}, f32[256,512]{1,0:T(8,128)S(1)}, u32[]{:S(2)}, u32[]{:S(2)}) collective-permute-start(f32[256,512]{1,0:T(8,128)S(1)} %get-tuple-element.17), channel_id=1, source_target_pairs={{0,1},{1,0},{2,3},{3,2},{4,5},{5,4},{6,7},{7,6},{8,9},{9,8},{10,11... | collective-permute-start | bytes 1572872 | tf_op jit(solution)/shard_map/ppermute | solution.py:74
  48.5 15.4 %copy-start = (s32[1,4096]{1,0:T(1,128)S(1)}, s32[1,4096]{1,0:T(1,128)}, u32[]{:S(2)}) copy-start(s32[1,4096]{1,0:T(1,128)} %index_ref.1) | copy-start | bytes 49156
  48.5 15.4 %copy-start.1 = (f32[1,4096]{1,0:T(1,128)S(1)}, f32[1,4096]{1,0:T(1,128)}, u32[]{:S(2)}) copy-start(f32[1,4096]{1,0:T(1,128)} %weight_ref.1) | copy-start | bytes 49156
  48.6 19.8 %collective-permute-start = (f32[256,512]{1,0:T(8,128)S(1)}, f32[256,512]{1,0:T(8,128)S(1)}, u32[]{:S(2)}, u32[]{:S(2)}) collective-permute-start(f32[256,512]{1,0:T(8,128)S(1)} %copy-done.10), channel_id=1, source_target_pairs={{1,2},{2,1},{3,4},{4,3},{5,6},{6,5},{7,8},{8,7},{9,10},{10,9},{11,... | collective-permute-start | bytes 1572872 | tf_op jit(solution)/shard_map/ppermute | solution.py:78
  56.3 12.0 %collective-permute-start.10 = (f32[256,512]{1,0:T(8,128)S(1)}, f32[256,512]{1,0:T(8,128)S(1)}, u32[]{:S(2)}, u32[]{:S(2)}) collective-permute-start(f32[256,512]{1,0:T(8,128)S(1)} %get-tuple-element.15), channel_id=1, source_target_pairs={{0,1},{1,0},{2,3},{3,2},{4,5},{5,4},{6,7},{7,6},{8,9},{9,8},{10,11... | collective-permute-start | bytes 1572872 | tf_op jit(solution)/shard_map/ppermute | solution.py:74
  58.2 12.6 %collective-permute-start.9 = (f32[256,512]{1,0:T(8,128)S(1)}, f32[256,512]{1,0:T(8,128)S(1)}, u32[]{:S(2)}, u32[]{:S(2)}) collective-permute-start(f32[256,512]{1,0:T(8,128)S(1)} %get-tuple-element.15), channel_id=1, source_target_pairs={{1,2},{2,1},{3,4},{4,3},{5,6},{6,5},{7,8},{8,7},{9,10},{10,9},{11,... | collective-permute-start | bytes 1572872 | tf_op jit(solution)/shard_map/ppermute | solution.py:74
  72.8 12.6 %collective-permute-start.11 = (f32[256,512]{1,0:T(8,128)S(1)}, f32[256,512]{1,0:T(8,128)S(1)}, u32[]{:S(2)}, u32[]{:S(2)}) collective-permute-start(f32[256,512]{1,0:T(8,128)S(1)} %add_select_fusion.5), channel_id=1, source_target_pairs={{1,2},{2,1},{3,4},{4,3},{5,6},{6,5},{7,8},{8,7},{9,10},{10,9},{11,... | collective-permute-start | bytes 1572872 | tf_op jit(solution)/shard_map/ppermute | solution.py:74
  78.6 6.9 %collective-permute-start.12 = (f32[256,512]{1,0:T(8,128)S(1)}, f32[256,512]{1,0:T(8,128)S(1)}, u32[]{:S(2)}, u32[]{:S(2)}) collective-permute-start(f32[256,512]{1,0:T(8,128)S(1)} %get-tuple-element.11), channel_id=1, source_target_pairs={{0,1},{1,0},{2,3},{3,2},{4,5},{5,4},{6,7},{7,6},{8,9},{9,8},{10,11... | collective-permute-start | bytes 1572872 | tf_op jit(solution)/shard_map/ppermute | solution.py:74
  86.2 12.6 %collective-permute-start.13 = (f32[256,512]{1,0:T(8,128)S(1)}, f32[256,512]{1,0:T(8,128)S(1)}, u32[]{:S(2)}, u32[]{:S(2)}) collective-permute-start(f32[256,512]{1,0:T(8,128)S(1)} %add_select_fusion.3), channel_id=1, source_target_pairs={{1,2},{2,1},{3,4},{4,3},{5,6},{6,5},{7,8},{8,7},{9,10},{10,9},{11,... | collective-permute-start | bytes 1572872 | tf_op jit(solution)/shard_map/ppermute | solution.py:74
  91.9 6.9 %collective-permute-start.14 = (f32[256,512]{1,0:T(8,128)S(1)}, f32[256,512]{1,0:T(8,128)S(1)}, u32[]{:S(2)}, u32[]{:S(2)}) collective-permute-start(f32[256,512]{1,0:T(8,128)S(1)} %get-tuple-element.8), channel_id=1, source_target_pairs={{0,1},{1,0},{2,3},{3,2},{4,5},{5,4},{6,7},{7,6},{8,9},{9,8},{10,11... | collective-permute-start | bytes 1572872 | tf_op jit(solution)/shard_map/ppermute | solution.py:74
  100.1 0.8 copy-start.5
  100.1 14.7 %copy-start.6 = (f32[256,512]{1,0:T(8,128)S(1)}, f32[256,512]{1,0:T(8,128)}, u32[]{:S(2)}) copy-start(f32[256,512]{1,0:T(8,128)} %get-tuple-element.18) | copy-start | bytes 1572868
  101.9 12.9 %collective-permute-start.15 = (f32[256,512]{1,0:T(8,128)}, f32[256,512]{1,0:T(8,128)}, u32[]{:S(2)}, u32[]{:S(2)}) collective-permute-start(f32[256,512]{1,0:T(8,128)} %add_select_fusion.1), channel_id=1, source_target_pairs={{1,2},{2,1},{3,4},{4,3},{5,6},{6,5},{7,8},{8,7},{9,10},{10,9},{11,... | collective-permute-start | bytes 1572872 | tf_op jit(solution)/shard_map/ppermute | solution.py:74
  107.6 7.2 %collective-permute-start.16 = (f32[256,512]{1,0:T(8,128)}, f32[256,512]{1,0:T(8,128)}, u32[]{:S(2)}, u32[]{:S(2)}) collective-permute-start(f32[256,512]{1,0:T(8,128)} %get-tuple-element.5), channel_id=1, source_target_pairs={{0,1},{1,0},{2,3},{3,2},{4,5},{5,4},{6,7},{7,6},{8,9},{9,8},{10,11... | collective-permute-start | bytes 1572872 | tf_op jit(solution)/shard_map/ppermute | solution.py:74
  117.5 0.8 copy-start.7
  118.3 18.9 %collective-permute-start.17 = (f32[64,512]{1,0:T(8,128)S(1)}, f32[64,512]{1,0:T(8,128)S(1)}, u32[]{:S(2)}, u32[]{:S(2)}) collective-permute-start(f32[64,512]{1,0:T(8,128)S(1)} %get-tuple-element.25), channel_id=1, source_target_pairs={{0,256},{64,320},{128,384},{192,448},{256,0},{320,64},{384,128},{4... | collective-permute-start | bytes 393224 | tf_op jit(solution)/shard_map/ppermute | solution.py:116
  123.2 14.0 %collective-permute-start.18 = (f32[64,512]{1,0:T(8,128)S(1)}, f32[64,512]{1,0:T(8,128)S(1)}, u32[]{:S(2)}, u32[]{:S(2)}) collective-permute-start(f32[64,512]{1,0:T(8,128)S(1)} %get-tuple-element.27), channel_id=1, source_target_pairs={{0,128},{64,192},{128,256},{192,320},{256,384},{320,448},{384,0},{... | collective-permute-start | bytes 393224 | tf_op jit(solution)/shard_map/ppermute | solution.py:116
  125.8 11.5 %collective-permute-start.19 = (f32[64,512]{1,0:T(8,128)S(1)}, f32[64,512]{1,0:T(8,128)S(1)}, u32[]{:S(2)}, u32[]{:S(2)}) collective-permute-start(f32[64,512]{1,0:T(8,128)S(1)} %get-tuple-element.26), channel_id=1, source_target_pairs={{0,384},{64,448},{128,0},{192,64},{256,128},{320,192},{384,256},{4... | collective-permute-start | bytes 393224 | tf_op jit(solution)/shard_map/ppermute | solution.py:116
  130.3 10.0 %collective-permute-start.21 = (f32[32,512]{1,0:T(8,128)S(1)}, f32[32,512]{1,0:T(8,128)S(1)}, u32[]{:S(2)}, u32[]{:S(2)}) collective-permute-start(f32[32,512]{1,0:T(8,128)S(1)} %dynamic-slice_bitcast_fusion), channel_id=1, source_target_pairs={{1,2},{2,1},{3,4},{4,3},{5,6},{6,5},{7,8},{8,7},{9,10},{10,9},{11,... | collective-permute-start | bytes 196616 | tf_op jit(solution)/shard_map/ppermute | solution.py:74
  135.2 5.1 %collective-permute-start.22 = (f32[32,512]{1,0:T(8,128)S(1)}, f32[32,512]{1,0:T(8,128)S(1)}, u32[]{:S(2)}, u32[]{:S(2)}) collective-permute-start(f32[32,512]{1,0:T(8,128)S(1)} %dynamic-slice_bitcast_fusion), channel_id=1, source_target_pairs={{0,1},{1,0},{2,3},{3,2},{4,5},{5,4},{6,7},{7,6},{8,9},{9,8},{10,11... | collective-permute-start | bytes 196616 | tf_op jit(solution)/shard_map/ppermute | solution.py:74
  138.2 11.7 %collective-permute-start.20 = (f32[32,512]{1,0:T(8,128)S(1)}, f32[32,512]{1,0:T(8,128)S(1)}, u32[]{:S(2)}, u32[]{:S(2)}) collective-permute-start(f32[32,512]{1,0:T(8,128)S(1)} %constant_dynamic-slice_fusion), channel_id=1, source_target_pairs={{0,64},{64,0},{128,192},{192,128},{256,320},{320,256},{384,448},{4... | collective-permute-start | bytes 196616 | tf_op jit(solution)/shard_map/ppermute | solution.py:122

commit v2 on v1

--- a/solution.py
+++ b/solution.py
@@ -4,6 +4,7 @@
 from jax.experimental import pallas as pl
 from jax.experimental.pallas import tpu as pltpu
 from jax.sharding import PartitionSpec as P
+
 
 source_gain = 0.2
 prior_gain = 0.5
@@ -57,6 +58,10 @@
     return total + wide[..., 1:-1, 2:] + wide[..., 1:-1, :-2] - 6.0 * field
 
 
+def hold(*values):
+    return lax.optimization_barrier(values)
+
+
 def local(forward_states, kappa, courant, direction, obs_index, obs_weight):
     states = forward_states[0, :, 0]
     kappa, courant, direction = kappa[0], courant[0], direction[0]
@@ -70,64 +75,64 @@
     far = [(g, g - 1 if g % 2 == 0 else g + 1) for g in range(slabs)]
     far = [(g, h) for g, h in far if 0 <= h < slabs]
 
-    def swap(far_field, near_field):
-        return lax.ppermute(far_field, "grid", far), lax.ppermute(near_field, "grid", near)
+    def across(field):
+        return lax.ppermute(field, "grid", far)
 
-    fars, nears = [], lax.ppermute(states, "grid", near)
-    for step in range(steps):
-        fars.append(lax.ppermute(states[step], "grid", far))
-    laps = [fars[k] + nears[k] + side_sum(states[k]) for k in range(steps)]
+    def beside(field):
+        return lax.ppermute(field, "grid", near)
+
+    overs = [across(states[0])]
+    nears = beside(states)
+    (later,) = hold(states)
+    for step in range(1, steps):
+        overs.append(across(later[step]))
+
+    far_gain = jnp.where(even, kappa + courant, kappa)
+    near_gain = jnp.where(even, kappa, kappa + courant)
+    pull = source_gain * direction
+    far_gain, near_gain, pull = hold(far_gain, near_gain, pull)
+
+    inner = [nears[k] + side_sum(later[k]) for k in range(steps)]
+    inner = list(hold(*inner))
+    laps = [overs[k] + inner[k] for k in range(steps)]
 
     weights = weight_field(obs_index, obs_weight, rows, columns)
 
-    tangent = source_gain * direction * laps[0]
+    tangent = pull * laps[0]
     for step in range(1, steps):
-        over, beside = swap(tangent, tangent)
-        below = jnp.where(even, over, beside)
-        tangent = (
-            tangent
-            + kappa * (over + beside + side_sum(tangent))
-            - courant * (tangent - below)
-            + source_gain * direction * laps[step]
-        )
+        over = across(tangent)
+        side = beside(tangent)
+        base = tangent + kappa * side_sum(tangent) - courant * tangent + pull * laps[step]
+        (base,) = hold(base)
+        (base,) = hold(base + near_gain * side)
+        tangent = base + far_gain * over
 
     adjoint = tangent * weights
-    partial_value = source_gain * laps[steps - 1] * adjoint
+    partial_value = None
     for step in range(steps - 2, -1, -1):
-        weighted = kappa * adjoint
-        carried = courant * adjoint
-        both = weighted + carried
-        over, beside = swap(
-            jnp.where(even, both, weighted), jnp.where(even, weighted, both)
-        )
-        adjoint = adjoint + (over + beside + side_sum(weighted)) - carried
-        partial_value = partial_value + source_gain * laps[step] * adjoint
+        over = across(far_gain * adjoint)
+        side = beside(near_gain * adjoint)
+        term = source_gain * laps[step + 1] * adjoint
+        partial_value = term if partial_value is None else partial_value + term
+        base = adjoint + side_sum(kappa * adjoint) - courant * adjoint
+        base, partial_value = hold(base, partial_value)
+        (base,) = hold(base + side)
+        if step:
+            adjoint = base + over
+    last = source_gain * laps[0]
+    last, rest = hold(last, partial_value + last * base)
+    partial_value = rest + last * over
 
     share = rows // scens
-    block = 2 * share
-    blocks = scens // 2
-    place, half = mine // 2, mine % 2
-    arrived = []
-    for hop in (2, 1, 3):
-        piece = lax.dynamic_slice_in_dim(
-            partial_value, ((place + hop) % blocks) * block, block, 0
-        )
-        ring = [(s, (s // 2 + hop) % blocks * 2 + s % 2) for s in range(scens)]
-        arrived.append(lax.ppermute(piece, "scen", ring))
-    total = lax.dynamic_slice_in_dim(partial_value, place * block, block, 0)
-    for piece in arrived:
-        total = total + piece
-    other = lax.dynamic_slice_in_dim(total, (1 - half) * share, share, 0)
-    kept = lax.dynamic_slice_in_dim(total, half * share, share, 0)
-    across = lax.ppermute(other, "scen", [(s, s ^ 1) for s in range(scens)])
+    pieces = lax.all_to_all(partial_value, "scen", 0, 0, tiled=True)
 
     own = lax.dynamic_slice_in_dim(direction, mine * share, share, 0)
-    over, beside = swap(own, own)
     tall = jnp.pad(direction, ((1, 1), (0, 0)))
     tall = lax.dynamic_slice_in_dim(tall, mine * share, share + 2, 0)
-    lap = over + beside + side_sum(tall)[1:-1]
+    lap = across(own) + beside(own) + side_sum(tall)[1:-1]
     prior = prior_gain * (own - prior_reach * lap)
-    return (kept + across + prior)[None]
+    (prior,) = hold(prior)
+    return (jnp.sum(pieces.reshape(scens, share, columns), 0) + prior)[None]
 
 
 def solution(mesh):

time: 152 us -> 161 us (1.059)
  the two profiles are of different devices: /device:TPU:40 before, /device:TPU:8 now
where the time goes in v2:
time: 161 us; the launch traced here: 160 us
  starting transfers between devices  81 us (50%)
  waiting for transfers between devices  57.2 us (36%)
  other arithmetic  11.6 us (7%)
  local copies, waits for them, and re-layouts  5.7 us (4%)
  Pallas kernels  4.3 us (3%)
    ppermute x11, starting transfers between devices, across(): return lax.ppermute(field, 'grid', far)  56.1 us
    ppermute x11, waiting for transfers between devices, across(): return lax.ppermute(field, 'grid', far)  50.6 us
    ppermute x8, starting transfers between devices, beside(): return lax.ppermute(field, 'grid', near)  15.4 us
    all_to_all x1, starting transfers between devices, local(): pieces = lax.all_to_all(partial_value, 'scen', 0, 0, tiled=True)  9.57 us
    all_to_all x1, waiting for transfers between devices, local(): pieces = lax.all_to_all(partial_value, 'scen', 0, 0, tiled=True)  6.59 us
    pallas_call x1, Pallas kernels, weight_field(): pl.pallas_call(weight_kernel, grid=(count // chunk,), in_specs=[pl.BlockS...  4.3 us
    add x1, other arithmetic, local(): inner = [nears[k] + side_sum(later[k]) for k in range(steps)]  3.72 us
  transfers between devices with their start and end apart: 20, of which 8 were waited for; matrix products, arithmetic and copies ran while one was open for 7% of the time, Pallas kernels for 3%

profile of v2, /device:TPU:8, one launch (start us, length us, event | category | flops | bytes accessed | tf_op | source)
XLA Modules:
  0.0 160.3 jit_solution(15962869513224248361)
XLA Ops:
  0.0 1.9 %collective-permute-start.1 = (f32[4,256,512]{2,1,0:T(8,128)}, f32[4,256,512]{2,1,0:T(8,128)}, u32[]{:S(2)}, u32[]{:S(2)}) collective-permute-start(f32[4,256,512]{2,1,0:T(8,128)} %bitcast.68), channel_id=1, source_target_pairs={{0,1},{1,0},{2,3},{3,2},{4,5},{5,4},{6,7},{7,6},{8,9},{9,8},{10,11... | collective-permute-start | bytes 6291464 | tf_op jit(solution)/shard_map/ppermute | solution.py:82
  1.9 1.9 %slice_bitcast_fusion.8 = f32[256,512]{1,0:T(8,128)} fusion(f32[1,4,1,256,512]{4,3,2,1,0:T(8,128)} %param.6), kind=kLoop, calls=%fused_computation.132 | loop fusion | bytes 1048576 | tf_op jit(solution)/shard_map/squeeze | solution.py:84
  3.8 11.1 %collective-permute-start = (f32[256,512]{1,0:T(8,128)}, f32[256,512]{1,0:T(8,128)S(1)}, u32[]{:S(2)}, u32[]{:S(2)}) collective-permute-start(f32[256,512]{1,0:T(8,128)} %slice_bitcast_fusion.8), channel_id=1, source_target_pairs={{1,2},{2,1},{3,4},{4,3},{5,6},{6,5},{7,8},{8,7},{9,10},{10,9},{11,... | collective-permute-start | bytes 1572872 | tf_op jit(solution)/shard_map/ppermute | solution.py:79
  14.9 2.7 %slice_bitcast_fusion = (f32[256,512]{1,0:T(8,128)S(1)}, f32[256,512]{1,0:T(8,128)}, f32[256,512]{1,0:T(8,128)}, f32[256,512]{1,0:T(8,128)}) fusion(f32[4,256,512]{2,1,0:T(8,128)} %bitcast.69), kind=kLoop, calls=%fused_computation.104 | loop fusion | bytes 4194304 | tf_op jit(solution)/shard_map/squeeze | solution.py:95
  17.6 1.9 %collective-permute-start.2 = (f32[256,512]{1,0:T(8,128)}, f32[256,512]{1,0:T(8,128)S(1)}, u32[]{:S(2)}, u32[]{:S(2)}) collective-permute-start(f32[256,512]{1,0:T(8,128)} %get-tuple-element.49), channel_id=1, source_target_pairs={{1,2},{2,1},{3,4},{4,3},{5,6},{6,5},{7,8},{8,7},{9,10},{10,9},{11,... | collective-permute-start | bytes 1572872 | tf_op jit(solution)/shard_map/ppermute | solution.py:79
  19.6 0.2 add_select_fusion
  19.8 0.0 collective-permute-done.1
  19.8 0.8 copy-done.5
  20.6 0.2 copy-done.6
  20.7 3.7 %fusion.19 = (f32[256,512]{1,0:T(8,128)S(1)}, f32[256,512]{1,0:T(8,128)S(1)}, f32[256,512]{1,0:T(8,128)S(1)}, f32[256,512]{1,0:T(8,128)S(1)}) fusion(f32[256,512]{1,0:T(8,128)S(1)} %get-tuple-element.47, f32[4,256,512]{2,1,0:T(8,128)} %collective-permute-done.1, f32[256,512]{1,0:T(8,128)S(1)} %copy-done.5, f32[256,512]{1,0:T(8,128)} %get-tuple-element.49, ...), kind=kLoop, calls=%fused_computation.61 | loop fusion | flops 3145728 | bytes 6291456 | tf_op jit(solution)/shard_map/add | solution.py:95
  24.5 0.2 add_multiply_fusion.1
  24.6 1.9 %collective-permute-start.3 = (f32[256,512]{1,0:T(8,128)S(1)}, f32[256,512]{1,0:T(8,128)S(1)}, u32[]{:S(2)}, u32[]{:S(2)}) collective-permute-start(f32[256,512]{1,0:T(8,128)S(1)} %add_multiply_fusion.1), channel_id=1, source_target_pairs={{0,1},{1,0},{2,3},{3,2},{4,5},{5,4},{6,7},{7,6},{8,9},{9,8},{10,11... | collective-permute-start | bytes 1572872 | tf_op jit(solution)/shard_map/ppermute | solution.py:82
  26.6 5.8 %collective-permute-start.5 = (f32[256,512]{1,0:T(8,128)S(1)}, f32[256,512]{1,0:T(8,128)S(1)}, u32[]{:S(2)}, u32[]{:S(2)}) collective-permute-start(f32[256,512]{1,0:T(8,128)S(1)} %copy-done.5), channel_id=1, source_target_pairs={{1,2},{2,1},{3,4},{4,3},{5,6},{6,5},{7,8},{8,7},{9,10},{10,9},{11,... | collective-permute-start | bytes 1572872 | tf_op jit(solution)/shard_map/ppermute | solution.py:79
  32.3 1.9 %collective-permute-start.4 = (f32[256,512]{1,0:T(8,128)S(1)}, f32[256,512]{1,0:T(8,128)S(1)}, u32[]{:S(2)}, u32[]{:S(2)}) collective-permute-start(f32[256,512]{1,0:T(8,128)S(1)} %add_multiply_fusion.1), channel_id=1, source_target_pairs={{1,2},{2,1},{3,4},{4,3},{5,6},{6,5},{7,8},{8,7},{9,10},{10,9},{11,... | collective-permute-start | bytes 1572872 | tf_op jit(solution)/shard_map/ppermute | solution.py:79
  34.3 0.6 fusion.27
  34.9 0.1 multiply_add_fusion.8
  35.1 9.9 %collective-permute-done.4 = f32[256,512]{1,0:T(8,128)S(1)} collective-permute-done((f32[256,512]{1,0:T(8,128)S(1)}, f32[256,512]{1,0:T(8,128)S(1)}, u32[]{:S(2)}, u32[]{:S(2)}) %collective-permute-start.4) | collective-permute-done | bytes 524320 | tf_op jit(solution)/shard_map/ppermute | solution.py:79
  44.9 0.2 multiply_add_fusion.7
  45.1 1.9 %collective-permute-start.6 = (f32[256,512]{1,0:T(8,128)S(1)}, f32[256,512]{1,0:T(8,128)S(1)}, u32[]{:S(2)}, u32[]{:S(2)}) collective-permute-start(f32[256,512]{1,0:T(8,128)S(1)} %multiply_add_fusion.7), channel_id=1, source_target_pairs={{0,1},{1,0},{2,3},{3,2},{4,5},{5,4},{6,7},{7,6},{8,9},{9,8},{10,11... | collective-permute-start | bytes 1572872 | tf_op jit(solution)/shard_map/ppermute | solution.py:82
  47.0 5.6 %collective-permute-start.8 = (f32[256,512]{1,0:T(8,128)S(1)}, f32[256,512]{1,0:T(8,128)S(1)}, u32[]{:S(2)}, u32[]{:S(2)}) collective-permute-start(f32[256,512]{1,0:T(8,128)S(1)} %get-tuple-element.47), channel_id=1, source_target_pairs={{1,2},{2,1},{3,4},{4,3},{5,6},{6,5},{7,8},{8,7},{9,10},{10,9},{11,... | collective-permute-start | bytes 1572872 | tf_op jit(solution)/shard_map/ppermute | solution.py:79
  52.7 2.1 %collective-permute-start.7 = (f32[256,512]{1,0:T(8,128)S(1)}, f32[256,512]{1,0:T(8,128)S(1)}, u32[]{:S(2)}, u32[]{:S(2)}) collective-permute-start(f32[256,512]{1,0:T(8,128)S(1)} %multiply_add_fusion.7), channel_id=1, source_target_pairs={{1,2},{2,1},{3,4},{4,3},{5,6},{6,5},{7,8},{8,7},{9,10},{10,9},{11,... | collective-permute-start | bytes 1572872 | tf_op jit(solution)/shard_map/ppermute | solution.py:79
  54.7 0.6 fusion.35
  55.4 0.0 copy-start
  55.4 0.0 copy-start.1
  55.4 0.1 multiply_add_fusion.6
  55.6 9.7 %collective-permute-done.7 = f32[256,512]{1,0:T(8,128)S(1)} collective-permute-done((f32[256,512]{1,0:T(8,128)S(1)}, f32[256,512]{1,0:T(8,128)S(1)}, u32[]{:S(2)}, u32[]{:S(2)}) %collective-permute-start.7) | collective-permute-done | bytes 524320 | tf_op jit(solution)/shard_map/ppermute | solution.py:79
  65.3 0.2 multiply_add_fusion.5
  65.4 1.9 %collective-permute-start.9 = (f32[256,512]{1,0:T(8,128)S(1)}, f32[256,512]{1,0:T(8,128)S(1)}, u32[]{:S(2)}, u32[]{:S(2)}) collective-permute-start(f32[256,512]{1,0:T(8,128)S(1)} %multiply_add_fusion.5), channel_id=1, source_target_pairs={{0,1},{1,0},{2,3},{3,2},{4,5},{5,4},{6,7},{7,6},{8,9},{9,8},{10,11... | collective-permute-start | bytes 1572872 | tf_op jit(solution)/shard_map/ppermute | solution.py:82
  67.4 4.3 %weight_field.1 = f32[256,512]{1,0:T(8,128)S(1)} custom-call(s32[1,4096]{1,0:T(1,128)S(1)} %copy-done, f32[1,4096]{1,0:T(1,128)S(1)} %copy-done.1), custom_call_target="tpu_custom_call" | custom-call | flops 3221225472 | bytes 524288 | tf_op jit(solution)/shard_map/weight_field/pallas_call | solution.py:41
  71.7 5.6 %collective-permute-start.10 = (f32[256,512]{1,0:T(8,128)S(1)}, f32[256,512]{1,0:T(8,128)S(1)}, u32[]{:S(2)}, u32[]{:S(2)}) collective-permute-start(f32[256,512]{1,0:T(8,128)S(1)} %multiply_add_fusion.5), channel_id=1, source_target_pairs={{1,2},{2,1},{3,4},{4,3},{5,6},{6,5},{7,8},{8,7},{9,10},{10,9},{11,... | collective-permute-start | bytes 1572872 | tf_op jit(solution)/shard_map/ppermute | solution.py:79
  77.3 0.6 fusion.43
  78.0 0.1 multiply_add_fusion.4
  78.1 6.2 %collective-permute-done.10 = f32[256,512]{1,0:T(8,128)S(1)} collective-permute-done((f32[256,512]{1,0:T(8,128)S(1)}, f32[256,512]{1,0:T(8,128)S(1)}, u32[]{:S(2)}, u32[]{:S(2)}) %collective-permute-start.10) | collective-permute-done | bytes 524320 | tf_op jit(solution)/shard_map/ppermute | solution.py:79
  84.3 0.2 fusion.70
  84.5 0.1 bitcast_multiply_fusion.7
  84.6 0.6 fusion.73
  85.2 1.9 %collective-permute-start.11 = (f32[256,512]{1,0:T(8,128)S(1)}, f32[256,512]{1,0:T(8,128)S(1)}, u32[]{:S(2)}, u32[]{:S(2)}) collective-permute-start(f32[256,512]{1,0:T(8,128)S(1)} %get-tuple-element.59), channel_id=1, source_target_pairs={{0,1},{1,0},{2,3},{3,2},{4,5},{5,4},{6,7},{7,6},{8,9},{9,8},{10,11... | collective-permute-start | bytes 1572872 | tf_op jit(solution)/shard_map/ppermute | solution.py:82
  87.1 5.6 %collective-permute-start.12 = (f32[256,512]{1,0:T(8,128)S(1)}, f32[256,512]{1,0:T(8,128)S(1)}, u32[]{:S(2)}, u32[]{:S(2)}) collective-permute-start(f32[256,512]{1,0:T(8,128)S(1)} %get-tuple-element.41), channel_id=1, source_target_pairs={{1,2},{2,1},{3,4},{4,3},{5,6},{6,5},{7,8},{8,7},{9,10},{10,9},{11,... | collective-permute-start | bytes 1572872 | tf_op jit(solution)/shard_map/ppermute | solution.py:79
  92.8 0.1 add.289
  92.8 6.9 %collective-permute-done.12 = f32[256,512]{1,0:T(8,128)S(1)} collective-permute-done((f32[256,512]{1,0:T(8,128)S(1)}, f32[256,512]{1,0:T(8,128)S(1)}, u32[]{:S(2)}, u32[]{:S(2)}) %collective-permute-start.12) | collective-permute-done | bytes 524320 | tf_op jit(solution)/shard_map/ppermute | solution.py:79
  99.7 0.1 fusion.69
  99.9 0.1 bitcast_multiply_fusion.6
  100.0 0.7 fusion.72
  100.6 1.9 %collective-permute-start.13 = (f32[256,512]{1,0:T(8,128)S(1)}, f32[256,512]{1,0:T(8,128)S(1)}, u32[]{:S(2)}, u32[]{:S(2)}) collective-permute-start(f32[256,512]{1,0:T(8,128)S(1)} %get-tuple-element.56), channel_id=1, source_target_pairs={{0,1},{1,0},{2,3},{3,2},{4,5},{5,4},{6,7},{7,6},{8,9},{9,8},{10,11... | collective-permute-start | bytes 1572872 | tf_op jit(solution)/shard_map/ppermute | solution.py:82
  102.6 5.6 %collective-permute-start.14 = (f32[256,512]{1,0:T(8,128)S(1)}, f32[256,512]{1,0:T(8,128)S(1)}, u32[]{:S(2)}, u32[]{:S(2)}) collective-permute-start(f32[256,512]{1,0:T(8,128)S(1)} %get-tuple-element.39), channel_id=1, source_target_pairs={{1,2},{2,1},{3,4},{4,3},{5,6},{6,5},{7,8},{8,7},{9,10},{10,9},{11,... | collective-permute-start | bytes 1572872 | tf_op jit(solution)/shard_map/ppermute | solution.py:79
  108.2 0.1 add.296
  108.3 6.9 %collective-permute-done.14 = f32[256,512]{1,0:T(8,128)S(1)} collective-permute-done((f32[256,512]{1,0:T(8,128)S(1)}, f32[256,512]{1,0:T(8,128)S(1)}, u32[]{:S(2)}, u32[]{:S(2)}) %collective-permute-start.14) | collective-permute-done | bytes 524320 | tf_op jit(solution)/shard_map/ppermute | solution.py:79
  115.2 0.1 fusion.68
  115.3 0.1 bitcast_multiply_fusion.8
  115.4 0.7 fusion.71
  116.1 1.9 %collective-permute-start.15 = (f32[256,512]{1,0:T(8,128)S(1)}, f32[256,512]{1,0:T(8,128)S(1)}, u32[]{:S(2)}, u32[]{:S(2)}) collective-permute-start(f32[256,512]{1,0:T(8,128)S(1)} %get-tuple-element.53), channel_id=1, source_target_pairs={{0,1},{1,0},{2,3},{3,2},{4,5},{5,4},{6,7},{7,6},{8,9},{9,8},{10,11... | collective-permute-start | bytes 1572872 | tf_op jit(solution)/shard_map/ppermute | solution.py:82
  118.0 5.6 %collective-permute-start.16 = (f32[256,512]{1,0:T(8,128)S(1)}, f32[256,512]{1,0:T(8,128)S(1)}, u32[]{:S(2)}, u32[]{:S(2)}) collective-permute-start(f32[256,512]{1,0:T(8,128)S(1)} %get-tuple-element.35), channel_id=1, source_target_pairs={{1,2},{2,1},{3,4},{4,3},{5,6},{6,5},{7,8},{8,7},{9,10},{10,9},{11,... | collective-permute-start | bytes 1572872 | tf_op jit(solution)/shard_map/ppermute | solution.py:79
  123.7 0.1 add.303
  123.8 0.2 multiply_add_fusion.1
  124.0 6.7 %collective-permute-done.16 = f32[256,512]{1,0:T(8,128)S(1)} collective-permute-done((f32[256,512]{1,0:T(8,128)S(1)}, f32[256,512]{1,0:T(8,128)S(1)}, u32[]{:S(2)}, u32[]{:S(2)}) %collective-permute-start.16) | collective-permute-done | bytes 524320 | tf_op jit(solution)/shard_map/ppermute | solution.py:79
  130.6 1.0 multiply_add_fusion
  131.6 9.6 %all-to-all-start = ((f32[8,32,512]{2,1,0:T(8,128)}), f32[8,32,512]{2,1,0:T(8,128)S(1)}, u32[]{:S(2)}, u32[]{:S(2)}) async-start(f32[8,32,512]{2,1,0:T(8,128)} %bitcast.13), calls=%async_computation | async-start | bytes 1048576 | tf_op jit(solution)/shard_map/all_to_all | solution.py:127
  141.2 5.3 %collective-permute-start.17 = (f32[32,512]{1,0:T(8,128)S(1)}, f32[32,512]{1,0:T(8,128)S(1)}, u32[]{:S(2)}, u32[]{:S(2)}) collective-permute-start(f32[32,512]{1,0:T(8,128)S(1)} %dynamic-slice_bitcast_fusion), channel_id=1, source_target_pairs={{1,2},{2,1},{3,4},{4,3},{5,6},{6,5},{7,8},{8,7},{9,10},{10,9},{11,... | collective-permute-start | bytes 196616 | tf_op jit(solution)/shard_map/ppermute | solution.py:79
  146.5 1.9 %collective-permute-start.18 = (f32[32,512]{1,0:T(8,128)S(1)}, f32[32,512]{1,0:T(8,128)S(1)}, u32[]{:S(2)}, u32[]{:S(2)}) collective-permute-start(f32[32,512]{1,0:T(8,128)S(1)} %dynamic-slice_bitcast_fusion), channel_id=1, source_target_pairs={{0,1},{1,0},{2,3},{3,2},{4,5},{5,4},{6,7},{7,6},{8,9},{9,8},{10,11... | collective-permute-start | bytes 196616 | tf_op jit(solution)/shard_map/ppermute | solution.py:82
  148.5 0.1 pad_slice_fusion.43
  148.6 4.4 %collective-permute-done.17 = f32[32,512]{1,0:T(8,128)S(1)} collective-permute-done((f32[32,512]{1,0:T(8,128)S(1)}, f32[32,512]{1,0:T(8,128)S(1)}, u32[]{:S(2)}, u32[]{:S(2)}) %collective-permute-start.17) | collective-permute-done | bytes 65568 | tf_op jit(solution)/shard_map/ppermute | solution.py:79
  153.0 0.1 fusion.67
  153.0 6.6 %all-to-all-done = f32[8,32,512]{2,1,0:T(8,128)S(1)} async-done(((f32[8,32,512]{2,1,0:T(8,128)}), f32[8,32,512]{2,1,0:T(8,128)S(1)}, u32[]{:S(2)}, u32[]{:S(2)}) %all-to-all-start) | async-done | bytes 524320 | tf_op jit(solution)/shard_map/all_to_all | solution.py:127
  159.7 0.6 add_bitcast_fusion
  (24 shorter events, 0.1 us)
Async XLA Ops:
  0.0 19.8 %collective-permute-start.1 = (f32[4,256,512]{2,1,0:T(8,128)}, f32[4,256,512]{2,1,0:T(8,128)}, u32[]{:S(2)}, u32[]{:S(2)}) collective-permute-start(f32[4,256,512]{2,1,0:T(8,128)} %bitcast.68), channel_id=1, source_target_pairs={{0,1},{1,0},{2,3},{3,2},{4,5},{5,4},{6,7},{7,6},{8,9},{9,8},{10,11... | collective-permute-start | bytes 6291464 | tf_op jit(solution)/shard_map/ppermute | solution.py:82
  3.8 15.7 %copy-start.2 = (f32[1,256,512]{2,1,0:T(8,128)S(1)}, f32[1,256,512]{2,1,0:T(8,128)}, u32[]{:S(2)}) copy-start(f32[1,256,512]{2,1,0:T(8,128)} %param.7) | copy-start | bytes 1572868
  3.8 15.7 %copy-start.3 = (f32[1,256,512]{2,1,0:T(8,128)S(1)}, f32[1,256,512]{2,1,0:T(8,128)}, u32[]{:S(2)}) copy-start(f32[1,256,512]{2,1,0:T(8,128)} %param.8) | copy-start | bytes 1572868
  3.8 15.7 %copy-start.4 = (f32[1,256,512]{2,1,0:T(8,128)S(1)}, f32[1,256,512]{2,1,0:T(8,128)}, u32[]{:S(2)}) copy-start(f32[1,256,512]{2,1,0:T(8,128)} %param.9) | copy-start | bytes 1572868
  3.8 20.7 %collective-permute-start = (f32[256,512]{1,0:T(8,128)}, f32[256,512]{1,0:T(8,128)S(1)}, u32[]{:S(2)}, u32[]{:S(2)}) collective-permute-start(f32[256,512]{1,0:T(8,128)} %slice_bitcast_fusion.8), channel_id=1, source_target_pairs={{1,2},{2,1},{3,4},{4,3},{5,6},{6,5},{7,8},{8,7},{9,10},{10,9},{11,... | collective-permute-start | bytes 1572872 | tf_op jit(solution)/shard_map/ppermute | solution.py:79
  17.6 16.7 %collective-permute-start.2 = (f32[256,512]{1,0:T(8,128)}, f32[256,512]{1,0:T(8,128)S(1)}, u32[]{:S(2)}, u32[]{:S(2)}) collective-permute-start(f32[256,512]{1,0:T(8,128)} %get-tuple-element.49), channel_id=1, source_target_pairs={{1,2},{2,1},{3,4},{4,3},{5,6},{6,5},{7,8},{8,7},{9,10},{10,9},{11,... | collective-permute-start | bytes 1572872 | tf_op jit(solution)/shard_map/ppermute | solution.py:79
  19.5 1.0 copy-start.5
  19.5 1.2 copy-start.6
  24.6 10.3 %collective-permute-start.3 = (f32[256,512]{1,0:T(8,128)S(1)}, f32[256,512]{1,0:T(8,128)S(1)}, u32[]{:S(2)}, u32[]{:S(2)}) collective-permute-start(f32[256,512]{1,0:T(8,128)S(1)} %add_multiply_fusion.1), channel_id=1, source_target_pairs={{0,1},{1,0},{2,3},{3,2},{4,5},{5,4},{6,7},{7,6},{8,9},{9,8},{10,11... | collective-permute-start | bytes 1572872 | tf_op jit(solution)/shard_map/ppermute | solution.py:82
  26.6 28.2 %collective-permute-start.5 = (f32[256,512]{1,0:T(8,128)S(1)}, f32[256,512]{1,0:T(8,128)S(1)}, u32[]{:S(2)}, u32[]{:S(2)}) collective-permute-start(f32[256,512]{1,0:T(8,128)S(1)} %copy-done.5), channel_id=1, source_target_pairs={{1,2},{2,1},{3,4},{4,3},{5,6},{6,5},{7,8},{8,7},{9,10},{10,9},{11,... | collective-permute-start | bytes 1572872 | tf_op jit(solution)/shard_map/ppermute | solution.py:79
  32.3 12.6 %collective-permute-start.4 = (f32[256,512]{1,0:T(8,128)S(1)}, f32[256,512]{1,0:T(8,128)S(1)}, u32[]{:S(2)}, u32[]{:S(2)}) collective-permute-start(f32[256,512]{1,0:T(8,128)S(1)} %add_multiply_fusion.1), channel_id=1, source_target_pairs={{1,2},{2,1},{3,4},{4,3},{5,6},{6,5},{7,8},{8,7},{9,10},{10,9},{11,... | collective-permute-start | bytes 1572872 | tf_op jit(solution)/shard_map/ppermute | solution.py:79
  45.1 10.3 %collective-permute-start.6 = (f32[256,512]{1,0:T(8,128)S(1)}, f32[256,512]{1,0:T(8,128)S(1)}, u32[]{:S(2)}, u32[]{:S(2)}) collective-permute-start(f32[256,512]{1,0:T(8,128)S(1)} %multiply_add_fusion.7), channel_id=1, source_target_pairs={{0,1},{1,0},{2,3},{3,2},{4,5},{5,4},{6,7},{7,6},{8,9},{9,8},{10,11... | collective-permute-start | bytes 1572872 | tf_op jit(solution)/shard_map/ppermute | solution.py:82
  47.0 30.3 %collective-permute-start.8 = (f32[256,512]{1,0:T(8,128)S(1)}, f32[256,512]{1,0:T(8,128)S(1)}, u32[]{:S(2)}, u32[]{:S(2)}) collective-permute-start(f32[256,512]{1,0:T(8,128)S(1)} %get-tuple-element.47), channel_id=1, source_target_pairs={{1,2},{2,1},{3,4},{4,3},{5,6},{6,5},{7,8},{8,7},{9,10},{10,9},{11,... | collective-permute-start | bytes 1572872 | tf_op jit(solution)/shard_map/ppermute | solution.py:79
  52.7 12.6 %collective-permute-start.7 = (f32[256,512]{1,0:T(8,128)S(1)}, f32[256,512]{1,0:T(8,128)S(1)}, u32[]{:S(2)}, u32[]{:S(2)}) collective-permute-start(f32[256,512]{1,0:T(8,128)S(1)} %multiply_add_fusion.7), channel_id=1, source_target_pairs={{1,2},{2,1},{3,4},{4,3},{5,6},{6,5},{7,8},{8,7},{9,10},{10,9},{11,... | collective-permute-start | bytes 1572872 | tf_op jit(solution)/shard_map/ppermute | solution.py:79
  55.4 12.0 %copy-start = (s32[1,4096]{1,0:T(1,128)S(1)}, s32[1,4096]{1,0:T(1,128)}, u32[]{:S(2)}) copy-start(s32[1,4096]{1,0:T(1,128)} %index_ref.1) | copy-start | bytes 49156
  55.4 12.0 %copy-start.1 = (f32[1,4096]{1,0:T(1,128)S(1)}, f32[1,4096]{1,0:T(1,128)}, u32[]{:S(2)}) copy-start(f32[1,4096]{1,0:T(1,128)} %weight_ref.1) | copy-start | bytes 49156
  65.4 12.5 %collective-permute-start.9 = (f32[256,512]{1,0:T(8,128)S(1)}, f32[256,512]{1,0:T(8,128)S(1)}, u32[]{:S(2)}, u32[]{:S(2)}) collective-permute-start(f32[256,512]{1,0:T(8,128)S(1)} %multiply_add_fusion.5), channel_id=1, source_target_pairs={{0,1},{1,0},{2,3},{3,2},{4,5},{5,4},{6,7},{7,6},{8,9},{9,8},{10,11... | collective-permute-start | bytes 1572872 | tf_op jit(solution)/shard_map/ppermute | solution.py:82
  71.7 12.6 %collective-permute-start.10 = (f32[256,512]{1,0:T(8,128)S(1)}, f32[256,512]{1,0:T(8,128)S(1)}, u32[]{:S(2)}, u32[]{:S(2)}) collective-permute-start(f32[256,512]{1,0:T(8,128)S(1)} %multiply_add_fusion.5), channel_id=1, source_target_pairs={{1,2},{2,1},{3,4},{4,3},{5,6},{6,5},{7,8},{8,7},{9,10},{10,9},{11,... | collective-permute-start | bytes 1572872 | tf_op jit(solution)/shard_map/ppermute | solution.py:79
  85.2 7.6 %collective-permute-start.11 = (f32[256,512]{1,0:T(8,128)S(1)}, f32[256,512]{1,0:T(8,128)S(1)}, u32[]{:S(2)}, u32[]{:S(2)}) collective-permute-start(f32[256,512]{1,0:T(8,128)S(1)} %get-tuple-element.59), channel_id=1, source_target_pairs={{0,1},{1,0},{2,3},{3,2},{4,5},{5,4},{6,7},{7,6},{8,9},{9,8},{10,11... | collective-permute-start | bytes 1572872 | tf_op jit(solution)/shard_map/ppermute | solution.py:82
  87.1 12.6 %collective-permute-start.12 = (f32[256,512]{1,0:T(8,128)S(1)}, f32[256,512]{1,0:T(8,128)S(1)}, u32[]{:S(2)}, u32[]{:S(2)}) collective-permute-start(f32[256,512]{1,0:T(8,128)S(1)} %get-tuple-element.41), channel_id=1, source_target_pairs={{1,2},{2,1},{3,4},{4,3},{5,6},{6,5},{7,8},{8,7},{9,10},{10,9},{11,... | collective-permute-start | bytes 1572872 | tf_op jit(solution)/shard_map/ppermute | solution.py:79
  100.6 7.6 %collective-permute-start.13 = (f32[256,512]{1,0:T(8,128)S(1)}, f32[256,512]{1,0:T(8,128)S(1)}, u32[]{:S(2)}, u32[]{:S(2)}) collective-permute-start(f32[256,512]{1,0:T(8,128)S(1)} %get-tuple-element.56), channel_id=1, source_target_pairs={{0,1},{1,0},{2,3},{3,2},{4,5},{5,4},{6,7},{7,6},{8,9},{9,8},{10,11... | collective-permute-start | bytes 1572872 | tf_op jit(solution)/shard_map/ppermute | solution.py:82
  102.6 12.6 %collective-permute-start.14 = (f32[256,512]{1,0:T(8,128)S(1)}, f32[256,512]{1,0:T(8,128)S(1)}, u32[]{:S(2)}, u32[]{:S(2)}) collective-permute-start(f32[256,512]{1,0:T(8,128)S(1)} %get-tuple-element.39), channel_id=1, source_target_pairs={{1,2},{2,1},{3,4},{4,3},{5,6},{6,5},{7,8},{8,7},{9,10},{10,9},{11,... | collective-permute-start | bytes 1572872 | tf_op jit(solution)/shard_map/ppermute | solution.py:79
  116.1 7.6 %collective-permute-start.15 = (f32[256,512]{1,0:T(8,128)S(1)}, f32[256,512]{1,0:T(8,128)S(1)}, u32[]{:S(2)}, u32[]{:S(2)}) collective-permute-start(f32[256,512]{1,0:T(8,128)S(1)} %get-tuple-element.53), channel_id=1, source_target_pairs={{0,1},{1,0},{2,3},{3,2},{4,5},{5,4},{6,7},{7,6},{8,9},{9,8},{10,11... | collective-permute-start | bytes 1572872 | tf_op jit(solution)/shard_map/ppermute | solution.py:82
  118.0 12.6 %collective-permute-start.16 = (f32[256,512]{1,0:T(8,128)S(1)}, f32[256,512]{1,0:T(8,128)S(1)}, u32[]{:S(2)}, u32[]{:S(2)}) collective-permute-start(f32[256,512]{1,0:T(8,128)S(1)} %get-tuple-element.35), channel_id=1, source_target_pairs={{1,2},{2,1},{3,4},{4,3},{5,6},{6,5},{7,8},{8,7},{9,10},{10,9},{11,... | collective-permute-start | bytes 1572872 | tf_op jit(solution)/shard_map/ppermute | solution.py:79
  131.6 28.0 %all-to-all-start = ((f32[8,32,512]{2,1,0:T(8,128)}), f32[8,32,512]{2,1,0:T(8,128)S(1)}, u32[]{:S(2)}, u32[]{:S(2)}) async-start(f32[8,32,512]{2,1,0:T(8,128)} %bitcast.13), calls=%async_computation | async-start | bytes 1048576 | tf_op jit(solution)/shard_map/all_to_all | solution.py:127
  141.2 11.8 %collective-permute-start.17 = (f32[32,512]{1,0:T(8,128)S(1)}, f32[32,512]{1,0:T(8,128)S(1)}, u32[]{:S(2)}, u32[]{:S(2)}) collective-permute-start(f32[32,512]{1,0:T(8,128)S(1)} %dynamic-slice_bitcast_fusion), channel_id=1, source_target_pairs={{1,2},{2,1},{3,4},{4,3},{5,6},{6,5},{7,8},{8,7},{9,10},{10,9},{11,... | collective-permute-start | bytes 196616 | tf_op jit(solution)/shard_map/ppermute | solution.py:79
  146.5 6.5 %collective-permute-start.18 = (f32[32,512]{1,0:T(8,128)S(1)}, f32[32,512]{1,0:T(8,128)S(1)}, u32[]{:S(2)}, u32[]{:S(2)}) collective-permute-start(f32[32,512]{1,0:T(8,128)S(1)} %dynamic-slice_bitcast_fusion), channel_id=1, source_target_pairs={{0,1},{1,0},{2,3},{3,2},{4,5},{5,4},{6,7},{7,6},{8,9},{9,8},{10,11... | collective-permute-start | bytes 196616 | tf_op jit(solution)/shard_map/ppermute | solution.py:82

commit v3 on v2

--- a/solution.py
+++ b/solution.py
@@ -68,8 +68,9 @@
     steps, rows, columns = states.shape
     slabs = lax.axis_size("grid")
     scens = lax.axis_size("scen")
-    even = lax.axis_index("grid") % 2 == 0
-    mine = lax.axis_index("scen")
+    share = rows // scens
+    even = (lax.axis_index("grid") & 1) == 0
+    first = (lax.axis_index("scen") * share).astype(jnp.uint32)
 
     near = [(g, g ^ 1) for g in range(slabs)]
     far = [(g, g - 1 if g % 2 == 0 else g + 1) for g in range(slabs)]
@@ -81,29 +82,42 @@
     def beside(field):
         return lax.ppermute(field, "grid", near)
 
-    overs = [across(states[0])]
+    states, even, first = hold(states, even, first)
+    over = across(states[0])
     nears = beside(states)
     (later,) = hold(states)
-    for step in range(1, steps):
-        overs.append(across(later[step]))
+    own = lax.dynamic_slice(direction, (first, jnp.uint32(0)), (share, columns))
+    sent, own = hold(jnp.concatenate([later[1], own]), own)
+    (later,) = hold(later)
+    fields = [states[0], sent[:rows], later[2], later[3]]
+    fields[2:] = hold(*fields[2:])
+    arrived = across(sent)
+    overs = [over, arrived[:rows]] + [across(fields[k]) for k in (2, 3)]
+    over_own = arrived[rows:]
 
     far_gain = jnp.where(even, kappa + courant, kappa)
     near_gain = jnp.where(even, kappa, kappa + courant)
-    pull = source_gain * direction
-    far_gain, near_gain, pull = hold(far_gain, near_gain, pull)
+    far_gain, near_gain = hold(far_gain, near_gain)
 
-    inner = [nears[k] + side_sum(later[k]) for k in range(steps)]
-    inner = list(hold(*inner))
-    laps = [overs[k] + inner[k] for k in range(steps)]
+    def lap_of(step):
+        return source_gain * (overs[step] + nears[step] + side_sum(fields[step]))
 
     weights = weight_field(obs_index, obs_weight, rows, columns)
 
-    tangent = pull * laps[0]
+    (inner,) = hold(nears[0] + side_sum(fields[0]))
+    laps = [source_gain * (inner + over)]
+    tangent = direction * laps[0]
+    tangent, laps[0] = hold(tangent, laps[0])
     for step in range(1, steps):
         over = across(tangent)
-        side = beside(tangent)
-        base = tangent + kappa * side_sum(tangent) - courant * tangent + pull * laps[step]
-        (base,) = hold(base)
+        if step == 1:
+            side = beside(jnp.concatenate([tangent, own]))
+            side, side_own = side[:rows], side[rows:]
+        else:
+            side = beside(tangent)
+        laps.append(lap_of(step))
+        base = tangent + kappa * side_sum(tangent) - courant * tangent + direction * laps[step]
+        base, laps[step] = hold(base, laps[step])
         (base,) = hold(base + near_gain * side)
         tangent = base + far_gain * over
 
@@ -112,26 +126,22 @@
     for step in range(steps - 2, -1, -1):
         over = across(far_gain * adjoint)
         side = beside(near_gain * adjoint)
-        term = source_gain * laps[step + 1] * adjoint
+        term = laps[step + 1] * adjoint
         partial_value = term if partial_value is None else partial_value + term
         base = adjoint + side_sum(kappa * adjoint) - courant * adjoint
         base, partial_value = hold(base, partial_value)
         (base,) = hold(base + side)
         if step:
             adjoint = base + over
-    last = source_gain * laps[0]
-    last, rest = hold(last, partial_value + last * base)
-    partial_value = rest + last * over
+    (rest,) = hold(partial_value + laps[0] * base)
+    partial_value = rest + laps[0] * over
 
-    share = rows // scens
     pieces = lax.all_to_all(partial_value, "scen", 0, 0, tiled=True)
 
-    own = lax.dynamic_slice_in_dim(direction, mine * share, share, 0)
     tall = jnp.pad(direction, ((1, 1), (0, 0)))
-    tall = lax.dynamic_slice_in_dim(tall, mine * share, share + 2, 0)
-    lap = across(own) + beside(own) + side_sum(tall)[1:-1]
-    prior = prior_gain * (own - prior_reach * lap)
-    (prior,) = hold(prior)
+    tall = lax.dynamic_slice(tall, (first, jnp.uint32(0)), (share + 2, columns))
+    lap = over_own + side_own + side_sum(tall)[1:-1]
+    (prior,) = hold(prior_gain * (own - prior_reach * lap))
     return (jnp.sum(pieces.reshape(scens, share, columns), 0) + prior)[None]
 
 

time: 161 us -> 157 us (0.975)
  waiting for transfers between devices: 57.2 us -> 67.5 us
  starting transfers between devices: 81 us -> 73.7 us
  other arithmetic: 11.6 us -> 8.05 us
  local copies, waits for them, and re-layouts: 5.7 us -> 2.44 us
    all_to_all x1, waiting for transfers between devices: 6.59 us -> 18.3 us  [local(): pieces = lax.all_to_all(partial_value, 'scen', 0, 0, tiled=True)]
    ppermute x11 -> x10, starting transfers between devices: 56.1 us -> 50.5 us  [across(): return lax.ppermute(field, 'grid', far)]
    add x6, other arithmetic: 6.79 us -> 3.9 us  [the longest x3 2.48 us: local(): tangent + kappa * side_sum(tangent) - courant * tangent]
    squeeze x2 -> x3, local copies, waits for them, and re-layouts: 4.58 us -> 2.23 us  [the longest x2 1.15 us: local(): fields = [states[0], sent[:rows], later[2], later[3]]]
    ppermute x8 -> x7, starting transfers between devices: 15.4 us -> 13.7 us  [beside(): return lax.ppermute(field, 'grid', near)]
    ppermute x11 -> x10, waiting for transfers between devices: 50.6 us -> 49.2 us  [across(): return lax.ppermute(field, 'grid', far)]
  transfers between devices with their start and end apart: 20 -> 18, of which waited for: 8 -> 8; matrix products, arithmetic and copies ran while one was open for 7% -> 4% of each run, Pallas kernels for 3% -> 3%
where the time goes in v3:
time: 157 us
  starting transfers between devices  73.7 us (47%)
  waiting for transfers between devices  67.5 us (43%)
  other arithmetic  8.05 us (5%)
  Pallas kernels  4.3 us (3%)
  local copies, waits for them, and re-layouts  2.44 us (2%)
    ppermute x10, starting transfers between devices, across(): return lax.ppermute(field, 'grid', far)  50.5 us
    ppermute x10, waiting for transfers between devices, across(): return lax.ppermute(field, 'grid', far)  49.2 us
    all_to_all x1, waiting for transfers between devices, local(): pieces = lax.all_to_all(partial_value, 'scen', 0, 0, tiled=True)  18.3 us
    ppermute x7, starting transfers between devices, beside(): return lax.ppermute(field, 'grid', near)  13.7 us
    all_to_all x1, starting transfers between devices, local(): pieces = lax.all_to_all(partial_value, 'scen', 0, 0, tiled=True)  9.56 us
    pallas_call x1, Pallas kernels, weight_field(): pl.pallas_call(weight_kernel, grid=(count // chunk,), in_specs=[pl.BlockS...  4.3 us
  transfers between devices with their start and end apart: 18, of which 8 were waited for; matrix products, arithmetic and copies ran while one was open for 4% of the time, Pallas kernels for 3%

profile of v3, /device:TPU:8, one launch (start us, length us, event | category | flops | bytes accessed | tf_op | source)
XLA Modules:
  0.0 156.5 jit_solution(15558811782407251572)
XLA Ops:
  0.0 2.0 %collective-permute-start = (f32[4,256,512]{2,1,0:T(8,128)}, f32[4,256,512]{2,1,0:T(8,128)S(1)}, u32[]{:S(2)}, u32[]{:S(2)}) collective-permute-start(f32[4,256,512]{2,1,0:T(8,128)} %bitcast.76), channel_id=1, source_target_pairs={{0,1},{1,0},{2,3},{3,2},{4,5},{5,4},{6,7},{7,6},{8,9},{9,8},{10,11... | collective-permute-start | bytes 6291464 | tf_op jit(solution)/shard_map/ppermute | solution.py:83
  2.1 1.1 slice_bitcast_fusion.7
  3.1 10.9 %collective-permute-start.1 = (f32[256,512]{1,0:T(8,128)S(1)}, f32[256,512]{1,0:T(8,128)S(1)}, u32[]{:S(2)}, u32[]{:S(2)}) collective-permute-start(f32[256,512]{1,0:T(8,128)S(1)} %slice_bitcast_fusion.7), channel_id=1, source_target_pairs={{1,2},{2,1},{3,4},{4,3},{5,6},{6,5},{7,8},{8,7},{9,10},{10,9},{11,... | collective-permute-start | bytes 1572872 | tf_op jit(solution)/shard_map/ppermute | solution.py:80
  14.1 1.1 slice_bitcast_fusion.5
  15.2 1.9 %collective-permute-start.2 = (f32[288,512]{1,0:T(8,128)S(1)}, f32[288,512]{1,0:T(8,128)S(1)}, u32[]{:S(2)}, u32[]{:S(2)}) collective-permute-start(f32[288,512]{1,0:T(8,128)S(1)} %pad_maximum_fusion), channel_id=1, source_target_pairs={{1,2},{2,1},{3,4},{4,3},{5,6},{6,5},{7,8},{8,7},{9,10},{10,9},{11,... | collective-permute-start | bytes 1769480 | tf_op jit(solution)/shard_map/ppermute | solution.py:80
  17.2 0.0 collective-permute-done
  17.2 0.3 fusion.4
  17.5 0.0 copy-start.5
  17.5 3.4 %collective-permute-done.1 = f32[256,512]{1,0:T(8,128)S(1)} collective-permute-done((f32[256,512]{1,0:T(8,128)S(1)}, f32[256,512]{1,0:T(8,128)S(1)}, u32[]{:S(2)}, u32[]{:S(2)}) %collective-permute-start.1) | collective-permute-done | bytes 524320 | tf_op jit(solution)/shard_map/ppermute | solution.py:80
  20.9 0.2 bitcast_multiply_fusion.9
  21.1 0.0 copy-start.3
  21.1 0.0 copy-start.4
  21.2 2.1 %collective-permute-start.3 = (f32[288,512]{1,0:T(8,128)S(1)}, f32[288,512]{1,0:T(8,128)S(1)}, u32[]{:S(2)}, u32[]{:S(2)}) collective-permute-start(f32[288,512]{1,0:T(8,128)S(1)} %pad_maximum_fusion.1), channel_id=1, source_target_pairs={{0,1},{1,0},{2,3},{3,2},{4,5},{5,4},{6,7},{7,6},{8,9},{9,8},{10,11... | collective-permute-start | bytes 1769480 | tf_op jit(solution)/shard_map/ppermute | solution.py:83
  23.3 0.1 slice_bitcast_fusion.2
  23.3 5.8 %collective-permute-start.5 = (f32[256,512]{1,0:T(8,128)S(1)}, f32[256,512]{1,0:T(8,128)S(1)}, u32[]{:S(2)}, u32[]{:S(2)}) collective-permute-start(f32[256,512]{1,0:T(8,128)S(1)} %get-tuple-element.37), channel_id=1, source_target_pairs={{1,2},{2,1},{3,4},{4,3},{5,6},{6,5},{7,8},{8,7},{9,10},{10,9},{11,... | collective-permute-start | bytes 1572872 | tf_op jit(solution)/shard_map/ppermute | solution.py:80
  29.1 1.9 %collective-permute-start.4 = (f32[256,512]{1,0:T(8,128)S(1)}, f32[256,512]{1,0:T(8,128)S(1)}, u32[]{:S(2)}, u32[]{:S(2)}) collective-permute-start(f32[256,512]{1,0:T(8,128)S(1)} %get-tuple-element.29), channel_id=1, source_target_pairs={{1,2},{2,1},{3,4},{4,3},{5,6},{6,5},{7,8},{8,7},{9,10},{10,9},{11,... | collective-permute-start | bytes 1572872 | tf_op jit(solution)/shard_map/ppermute | solution.py:80
  31.1 0.0 collective-permute-done.2
  31.1 0.9 fusion.12
  32.0 0.1 fusion.67
  32.2 9.6 %collective-permute-done.4 = f32[256,512]{1,0:T(8,128)S(1)} collective-permute-done((f32[256,512]{1,0:T(8,128)S(1)}, f32[256,512]{1,0:T(8,128)S(1)}, u32[]{:S(2)}, u32[]{:S(2)}) %collective-permute-start.4) | collective-permute-done | bytes 524320 | tf_op jit(solution)/shard_map/ppermute | solution.py:80
  41.7 0.1 multiply_add_fusion.7
  41.9 1.9 %collective-permute-start.6 = (f32[256,512]{1,0:T(8,128)S(1)}, f32[256,512]{1,0:T(8,128)S(1)}, u32[]{:S(2)}, u32[]{:S(2)}) collective-permute-start(f32[256,512]{1,0:T(8,128)S(1)} %multiply_add_fusion.7), channel_id=1, source_target_pairs={{0,1},{1,0},{2,3},{3,2},{4,5},{5,4},{6,7},{7,6},{8,9},{9,8},{10,11... | collective-permute-start | bytes 1572872 | tf_op jit(solution)/shard_map/ppermute | solution.py:83
  43.8 5.6 %collective-permute-start.8 = (f32[256,512]{1,0:T(8,128)S(1)}, f32[256,512]{1,0:T(8,128)S(1)}, u32[]{:S(2)}, u32[]{:S(2)}) collective-permute-start(f32[256,512]{1,0:T(8,128)S(1)} %get-tuple-element.39), channel_id=1, source_target_pairs={{1,2},{2,1},{3,4},{4,3},{5,6},{6,5},{7,8},{8,7},{9,10},{10,9},{11,... | collective-permute-start | bytes 1572872 | tf_op jit(solution)/shard_map/ppermute | solution.py:80
  49.4 2.1 %collective-permute-start.7 = (f32[256,512]{1,0:T(8,128)S(1)}, f32[256,512]{1,0:T(8,128)S(1)}, u32[]{:S(2)}, u32[]{:S(2)}) collective-permute-start(f32[256,512]{1,0:T(8,128)S(1)} %multiply_add_fusion.7), channel_id=1, source_target_pairs={{1,2},{2,1},{3,4},{4,3},{5,6},{6,5},{7,8},{8,7},{9,10},{10,9},{11,... | collective-permute-start | bytes 1572872 | tf_op jit(solution)/shard_map/ppermute | solution.py:80
  51.5 0.8 fusion.26
  52.3 0.0 copy-start
  52.3 0.0 copy-start.1
  52.4 0.1 multiply_add_fusion.6
  52.5 9.5 %collective-permute-done.7 = f32[256,512]{1,0:T(8,128)S(1)} collective-permute-done((f32[256,512]{1,0:T(8,128)S(1)}, f32[256,512]{1,0:T(8,128)S(1)}, u32[]{:S(2)}, u32[]{:S(2)}) %collective-permute-start.7) | collective-permute-done | bytes 524320 | tf_op jit(solution)/shard_map/ppermute | solution.py:80
  62.0 0.1 multiply_add_fusion.5
  62.2 1.9 %collective-permute-start.9 = (f32[256,512]{1,0:T(8,128)S(1)}, f32[256,512]{1,0:T(8,128)S(1)}, u32[]{:S(2)}, u32[]{:S(2)}) collective-permute-start(f32[256,512]{1,0:T(8,128)S(1)} %multiply_add_fusion.5), channel_id=1, source_target_pairs={{0,1},{1,0},{2,3},{3,2},{4,5},{5,4},{6,7},{7,6},{8,9},{9,8},{10,11... | collective-permute-start | bytes 1572872 | tf_op jit(solution)/shard_map/ppermute | solution.py:83
  64.1 4.3 %weight_field.1 = f32[256,512]{1,0:T(8,128)S(1)} custom-call(s32[1,4096]{1,0:T(1,128)S(1)} %copy-done, f32[1,4096]{1,0:T(1,128)S(1)} %copy-done.1), custom_call_target="tpu_custom_call" | custom-call | flops 3221225472 | bytes 524288 | tf_op jit(solution)/shard_map/weight_field/pallas_call | solution.py:41
  68.5 5.6 %collective-permute-start.10 = (f32[256,512]{1,0:T(8,128)S(1)}, f32[256,512]{1,0:T(8,128)S(1)}, u32[]{:S(2)}, u32[]{:S(2)}) collective-permute-start(f32[256,512]{1,0:T(8,128)S(1)} %multiply_add_fusion.5), channel_id=1, source_target_pairs={{1,2},{2,1},{3,4},{4,3},{5,6},{6,5},{7,8},{8,7},{9,10},{10,9},{11,... | collective-permute-start | bytes 1572872 | tf_op jit(solution)/shard_map/ppermute | solution.py:80
  74.0 0.8 fusion.40
  74.8 0.1 multiply_add_fusion.4
  75.0 6.1 %collective-permute-done.10 = f32[256,512]{1,0:T(8,128)S(1)} collective-permute-done((f32[256,512]{1,0:T(8,128)S(1)}, f32[256,512]{1,0:T(8,128)S(1)}, u32[]{:S(2)}, u32[]{:S(2)}) %collective-permute-start.10) | collective-permute-done | bytes 524320 | tf_op jit(solution)/shard_map/ppermute | solution.py:80
  81.1 0.2 fusion.77
  81.3 0.1 bitcast_multiply_fusion.7
  81.4 0.4 fusion.83
  81.8 1.9 %collective-permute-start.11 = (f32[256,512]{1,0:T(8,128)S(1)}, f32[256,512]{1,0:T(8,128)S(1)}, u32[]{:S(2)}, u32[]{:S(2)}) collective-permute-start(f32[256,512]{1,0:T(8,128)S(1)} %get-tuple-element.75), channel_id=1, source_target_pairs={{0,1},{1,0},{2,3},{3,2},{4,5},{5,4},{6,7},{7,6},{8,9},{9,8},{10,11... | collective-permute-start | bytes 1572872 | tf_op jit(solution)/shard_map/ppermute | solution.py:83
  83.7 5.6 %collective-permute-start.12 = (f32[256,512]{1,0:T(8,128)S(1)}, f32[256,512]{1,0:T(8,128)S(1)}, u32[]{:S(2)}, u32[]{:S(2)}) collective-permute-start(f32[256,512]{1,0:T(8,128)S(1)} %get-tuple-element.55), channel_id=1, source_target_pairs={{1,2},{2,1},{3,4},{4,3},{5,6},{6,5},{7,8},{8,7},{9,10},{10,9},{11,... | collective-permute-start | bytes 1572872 | tf_op jit(solution)/shard_map/ppermute | solution.py:80
  89.3 0.1 add.278
  89.4 6.9 %collective-permute-done.12 = f32[256,512]{1,0:T(8,128)S(1)} collective-permute-done((f32[256,512]{1,0:T(8,128)S(1)}, f32[256,512]{1,0:T(8,128)S(1)}, u32[]{:S(2)}, u32[]{:S(2)}) %collective-permute-start.12) | collective-permute-done | bytes 524320 | tf_op jit(solution)/shard_map/ppermute | solution.py:80
  96.3 0.1 fusion.76
  96.5 0.1 bitcast_multiply_fusion.6
  96.6 0.5 fusion.82
  97.1 1.9 %collective-permute-start.13 = (f32[256,512]{1,0:T(8,128)S(1)}, f32[256,512]{1,0:T(8,128)S(1)}, u32[]{:S(2)}, u32[]{:S(2)}) collective-permute-start(f32[256,512]{1,0:T(8,128)S(1)} %get-tuple-element.72), channel_id=1, source_target_pairs={{0,1},{1,0},{2,3},{3,2},{4,5},{5,4},{6,7},{7,6},{8,9},{9,8},{10,11... | collective-permute-start | bytes 1572872 | tf_op jit(solution)/shard_map/ppermute | solution.py:83
  99.0 5.6 %collective-permute-start.14 = (f32[256,512]{1,0:T(8,128)S(1)}, f32[256,512]{1,0:T(8,128)S(1)}, u32[]{:S(2)}, u32[]{:S(2)}) collective-permute-start(f32[256,512]{1,0:T(8,128)S(1)} %get-tuple-element.53), channel_id=1, source_target_pairs={{1,2},{2,1},{3,4},{4,3},{5,6},{6,5},{7,8},{8,7},{9,10},{10,9},{11,... | collective-permute-start | bytes 1572872 | tf_op jit(solution)/shard_map/ppermute | solution.py:80
  104.6 0.1 add.285
  104.7 6.9 %collective-permute-done.14 = f32[256,512]{1,0:T(8,128)S(1)} collective-permute-done((f32[256,512]{1,0:T(8,128)S(1)}, f32[256,512]{1,0:T(8,128)S(1)}, u32[]{:S(2)}, u32[]{:S(2)}) %collective-permute-start.14) | collective-permute-done | bytes 524320 | tf_op jit(solution)/shard_map/ppermute | solution.py:80
  111.6 0.1 fusion.75
  111.8 0.1 bitcast_multiply_fusion.8
  111.9 0.5 fusion.81
  112.4 1.9 %collective-permute-start.15 = (f32[256,512]{1,0:T(8,128)S(1)}, f32[256,512]{1,0:T(8,128)S(1)}, u32[]{:S(2)}, u32[]{:S(2)}) collective-permute-start(f32[256,512]{1,0:T(8,128)S(1)} %get-tuple-element.69), channel_id=1, source_target_pairs={{0,1},{1,0},{2,3},{3,2},{4,5},{5,4},{6,7},{7,6},{8,9},{9,8},{10,11... | collective-permute-start | bytes 1572872 | tf_op jit(solution)/shard_map/ppermute | solution.py:83
  114.3 5.6 %collective-permute-start.16 = (f32[256,512]{1,0:T(8,128)S(1)}, f32[256,512]{1,0:T(8,128)S(1)}, u32[]{:S(2)}, u32[]{:S(2)}) collective-permute-start(f32[256,512]{1,0:T(8,128)S(1)} %get-tuple-element.51), channel_id=1, source_target_pairs={{1,2},{2,1},{3,4},{4,3},{5,6},{6,5},{7,8},{8,7},{9,10},{10,9},{11,... | collective-permute-start | bytes 1572872 | tf_op jit(solution)/shard_map/ppermute | solution.py:80
  119.9 0.1 add.292
  120.0 0.1 multiply_add_fusion.1
  120.1 6.8 %collective-permute-done.16 = f32[256,512]{1,0:T(8,128)S(1)} collective-permute-done((f32[256,512]{1,0:T(8,128)S(1)}, f32[256,512]{1,0:T(8,128)S(1)}, u32[]{:S(2)}, u32[]{:S(2)}) %collective-permute-start.16) | collective-permute-done | bytes 524320 | tf_op jit(solution)/shard_map/ppermute | solution.py:80
  126.9 0.9 multiply_add_fusion
  127.8 9.6 %all-to-all-start = ((f32[8,32,512]{2,1,0:T(8,128)}), f32[8,32,512]{2,1,0:T(8,128)S(1)}, u32[]{:S(2)}, u32[]{:S(2)}) async-start(f32[8,32,512]{2,1,0:T(8,128)} %bitcast.13), calls=%async_computation | async-start | bytes 1048576 | tf_op jit(solution)/shard_map/all_to_all | solution.py:139
  137.4 0.1 pad_slice_fusion.43
  137.5 0.1 fusion.74
  137.6 18.3 %all-to-all-done = f32[8,32,512]{2,1,0:T(8,128)S(1)} async-done(((f32[8,32,512]{2,1,0:T(8,128)}), f32[8,32,512]{2,1,0:T(8,128)S(1)}, u32[]{:S(2)}, u32[]{:S(2)}) %all-to-all-start) | async-done | bytes 524320 | tf_op jit(solution)/shard_map/all_to_all | solution.py:139
  155.9 0.6 add_bitcast_fusion
  (21 shorter events, 0.2 us)
Async XLA Ops:
  0.0 15.2 %copy-start.2 = (f32[1,256,512]{2,1,0:T(8,128)S(1)}, f32[1,256,512]{2,1,0:T(8,128)}, u32[]{:S(2)}) copy-start(f32[1,256,512]{2,1,0:T(8,128)} %param.9) | copy-start | bytes 1572868
  0.0 17.2 %collective-permute-start = (f32[4,256,512]{2,1,0:T(8,128)}, f32[4,256,512]{2,1,0:T(8,128)S(1)}, u32[]{:S(2)}, u32[]{:S(2)}) collective-permute-start(f32[4,256,512]{2,1,0:T(8,128)} %bitcast.76), channel_id=1, source_target_pairs={{0,1},{1,0},{2,3},{3,2},{4,5},{5,4},{6,7},{7,6},{8,9},{9,8},{10,11... | collective-permute-start | bytes 6291464 | tf_op jit(solution)/shard_map/ppermute | solution.py:83
  3.1 17.8 %collective-permute-start.1 = (f32[256,512]{1,0:T(8,128)S(1)}, f32[256,512]{1,0:T(8,128)S(1)}, u32[]{:S(2)}, u32[]{:S(2)}) collective-permute-start(f32[256,512]{1,0:T(8,128)S(1)} %slice_bitcast_fusion.7), channel_id=1, source_target_pairs={{1,2},{2,1},{3,4},{4,3},{5,6},{6,5},{7,8},{8,7},{9,10},{10,9},{11,... | collective-permute-start | bytes 1572872 | tf_op jit(solution)/shard_map/ppermute | solution.py:80
  15.2 15.8 %collective-permute-start.2 = (f32[288,512]{1,0:T(8,128)S(1)}, f32[288,512]{1,0:T(8,128)S(1)}, u32[]{:S(2)}, u32[]{:S(2)}) collective-permute-start(f32[288,512]{1,0:T(8,128)S(1)} %pad_maximum_fusion), channel_id=1, source_target_pairs={{1,2},{2,1},{3,4},{4,3},{5,6},{6,5},{7,8},{8,7},{9,10},{10,9},{11,... | collective-permute-start | bytes 1769480 | tf_op jit(solution)/shard_map/ppermute | solution.py:80
  17.5 5.7 %copy-start.5 = (f32[1,4,1,256,512]{4,3,2,1,0:T(8,128)S(1)}, f32[1,4,1,256,512]{4,3,2,1,0:T(8,128)}, u32[]{:S(2)}) copy-start(f32[1,4,1,256,512]{4,3,2,1,0:T(8,128)} %param.6) | copy-start | bytes 6291460
  21.1 10.0 %copy-start.3 = (f32[1,256,512]{2,1,0:T(8,128)S(1)}, f32[1,256,512]{2,1,0:T(8,128)}, u32[]{:S(2)}) copy-start(f32[1,256,512]{2,1,0:T(8,128)} %param.7) | copy-start | bytes 1572868
  21.1 10.0 %copy-start.4 = (f32[1,256,512]{2,1,0:T(8,128)S(1)}, f32[1,256,512]{2,1,0:T(8,128)}, u32[]{:S(2)}) copy-start(f32[1,256,512]{2,1,0:T(8,128)} %param.8) | copy-start | bytes 1572868
  21.2 10.8 %collective-permute-start.3 = (f32[288,512]{1,0:T(8,128)S(1)}, f32[288,512]{1,0:T(8,128)S(1)}, u32[]{:S(2)}, u32[]{:S(2)}) collective-permute-start(f32[288,512]{1,0:T(8,128)S(1)} %pad_maximum_fusion.1), channel_id=1, source_target_pairs={{0,1},{1,0},{2,3},{3,2},{4,5},{5,4},{6,7},{7,6},{8,9},{9,8},{10,11... | collective-permute-start | bytes 1769480 | tf_op jit(solution)/shard_map/ppermute | solution.py:83
  23.3 28.2 %collective-permute-start.5 = (f32[256,512]{1,0:T(8,128)S(1)}, f32[256,512]{1,0:T(8,128)S(1)}, u32[]{:S(2)}, u32[]{:S(2)}) collective-permute-start(f32[256,512]{1,0:T(8,128)S(1)} %get-tuple-element.37), channel_id=1, source_target_pairs={{1,2},{2,1},{3,4},{4,3},{5,6},{6,5},{7,8},{8,7},{9,10},{10,9},{11,... | collective-permute-start | bytes 1572872 | tf_op jit(solution)/shard_map/ppermute | solution.py:80
  29.1 12.6 %collective-permute-start.4 = (f32[256,512]{1,0:T(8,128)S(1)}, f32[256,512]{1,0:T(8,128)S(1)}, u32[]{:S(2)}, u32[]{:S(2)}) collective-permute-start(f32[256,512]{1,0:T(8,128)S(1)} %get-tuple-element.29), channel_id=1, source_target_pairs={{1,2},{2,1},{3,4},{4,3},{5,6},{6,5},{7,8},{8,7},{9,10},{10,9},{11,... | collective-permute-start | bytes 1572872 | tf_op jit(solution)/shard_map/ppermute | solution.py:80
  41.9 10.4 %collective-permute-start.6 = (f32[256,512]{1,0:T(8,128)S(1)}, f32[256,512]{1,0:T(8,128)S(1)}, u32[]{:S(2)}, u32[]{:S(2)}) collective-permute-start(f32[256,512]{1,0:T(8,128)S(1)} %multiply_add_fusion.7), channel_id=1, source_target_pairs={{0,1},{1,0},{2,3},{3,2},{4,5},{5,4},{6,7},{7,6},{8,9},{9,8},{10,11... | collective-permute-start | bytes 1572872 | tf_op jit(solution)/shard_map/ppermute | solution.py:83
  43.8 30.2 %collective-permute-start.8 = (f32[256,512]{1,0:T(8,128)S(1)}, f32[256,512]{1,0:T(8,128)S(1)}, u32[]{:S(2)}, u32[]{:S(2)}) collective-permute-start(f32[256,512]{1,0:T(8,128)S(1)} %get-tuple-element.39), channel_id=1, source_target_pairs={{1,2},{2,1},{3,4},{4,3},{5,6},{6,5},{7,8},{8,7},{9,10},{10,9},{11,... | collective-permute-start | bytes 1572872 | tf_op jit(solution)/shard_map/ppermute | solution.py:80
  49.4 12.7 %collective-permute-start.7 = (f32[256,512]{1,0:T(8,128)S(1)}, f32[256,512]{1,0:T(8,128)S(1)}, u32[]{:S(2)}, u32[]{:S(2)}) collective-permute-start(f32[256,512]{1,0:T(8,128)S(1)} %multiply_add_fusion.7), channel_id=1, source_target_pairs={{1,2},{2,1},{3,4},{4,3},{5,6},{6,5},{7,8},{8,7},{9,10},{10,9},{11,... | collective-permute-start | bytes 1572872 | tf_op jit(solution)/shard_map/ppermute | solution.py:80
  52.3 11.8 %copy-start = (s32[1,4096]{1,0:T(1,128)S(1)}, s32[1,4096]{1,0:T(1,128)}, u32[]{:S(2)}) copy-start(s32[1,4096]{1,0:T(1,128)} %index_ref.1) | copy-start | bytes 49156
  52.3 11.8 %copy-start.1 = (f32[1,4096]{1,0:T(1,128)S(1)}, f32[1,4096]{1,0:T(1,128)}, u32[]{:S(2)}) copy-start(f32[1,4096]{1,0:T(1,128)} %weight_ref.1) | copy-start | bytes 49156
  62.2 12.6 %collective-permute-start.9 = (f32[256,512]{1,0:T(8,128)S(1)}, f32[256,512]{1,0:T(8,128)S(1)}, u32[]{:S(2)}, u32[]{:S(2)}) collective-permute-start(f32[256,512]{1,0:T(8,128)S(1)} %multiply_add_fusion.5), channel_id=1, source_target_pairs={{0,1},{1,0},{2,3},{3,2},{4,5},{5,4},{6,7},{7,6},{8,9},{9,8},{10,11... | collective-permute-start | bytes 1572872 | tf_op jit(solution)/shard_map/ppermute | solution.py:83
  68.5 12.6 %collective-permute-start.10 = (f32[256,512]{1,0:T(8,128)S(1)}, f32[256,512]{1,0:T(8,128)S(1)}, u32[]{:S(2)}, u32[]{:S(2)}) collective-permute-start(f32[256,512]{1,0:T(8,128)S(1)} %multiply_add_fusion.5), channel_id=1, source_target_pairs={{1,2},{2,1},{3,4},{4,3},{5,6},{6,5},{7,8},{8,7},{9,10},{10,9},{11,... | collective-permute-start | bytes 1572872 | tf_op jit(solution)/shard_map/ppermute | solution.py:80
  81.8 7.5 %collective-permute-start.11 = (f32[256,512]{1,0:T(8,128)S(1)}, f32[256,512]{1,0:T(8,128)S(1)}, u32[]{:S(2)}, u32[]{:S(2)}) collective-permute-start(f32[256,512]{1,0:T(8,128)S(1)} %get-tuple-element.75), channel_id=1, source_target_pairs={{0,1},{1,0},{2,3},{3,2},{4,5},{5,4},{6,7},{7,6},{8,9},{9,8},{10,11... | collective-permute-start | bytes 1572872 | tf_op jit(solution)/shard_map/ppermute | solution.py:83
  83.7 12.6 %collective-permute-start.12 = (f32[256,512]{1,0:T(8,128)S(1)}, f32[256,512]{1,0:T(8,128)S(1)}, u32[]{:S(2)}, u32[]{:S(2)}) collective-permute-start(f32[256,512]{1,0:T(8,128)S(1)} %get-tuple-element.55), channel_id=1, source_target_pairs={{1,2},{2,1},{3,4},{4,3},{5,6},{6,5},{7,8},{8,7},{9,10},{10,9},{11,... | collective-permute-start | bytes 1572872 | tf_op jit(solution)/shard_map/ppermute | solution.py:80
  97.1 7.5 %collective-permute-start.13 = (f32[256,512]{1,0:T(8,128)S(1)}, f32[256,512]{1,0:T(8,128)S(1)}, u32[]{:S(2)}, u32[]{:S(2)}) collective-permute-start(f32[256,512]{1,0:T(8,128)S(1)} %get-tuple-element.72), channel_id=1, source_target_pairs={{0,1},{1,0},{2,3},{3,2},{4,5},{5,4},{6,7},{7,6},{8,9},{9,8},{10,11... | collective-permute-start | bytes 1572872 | tf_op jit(solution)/shard_map/ppermute | solution.py:83
  99.0 12.6 %collective-permute-start.14 = (f32[256,512]{1,0:T(8,128)S(1)}, f32[256,512]{1,0:T(8,128)S(1)}, u32[]{:S(2)}, u32[]{:S(2)}) collective-permute-start(f32[256,512]{1,0:T(8,128)S(1)} %get-tuple-element.53), channel_id=1, source_target_pairs={{1,2},{2,1},{3,4},{4,3},{5,6},{6,5},{7,8},{8,7},{9,10},{10,9},{11,... | collective-permute-start | bytes 1572872 | tf_op jit(solution)/shard_map/ppermute | solution.py:80
  112.4 7.5 %collective-permute-start.15 = (f32[256,512]{1,0:T(8,128)S(1)}, f32[256,512]{1,0:T(8,128)S(1)}, u32[]{:S(2)}, u32[]{:S(2)}) collective-permute-start(f32[256,512]{1,0:T(8,128)S(1)} %get-tuple-element.69), channel_id=1, source_target_pairs={{0,1},{1,0},{2,3},{3,2},{4,5},{5,4},{6,7},{7,6},{8,9},{9,8},{10,11... | collective-permute-start | bytes 1572872 | tf_op jit(solution)/shard_map/ppermute | solution.py:83
  114.3 12.6 %collective-permute-start.16 = (f32[256,512]{1,0:T(8,128)S(1)}, f32[256,512]{1,0:T(8,128)S(1)}, u32[]{:S(2)}, u32[]{:S(2)}) collective-permute-start(f32[256,512]{1,0:T(8,128)S(1)} %get-tuple-element.51), channel_id=1, source_target_pairs={{1,2},{2,1},{3,4},{4,3},{5,6},{6,5},{7,8},{8,7},{9,10},{10,9},{11,... | collective-permute-start | bytes 1572872 | tf_op jit(solution)/shard_map/ppermute | solution.py:80
  127.8 28.0 %all-to-all-start = ((f32[8,32,512]{2,1,0:T(8,128)}), f32[8,32,512]{2,1,0:T(8,128)S(1)}, u32[]{:S(2)}, u32[]{:S(2)}) async-start(f32[8,32,512]{2,1,0:T(8,128)} %bitcast.13), calls=%async_computation | async-start | bytes 1048576 | tf_op jit(solution)/shard_map/all_to_all | solution.py:139

commit v4 on v3

--- a/solution.py
+++ b/solution.py
@@ -82,17 +82,20 @@
     def beside(field):
         return lax.ppermute(field, "grid", near)
 
-    states, even, first = hold(states, even, first)
+    upper = (lax.axis_index("scen") & 1) == 1
+    states, even, first, upper = hold(states, even, first, upper)
     over = across(states[0])
     nears = beside(states)
     (later,) = hold(states)
+    fields = [states[0]]
+    for step in range(1, steps):
+        (field,) = hold(later[step])
+        fields.append(field)
+        (later,) = hold(later)
     own = lax.dynamic_slice(direction, (first, jnp.uint32(0)), (share, columns))
-    sent, own = hold(jnp.concatenate([later[1], own]), own)
-    (later,) = hold(later)
-    fields = [states[0], sent[:rows], later[2], later[3]]
-    fields[2:] = hold(*fields[2:])
+    sent, own = hold(jnp.concatenate([fields[2], own]), own)
     arrived = across(sent)
-    overs = [over, arrived[:rows]] + [across(fields[k]) for k in (2, 3)]
+    overs = [over, across(fields[1]), arrived[:rows], across(fields[3])]
     over_own = arrived[rows:]
 
     far_gain = jnp.where(even, kappa + courant, kappa)
@@ -110,13 +113,14 @@
     tangent, laps[0] = hold(tangent, laps[0])
     for step in range(1, steps):
         over = across(tangent)
-        if step == 1:
+        if step == 2:
             side = beside(jnp.concatenate([tangent, own]))
             side, side_own = side[:rows], side[rows:]
         else:
             side = beside(tangent)
         laps.append(lap_of(step))
-        base = tangent + kappa * side_sum(tangent) - courant * tangent + direction * laps[step]
+        base = tangent + kappa * side_sum(tangent) - courant * tangent
+        base = base + direction * laps[step]
         base, laps[step] = hold(base, laps[step])
         (base,) = hold(base + near_gain * side)
         tangent = base + far_gain * over
@@ -136,13 +140,22 @@
     (rest,) = hold(partial_value + laps[0] * base)
     partial_value = rest + laps[0] * over
 
-    pieces = lax.all_to_all(partial_value, "scen", 0, 0, tiled=True)
+    groups = [list(range(side, scens, 2)) for side in range(2)]
+    pieces = lax.all_to_all(
+        partial_value, "scen", 0, 0, axis_index_groups=groups, tiled=True
+    )
 
     tall = jnp.pad(direction, ((1, 1), (0, 0)))
     tall = lax.dynamic_slice(tall, (first, jnp.uint32(0)), (share + 2, columns))
     lap = over_own + side_own + side_sum(tall)[1:-1]
     (prior,) = hold(prior_gain * (own - prior_reach * lap))
-    return (jnp.sum(pieces.reshape(scens, share, columns), 0) + prior)[None]
+    pieces = pieces.reshape(scens // 2, 2, share, columns)
+    kept = jnp.where(upper, pieces[:, 1], pieces[:, 0])
+    other = jnp.where(upper, pieces[:, 0], pieces[:, 1])
+    (other,) = hold(jnp.sum(other, 0))
+    other = lax.ppermute(other, "scen", [(s, s ^ 1) for s in range(scens)])
+    (kept,) = hold(jnp.sum(kept, 0) + prior)
+    return (kept + other)[None]
 
 
 def solution(mesh):

time: 157 us -> 154 us (0.981)
  the two profiles are of different devices: /device:TPU:8 before, /device:TPU:40 now
where the time goes in v4:
time: 154 us
  starting transfers between devices  71.6 us (46%)
  waiting for transfers between devices  65.7 us (43%)
  other arithmetic  9.01 us (6%)
  Pallas kernels  4.3 us (3%)
  local copies, waits for them, and re-layouts  2.4 us (2%)
    ppermute x10, starting transfers between devices, across(): return lax.ppermute(field, 'grid', far)  51.6 us
    ppermute x10, waiting for transfers between devices, across(): return lax.ppermute(field, 'grid', far)  49.7 us
    ppermute x7, starting transfers between devices, beside(): return lax.ppermute(field, 'grid', near)  13.7 us
    all_to_all x1, waiting for transfers between devices, local(): lax.all_to_all(partial_value, 'scen', 0, 0, axis_index_groups=groups, til...  8.2 us
    ppermute x1, waiting for transfers between devices, local(): other = lax.ppermute(other, 'scen', [(s, s ^ 1) for s in range(scens)])  7.82 us
    pallas_call x1, Pallas kernels, weight_field(): pl.pallas_call(weight_kernel, grid=(count // chunk,), in_specs=[pl.BlockS...  4.3 us
    all_to_all x1, starting transfers between devices, local(): lax.all_to_all(partial_value, 'scen', 0, 0, axis_index_groups=groups, til...  4.29 us
  transfers between devices with their start and end apart: 19, of which 9 were waited for; matrix products, arithmetic and copies ran while one was open for 5% of the time, Pallas kernels for 3%

profile of v4, /device:TPU:40, one launch (start us, length us, event | category | flops | bytes accessed | tf_op | source)
XLA Modules:
  0.0 153.5 jit_solution(13049744564401240371)
XLA Ops:
  0.0 2.2 %collective-permute-start = (f32[4,256,512]{2,1,0:T(8,128)}, f32[4,256,512]{2,1,0:T(8,128)S(1)}, u32[]{:S(2)}, u32[]{:S(2)}) collective-permute-start(f32[4,256,512]{2,1,0:T(8,128)} %bitcast.77), channel_id=1, source_target_pairs={{0,1},{1,0},{2,3},{3,2},{4,5},{5,4},{6,7},{7,6},{8,9},{9,8},{10,11... | collective-permute-start | bytes 6291464 | tf_op jit(solution)/shard_map/ppermute | solution.py:83
  2.2 1.1 slice_bitcast_fusion.7
  3.3 11.8 %collective-permute-start.1 = (f32[256,512]{1,0:T(8,128)S(1)}, f32[256,512]{1,0:T(8,128)S(1)}, u32[]{:S(2)}, u32[]{:S(2)}) collective-permute-start(f32[256,512]{1,0:T(8,128)S(1)} %slice_bitcast_fusion.7), channel_id=1, source_target_pairs={{1,2},{2,1},{3,4},{4,3},{5,6},{6,5},{7,8},{8,7},{9,10},{10,9},{11,... | collective-permute-start | bytes 1572872 | tf_op jit(solution)/shard_map/ppermute | solution.py:80
  15.1 1.1 slice_bitcast_fusion.5
  16.2 1.9 %collective-permute-start.2 = (f32[256,512]{1,0:T(8,128)S(1)}, f32[256,512]{1,0:T(8,128)S(1)}, u32[]{:S(2)}, u32[]{:S(2)}) collective-permute-start(f32[256,512]{1,0:T(8,128)S(1)} %slice_bitcast_fusion.5), channel_id=1, source_target_pairs={{1,2},{2,1},{3,4},{4,3},{5,6},{6,5},{7,8},{8,7},{9,10},{10,9},{11,... | collective-permute-start | bytes 1572872 | tf_op jit(solution)/shard_map/ppermute | solution.py:80
  18.2 0.0 collective-permute-done
  18.2 0.3 fusion.4
  18.5 0.0 copy-start.3
  18.5 0.0 copy-start.4
  18.6 3.4 %collective-permute-done.1 = f32[256,512]{1,0:T(8,128)S(1)} collective-permute-done((f32[256,512]{1,0:T(8,128)S(1)}, f32[256,512]{1,0:T(8,128)S(1)}, u32[]{:S(2)}, u32[]{:S(2)}) %collective-permute-start.1) | collective-permute-done | bytes 524320 | tf_op jit(solution)/shard_map/ppermute | solution.py:80
  22.0 0.2 bitcast_multiply_fusion.9
  22.1 1.9 %collective-permute-start.3 = (f32[256,512]{1,0:T(8,128)S(1)}, f32[256,512]{1,0:T(8,128)S(1)}, u32[]{:S(2)}, u32[]{:S(2)}) collective-permute-start(f32[256,512]{1,0:T(8,128)S(1)} %get-tuple-element.29), channel_id=1, source_target_pairs={{0,1},{1,0},{2,3},{3,2},{4,5},{5,4},{6,7},{7,6},{8,9},{9,8},{10,11... | collective-permute-start | bytes 1572872 | tf_op jit(solution)/shard_map/ppermute | solution.py:83
  24.1 5.8 %collective-permute-start.5 = (f32[288,512]{1,0:T(8,128)S(1)}, f32[288,512]{1,0:T(8,128)S(1)}, u32[]{:S(2)}, u32[]{:S(2)}) collective-permute-start(f32[288,512]{1,0:T(8,128)S(1)} %pad_maximum_fusion), channel_id=1, source_target_pairs={{1,2},{2,1},{3,4},{4,3},{5,6},{6,5},{7,8},{8,7},{9,10},{10,9},{11,... | collective-permute-start | bytes 1769480 | tf_op jit(solution)/shard_map/ppermute | solution.py:80
  29.9 1.9 %collective-permute-start.4 = (f32[256,512]{1,0:T(8,128)S(1)}, f32[256,512]{1,0:T(8,128)S(1)}, u32[]{:S(2)}, u32[]{:S(2)}) collective-permute-start(f32[256,512]{1,0:T(8,128)S(1)} %get-tuple-element.29), channel_id=1, source_target_pairs={{1,2},{2,1},{3,4},{4,3},{5,6},{6,5},{7,8},{8,7},{9,10},{10,9},{11,... | collective-permute-start | bytes 1572872 | tf_op jit(solution)/shard_map/ppermute | solution.py:80
  31.8 0.0 collective-permute-done.2
  31.8 0.9 fusion.12
  32.8 0.1 multiply_add_fusion.7
  32.9 10.1 %collective-permute-done.4 = f32[256,512]{1,0:T(8,128)S(1)} collective-permute-done((f32[256,512]{1,0:T(8,128)S(1)}, f32[256,512]{1,0:T(8,128)S(1)}, u32[]{:S(2)}, u32[]{:S(2)}) %collective-permute-start.4) | collective-permute-done | bytes 524320 | tf_op jit(solution)/shard_map/ppermute | solution.py:80
  43.1 0.1 multiply_add_fusion.6
  43.3 1.9 %collective-permute-start.6 = (f32[288,512]{1,0:T(8,128)S(1)}, f32[288,512]{1,0:T(8,128)S(1)}, u32[]{:S(2)}, u32[]{:S(2)}) collective-permute-start(f32[288,512]{1,0:T(8,128)S(1)} %pad_maximum_fusion.1), channel_id=1, source_target_pairs={{0,1},{1,0},{2,3},{3,2},{4,5},{5,4},{6,7},{7,6},{8,9},{9,8},{10,11... | collective-permute-start | bytes 1769480 | tf_op jit(solution)/shard_map/ppermute | solution.py:83
  45.2 5.8 %collective-permute-start.8 = (f32[256,512]{1,0:T(8,128)S(1)}, f32[256,512]{1,0:T(8,128)S(1)}, u32[]{:S(2)}, u32[]{:S(2)}) collective-permute-start(f32[256,512]{1,0:T(8,128)S(1)} %slice_bitcast_fusion.1), channel_id=1, source_target_pairs={{1,2},{2,1},{3,4},{4,3},{5,6},{6,5},{7,8},{8,7},{9,10},{10,9},{11,... | collective-permute-start | bytes 1572872 | tf_op jit(solution)/shard_map/ppermute | solution.py:80
  51.0 1.9 %collective-permute-start.7 = (f32[256,512]{1,0:T(8,128)S(1)}, f32[256,512]{1,0:T(8,128)S(1)}, u32[]{:S(2)}, u32[]{:S(2)}) collective-permute-start(f32[256,512]{1,0:T(8,128)S(1)} %multiply_add_fusion.6), channel_id=1, source_target_pairs={{1,2},{2,1},{3,4},{4,3},{5,6},{6,5},{7,8},{8,7},{9,10},{10,9},{11,... | collective-permute-start | bytes 1572872 | tf_op jit(solution)/shard_map/ppermute | solution.py:80
  52.9 0.8 fusion.26
  53.7 0.0 copy-start
  53.8 0.0 copy-start.1
  53.8 0.2 fusion.66
  53.9 9.7 %collective-permute-done.7 = f32[256,512]{1,0:T(8,128)S(1)} collective-permute-done((f32[256,512]{1,0:T(8,128)S(1)}, f32[256,512]{1,0:T(8,128)S(1)}, u32[]{:S(2)}, u32[]{:S(2)}) %collective-permute-start.7) | collective-permute-done | bytes 524320 | tf_op jit(solution)/shard_map/ppermute | solution.py:80
  63.6 0.2 multiply_add_fusion.5
  63.8 1.9 %collective-permute-start.9 = (f32[256,512]{1,0:T(8,128)S(1)}, f32[256,512]{1,0:T(8,128)S(1)}, u32[]{:S(2)}, u32[]{:S(2)}) collective-permute-start(f32[256,512]{1,0:T(8,128)S(1)} %multiply_add_fusion.5), channel_id=1, source_target_pairs={{0,1},{1,0},{2,3},{3,2},{4,5},{5,4},{6,7},{7,6},{8,9},{9,8},{10,11... | collective-permute-start | bytes 1572872 | tf_op jit(solution)/shard_map/ppermute | solution.py:83
  65.7 4.3 %weight_field.1 = f32[256,512]{1,0:T(8,128)S(1)} custom-call(s32[1,4096]{1,0:T(1,128)S(1)} %copy-done, f32[1,4096]{1,0:T(1,128)S(1)} %copy-done.1), custom_call_target="tpu_custom_call" | custom-call | flops 3221225472 | bytes 524288 | tf_op jit(solution)/shard_map/weight_field/pallas_call | solution.py:41
  70.0 5.6 %collective-permute-start.10 = (f32[256,512]{1,0:T(8,128)S(1)}, f32[256,512]{1,0:T(8,128)S(1)}, u32[]{:S(2)}, u32[]{:S(2)}) collective-permute-start(f32[256,512]{1,0:T(8,128)S(1)} %multiply_add_fusion.5), channel_id=1, source_target_pairs={{1,2},{2,1},{3,4},{4,3},{5,6},{6,5},{7,8},{8,7},{9,10},{10,9},{11,... | collective-permute-start | bytes 1572872 | tf_op jit(solution)/shard_map/ppermute | solution.py:80
  75.7 0.8 fusion.40
  76.5 0.2 multiply_add_fusion.4
  76.7 6.0 %collective-permute-done.10 = f32[256,512]{1,0:T(8,128)S(1)} collective-permute-done((f32[256,512]{1,0:T(8,128)S(1)}, f32[256,512]{1,0:T(8,128)S(1)}, u32[]{:S(2)}, u32[]{:S(2)}) %collective-permute-start.10) | collective-permute-done | bytes 524320 | tf_op jit(solution)/shard_map/ppermute | solution.py:80
  82.6 0.2 fusion.77
  82.9 0.1 bitcast_multiply_fusion.7
  83.0 0.4 fusion.83
  83.4 1.9 %collective-permute-start.11 = (f32[256,512]{1,0:T(8,128)S(1)}, f32[256,512]{1,0:T(8,128)S(1)}, u32[]{:S(2)}, u32[]{:S(2)}) collective-permute-start(f32[256,512]{1,0:T(8,128)S(1)} %get-tuple-element.73), channel_id=1, source_target_pairs={{0,1},{1,0},{2,3},{3,2},{4,5},{5,4},{6,7},{7,6},{8,9},{9,8},{10,11... | collective-permute-start | bytes 1572872 | tf_op jit(solution)/shard_map/ppermute | solution.py:83
  85.3 5.6 %collective-permute-start.12 = (f32[256,512]{1,0:T(8,128)S(1)}, f32[256,512]{1,0:T(8,128)S(1)}, u32[]{:S(2)}, u32[]{:S(2)}) collective-permute-start(f32[256,512]{1,0:T(8,128)S(1)} %get-tuple-element.55), channel_id=1, source_target_pairs={{1,2},{2,1},{3,4},{4,3},{5,6},{6,5},{7,8},{8,7},{9,10},{10,9},{11,... | collective-permute-start | bytes 1572872 | tf_op jit(solution)/shard_map/ppermute | solution.py:80
  90.9 0.1 add.281
  91.0 6.9 %collective-permute-done.12 = f32[256,512]{1,0:T(8,128)S(1)} collective-permute-done((f32[256,512]{1,0:T(8,128)S(1)}, f32[256,512]{1,0:T(8,128)S(1)}, u32[]{:S(2)}, u32[]{:S(2)}) %collective-permute-start.12) | collective-permute-done | bytes 524320 | tf_op jit(solution)/shard_map/ppermute | solution.py:80
  97.9 0.1 fusion.76
  98.1 0.1 bitcast_multiply_fusion.6
  98.2 0.5 fusion.82
  98.7 1.9 %collective-permute-start.13 = (f32[256,512]{1,0:T(8,128)S(1)}, f32[256,512]{1,0:T(8,128)S(1)}, u32[]{:S(2)}, u32[]{:S(2)}) collective-permute-start(f32[256,512]{1,0:T(8,128)S(1)} %get-tuple-element.70), channel_id=1, source_target_pairs={{0,1},{1,0},{2,3},{3,2},{4,5},{5,4},{6,7},{7,6},{8,9},{9,8},{10,11... | collective-permute-start | bytes 1572872 | tf_op jit(solution)/shard_map/ppermute | solution.py:83
  100.6 5.6 %collective-permute-start.14 = (f32[256,512]{1,0:T(8,128)S(1)}, f32[256,512]{1,0:T(8,128)S(1)}, u32[]{:S(2)}, u32[]{:S(2)}) collective-permute-start(f32[256,512]{1,0:T(8,128)S(1)} %get-tuple-element.53), channel_id=1, source_target_pairs={{1,2},{2,1},{3,4},{4,3},{5,6},{6,5},{7,8},{8,7},{9,10},{10,9},{11,... | collective-permute-start | bytes 1572872 | tf_op jit(solution)/shard_map/ppermute | solution.py:80
  106.2 0.1 add.288
  106.3 6.9 %collective-permute-done.14 = f32[256,512]{1,0:T(8,128)S(1)} collective-permute-done((f32[256,512]{1,0:T(8,128)S(1)}, f32[256,512]{1,0:T(8,128)S(1)}, u32[]{:S(2)}, u32[]{:S(2)}) %collective-permute-start.14) | collective-permute-done | bytes 524320 | tf_op jit(solution)/shard_map/ppermute | solution.py:80
  113.2 0.1 fusion.75
  113.4 0.1 bitcast_multiply_fusion.8
  113.4 0.5 fusion.81
  113.9 1.9 %collective-permute-start.15 = (f32[256,512]{1,0:T(8,128)S(1)}, f32[256,512]{1,0:T(8,128)S(1)}, u32[]{:S(2)}, u32[]{:S(2)}) collective-permute-start(f32[256,512]{1,0:T(8,128)S(1)} %get-tuple-element.67), channel_id=1, source_target_pairs={{0,1},{1,0},{2,3},{3,2},{4,5},{5,4},{6,7},{7,6},{8,9},{9,8},{10,11... | collective-permute-start | bytes 1572872 | tf_op jit(solution)/shard_map/ppermute | solution.py:83
  115.9 5.6 %collective-permute-start.16 = (f32[256,512]{1,0:T(8,128)S(1)}, f32[256,512]{1,0:T(8,128)S(1)}, u32[]{:S(2)}, u32[]{:S(2)}) collective-permute-start(f32[256,512]{1,0:T(8,128)S(1)} %get-tuple-element.51), channel_id=1, source_target_pairs={{1,2},{2,1},{3,4},{4,3},{5,6},{6,5},{7,8},{8,7},{9,10},{10,9},{11,... | collective-permute-start | bytes 1572872 | tf_op jit(solution)/shard_map/ppermute | solution.py:80
  121.5 0.1 add.295
  121.6 0.1 multiply_add_fusion.1
  121.8 6.7 %collective-permute-done.16 = f32[256,512]{1,0:T(8,128)S(1)} collective-permute-done((f32[256,512]{1,0:T(8,128)S(1)}, f32[256,512]{1,0:T(8,128)S(1)}, u32[]{:S(2)}, u32[]{:S(2)}) %collective-permute-start.16) | collective-permute-done | bytes 524320 | tf_op jit(solution)/shard_map/ppermute | solution.py:80
  128.5 0.9 multiply_add_fusion
  129.4 4.3 %all-to-all-start = ((f32[4,64,512]{2,1,0:T(8,128)}), f32[4,64,512]{2,1,0:T(8,128)S(1)}, u32[]{:S(2)}, u32[]{:S(2)}) async-start(f32[4,64,512]{2,1,0:T(8,128)} %bitcast.13), calls=%async_computation | async-start | bytes 1048576 | tf_op jit(solution)/shard_map/all_to_all | solution.py:144
  133.7 0.1 pad_slice_fusion.43
  133.8 8.2 %all-to-all-done = f32[4,64,512]{2,1,0:T(8,128)S(1)} async-done(((f32[4,64,512]{2,1,0:T(8,128)}), f32[4,64,512]{2,1,0:T(8,128)S(1)}, u32[]{:S(2)}, u32[]{:S(2)}) %all-to-all-start) | async-done | bytes 524320 | tf_op jit(solution)/shard_map/all_to_all | solution.py:144
  142.1 2.0 %collective-permute-start.17 = (f32[32,512]{1,0:T(8,128)S(1)}, f32[32,512]{1,0:T(8,128)S(1)}, u32[]{:S(2)}, u32[]{:S(2)}) collective-permute-start(f32[32,512]{1,0:T(8,128)S(1)} %get-tuple-element.49), channel_id=1, source_target_pairs={{0,64},{64,0},{128,192},{192,128},{256,320},{320,256},{384,448},{4... | collective-permute-start | bytes 196616 | tf_op jit(solution)/shard_map/ppermute | solution.py:156
  144.1 0.9 fusion.74
  145.0 7.8 %collective-permute-done.17 = f32[32,512]{1,0:T(8,128)S(1)} collective-permute-done((f32[32,512]{1,0:T(8,128)S(1)}, f32[32,512]{1,0:T(8,128)S(1)}, u32[]{:S(2)}, u32[]{:S(2)}) %collective-permute-start.17) | collective-permute-done | bytes 65568 | tf_op jit(solution)/shard_map/ppermute | solution.py:156
  152.9 0.6 add_bitcast_fusion
  (26 shorter events, 0.3 us)
Async XLA Ops:
  0.0 18.1 %copy-start.5 = (f32[1,4,1,256,512]{4,3,2,1,0:T(8,128)S(1)}, f32[1,4,1,256,512]{4,3,2,1,0:T(8,128)}, u32[]{:S(2)}) copy-start(f32[1,4,1,256,512]{4,3,2,1,0:T(8,128)} %param.6) | copy-start | bytes 6291460
  0.0 22.0 %copy-start.2 = (f32[1,256,512]{2,1,0:T(8,128)S(1)}, f32[1,256,512]{2,1,0:T(8,128)}, u32[]{:S(2)}) copy-start(f32[1,256,512]{2,1,0:T(8,128)} %param.9) | copy-start | bytes 1572868
  0.0 18.2 %collective-permute-start = (f32[4,256,512]{2,1,0:T(8,128)}, f32[4,256,512]{2,1,0:T(8,128)S(1)}, u32[]{:S(2)}, u32[]{:S(2)}) collective-permute-start(f32[4,256,512]{2,1,0:T(8,128)} %bitcast.77), channel_id=1, source_target_pairs={{0,1},{1,0},{2,3},{3,2},{4,5},{5,4},{6,7},{7,6},{8,9},{9,8},{10,11... | collective-permute-start | bytes 6291464 | tf_op jit(solution)/shard_map/ppermute | solution.py:83
  3.3 18.7 %collective-permute-start.1 = (f32[256,512]{1,0:T(8,128)S(1)}, f32[256,512]{1,0:T(8,128)S(1)}, u32[]{:S(2)}, u32[]{:S(2)}) collective-permute-start(f32[256,512]{1,0:T(8,128)S(1)} %slice_bitcast_fusion.7), channel_id=1, source_target_pairs={{1,2},{2,1},{3,4},{4,3},{5,6},{6,5},{7,8},{8,7},{9,10},{10,9},{11,... | collective-permute-start | bytes 1572872 | tf_op jit(solution)/shard_map/ppermute | solution.py:80
  16.2 15.6 %collective-permute-start.2 = (f32[256,512]{1,0:T(8,128)S(1)}, f32[256,512]{1,0:T(8,128)S(1)}, u32[]{:S(2)}, u32[]{:S(2)}) collective-permute-start(f32[256,512]{1,0:T(8,128)S(1)} %slice_bitcast_fusion.5), channel_id=1, source_target_pairs={{1,2},{2,1},{3,4},{4,3},{5,6},{6,5},{7,8},{8,7},{9,10},{10,9},{11,... | collective-permute-start | bytes 1572872 | tf_op jit(solution)/shard_map/ppermute | solution.py:80
  18.5 13.3 %copy-start.3 = (f32[1,256,512]{2,1,0:T(8,128)S(1)}, f32[1,256,512]{2,1,0:T(8,128)}, u32[]{:S(2)}) copy-start(f32[1,256,512]{2,1,0:T(8,128)} %param.7) | copy-start | bytes 1572868
  18.5 13.3 %copy-start.4 = (f32[1,256,512]{2,1,0:T(8,128)S(1)}, f32[1,256,512]{2,1,0:T(8,128)}, u32[]{:S(2)}) copy-start(f32[1,256,512]{2,1,0:T(8,128)} %param.8) | copy-start | bytes 1572868
  22.1 10.7 %collective-permute-start.3 = (f32[256,512]{1,0:T(8,128)S(1)}, f32[256,512]{1,0:T(8,128)S(1)}, u32[]{:S(2)}, u32[]{:S(2)}) collective-permute-start(f32[256,512]{1,0:T(8,128)S(1)} %get-tuple-element.29), channel_id=1, source_target_pairs={{0,1},{1,0},{2,3},{3,2},{4,5},{5,4},{6,7},{7,6},{8,9},{9,8},{10,11... | collective-permute-start | bytes 1572872 | tf_op jit(solution)/shard_map/ppermute | solution.py:83
  24.1 28.8 %collective-permute-start.5 = (f32[288,512]{1,0:T(8,128)S(1)}, f32[288,512]{1,0:T(8,128)S(1)}, u32[]{:S(2)}, u32[]{:S(2)}) collective-permute-start(f32[288,512]{1,0:T(8,128)S(1)} %pad_maximum_fusion), channel_id=1, source_target_pairs={{1,2},{2,1},{3,4},{4,3},{5,6},{6,5},{7,8},{8,7},{9,10},{10,9},{11,... | collective-permute-start | bytes 1769480 | tf_op jit(solution)/shard_map/ppermute | solution.py:80
  29.9 13.2 %collective-permute-start.4 = (f32[256,512]{1,0:T(8,128)S(1)}, f32[256,512]{1,0:T(8,128)S(1)}, u32[]{:S(2)}, u32[]{:S(2)}) collective-permute-start(f32[256,512]{1,0:T(8,128)S(1)} %get-tuple-element.29), channel_id=1, source_target_pairs={{1,2},{2,1},{3,4},{4,3},{5,6},{6,5},{7,8},{8,7},{9,10},{10,9},{11,... | collective-permute-start | bytes 1572872 | tf_op jit(solution)/shard_map/ppermute | solution.py:80
  43.3 10.5 %collective-permute-start.6 = (f32[288,512]{1,0:T(8,128)S(1)}, f32[288,512]{1,0:T(8,128)S(1)}, u32[]{:S(2)}, u32[]{:S(2)}) collective-permute-start(f32[288,512]{1,0:T(8,128)S(1)} %pad_maximum_fusion.1), channel_id=1, source_target_pairs={{0,1},{1,0},{2,3},{3,2},{4,5},{5,4},{6,7},{7,6},{8,9},{9,8},{10,11... | collective-permute-start | bytes 1769480 | tf_op jit(solution)/shard_map/ppermute | solution.py:83
  45.2 30.4 %collective-permute-start.8 = (f32[256,512]{1,0:T(8,128)S(1)}, f32[256,512]{1,0:T(8,128)S(1)}, u32[]{:S(2)}, u32[]{:S(2)}) collective-permute-start(f32[256,512]{1,0:T(8,128)S(1)} %slice_bitcast_fusion.1), channel_id=1, source_target_pairs={{1,2},{2,1},{3,4},{4,3},{5,6},{6,5},{7,8},{8,7},{9,10},{10,9},{11,... | collective-permute-start | bytes 1572872 | tf_op jit(solution)/shard_map/ppermute | solution.py:80
  51.0 12.6 %collective-permute-start.7 = (f32[256,512]{1,0:T(8,128)S(1)}, f32[256,512]{1,0:T(8,128)S(1)}, u32[]{:S(2)}, u32[]{:S(2)}) collective-permute-start(f32[256,512]{1,0:T(8,128)S(1)} %multiply_add_fusion.6), channel_id=1, source_target_pairs={{1,2},{2,1},{3,4},{4,3},{5,6},{6,5},{7,8},{8,7},{9,10},{10,9},{11,... | collective-permute-start | bytes 1572872 | tf_op jit(solution)/shard_map/ppermute | solution.py:80
  53.7 10.0 %copy-start.6 = (f32[288,512]{1,0:T(8,128)}, f32[288,512]{1,0:T(8,128)S(1)}, u32[]{:S(2)}) copy-start(f32[288,512]{1,0:T(8,128)S(1)} %collective-permute-done.6) | copy-start | bytes 1769476
  53.7 12.0 %copy-start = (s32[1,4096]{1,0:T(1,128)S(1)}, s32[1,4096]{1,0:T(1,128)}, u32[]{:S(2)}) copy-start(s32[1,4096]{1,0:T(1,128)} %index_ref.1) | copy-start | bytes 49156
  53.8 12.0 %copy-start.1 = (f32[1,4096]{1,0:T(1,128)S(1)}, f32[1,4096]{1,0:T(1,128)}, u32[]{:S(2)}) copy-start(f32[1,4096]{1,0:T(1,128)} %weight_ref.1) | copy-start | bytes 49156
  63.8 12.7 %collective-permute-start.9 = (f32[256,512]{1,0:T(8,128)S(1)}, f32[256,512]{1,0:T(8,128)S(1)}, u32[]{:S(2)}, u32[]{:S(2)}) collective-permute-start(f32[256,512]{1,0:T(8,128)S(1)} %multiply_add_fusion.5), channel_id=1, source_target_pairs={{0,1},{1,0},{2,3},{3,2},{4,5},{5,4},{6,7},{7,6},{8,9},{9,8},{10,11... | collective-permute-start | bytes 1572872 | tf_op jit(solution)/shard_map/ppermute | solution.py:83
  70.0 12.6 %collective-permute-start.10 = (f32[256,512]{1,0:T(8,128)S(1)}, f32[256,512]{1,0:T(8,128)S(1)}, u32[]{:S(2)}, u32[]{:S(2)}) collective-permute-start(f32[256,512]{1,0:T(8,128)S(1)} %multiply_add_fusion.5), channel_id=1, source_target_pairs={{1,2},{2,1},{3,4},{4,3},{5,6},{6,5},{7,8},{8,7},{9,10},{10,9},{11,... | collective-permute-start | bytes 1572872 | tf_op jit(solution)/shard_map/ppermute | solution.py:80
  83.4 7.6 %collective-permute-start.11 = (f32[256,512]{1,0:T(8,128)S(1)}, f32[256,512]{1,0:T(8,128)S(1)}, u32[]{:S(2)}, u32[]{:S(2)}) collective-permute-start(f32[256,512]{1,0:T(8,128)S(1)} %get-tuple-element.73), channel_id=1, source_target_pairs={{0,1},{1,0},{2,3},{3,2},{4,5},{5,4},{6,7},{7,6},{8,9},{9,8},{10,11... | collective-permute-start | bytes 1572872 | tf_op jit(solution)/shard_map/ppermute | solution.py:83
  85.3 12.6 %collective-permute-start.12 = (f32[256,512]{1,0:T(8,128)S(1)}, f32[256,512]{1,0:T(8,128)S(1)}, u32[]{:S(2)}, u32[]{:S(2)}) collective-permute-start(f32[256,512]{1,0:T(8,128)S(1)} %get-tuple-element.55), channel_id=1, source_target_pairs={{1,2},{2,1},{3,4},{4,3},{5,6},{6,5},{7,8},{8,7},{9,10},{10,9},{11,... | collective-permute-start | bytes 1572872 | tf_op jit(solution)/shard_map/ppermute | solution.py:80
  98.7 7.6 %collective-permute-start.13 = (f32[256,512]{1,0:T(8,128)S(1)}, f32[256,512]{1,0:T(8,128)S(1)}, u32[]{:S(2)}, u32[]{:S(2)}) collective-permute-start(f32[256,512]{1,0:T(8,128)S(1)} %get-tuple-element.70), channel_id=1, source_target_pairs={{0,1},{1,0},{2,3},{3,2},{4,5},{5,4},{6,7},{7,6},{8,9},{9,8},{10,11... | collective-permute-start | bytes 1572872 | tf_op jit(solution)/shard_map/ppermute | solution.py:83
  100.6 12.6 %collective-permute-start.14 = (f32[256,512]{1,0:T(8,128)S(1)}, f32[256,512]{1,0:T(8,128)S(1)}, u32[]{:S(2)}, u32[]{:S(2)}) collective-permute-start(f32[256,512]{1,0:T(8,128)S(1)} %get-tuple-element.53), channel_id=1, source_target_pairs={{1,2},{2,1},{3,4},{4,3},{5,6},{6,5},{7,8},{8,7},{9,10},{10,9},{11,... | collective-permute-start | bytes 1572872 | tf_op jit(solution)/shard_map/ppermute | solution.py:80
  113.9 7.6 %collective-permute-start.15 = (f32[256,512]{1,0:T(8,128)S(1)}, f32[256,512]{1,0:T(8,128)S(1)}, u32[]{:S(2)}, u32[]{:S(2)}) collective-permute-start(f32[256,512]{1,0:T(8,128)S(1)} %get-tuple-element.67), channel_id=1, source_target_pairs={{0,1},{1,0},{2,3},{3,2},{4,5},{5,4},{6,7},{7,6},{8,9},{9,8},{10,11... | collective-permute-start | bytes 1572872 | tf_op jit(solution)/shard_map/ppermute | solution.py:83
  115.9 12.6 %collective-permute-start.16 = (f32[256,512]{1,0:T(8,128)S(1)}, f32[256,512]{1,0:T(8,128)S(1)}, u32[]{:S(2)}, u32[]{:S(2)}) collective-permute-start(f32[256,512]{1,0:T(8,128)S(1)} %get-tuple-element.51), channel_id=1, source_target_pairs={{1,2},{2,1},{3,4},{4,3},{5,6},{6,5},{7,8},{8,7},{9,10},{10,9},{11,... | collective-permute-start | bytes 1572872 | tf_op jit(solution)/shard_map/ppermute | solution.py:80
  129.4 12.6 %all-to-all-start = ((f32[4,64,512]{2,1,0:T(8,128)}), f32[4,64,512]{2,1,0:T(8,128)S(1)}, u32[]{:S(2)}, u32[]{:S(2)}) async-start(f32[4,64,512]{2,1,0:T(8,128)} %bitcast.13), calls=%async_computation | async-start | bytes 1048576 | tf_op jit(solution)/shard_map/all_to_all | solution.py:144
  142.1 10.8 %collective-permute-start.17 = (f32[32,512]{1,0:T(8,128)S(1)}, f32[32,512]{1,0:T(8,128)S(1)}, u32[]{:S(2)}, u32[]{:S(2)}) collective-permute-start(f32[32,512]{1,0:T(8,128)S(1)} %get-tuple-element.49), channel_id=1, source_target_pairs={{0,64},{64,0},{128,192},{192,128},{256,320},{320,256},{384,448},{4... | collective-permute-start | bytes 196616 | tf_op jit(solution)/shard_map/ppermute | solution.py:156

commit v5 on v4

--- a/solution.py
+++ b/solution.py
@@ -126,30 +126,41 @@
         tangent = base + far_gain * over
 
     adjoint = tangent * weights
+    lap_over = across(laps[0])
     partial_value = None
     for step in range(steps - 2, -1, -1):
-        over = across(far_gain * adjoint)
+        sent = far_gain * adjoint
+        if step:
+            over = across(sent)
         side = beside(near_gain * adjoint)
         term = laps[step + 1] * adjoint
         partial_value = term if partial_value is None else partial_value + term
         base = adjoint + side_sum(kappa * adjoint) - courant * adjoint
         base, partial_value = hold(base, partial_value)
-        (base,) = hold(base + side)
         if step:
+            (base,) = hold(base + side)
             adjoint = base + over
-    (rest,) = hold(partial_value + laps[0] * base)
-    partial_value = rest + laps[0] * over
+    product, rest = hold(lap_over * sent, partial_value + laps[0] * base)
+    value = rest + laps[0] * side
+    value = jnp.concatenate(
+        [jnp.where(even, product, value), jnp.where(even, value, product)]
+    )
 
-    groups = [list(range(side, scens, 2)) for side in range(2)]
+    pairs = [(g, (g + 1) % slabs) for g in range(1, slabs, 2)]
+    groups = [
+        [(2 * x + side) * slabs + g for g in pair for x in range(scens // 2)]
+        for pair in pairs
+        for side in range(2)
+    ]
     pieces = lax.all_to_all(
-        partial_value, "scen", 0, 0, axis_index_groups=groups, tiled=True
+        value, ("scen", "grid"), 0, 0, axis_index_groups=groups, tiled=True
     )
 
     tall = jnp.pad(direction, ((1, 1), (0, 0)))
     tall = lax.dynamic_slice(tall, (first, jnp.uint32(0)), (share + 2, columns))
     lap = over_own + side_own + side_sum(tall)[1:-1]
     (prior,) = hold(prior_gain * (own - prior_reach * lap))
-    pieces = pieces.reshape(scens // 2, 2, share, columns)
+    pieces = pieces.reshape(scens, 2, share, columns)
     kept = jnp.where(upper, pieces[:, 1], pieces[:, 0])
     other = jnp.where(upper, pieces[:, 0], pieces[:, 1])
     (other,) = hold(jnp.sum(other, 0))

time: 154 us -> 151 us (0.981)
  waiting for transfers between devices: 65.7 us -> 62.6 us
    ppermute x10, waiting for transfers between devices: 49.7 us -> 44.3 us  [across(): return lax.ppermute(field, 'grid', far)]
    ppermute x10, starting transfers between devices: 51.6 us -> 48 us  [across(): return lax.ppermute(field, 'grid', far)]
    all_to_all x1, starting transfers between devices: 4.29 us -> 7.71 us  [local(): lax.all_to_all(value, ('scen', 'grid'), 0, 0, axis_index_groups=groups, t...]
    all_to_all x1, waiting for transfers between devices: 8.2 us -> 10.5 us  [local(): lax.all_to_all(value, ('scen', 'grid'), 0, 0, axis_index_groups=groups, t...]
  transfers between devices with their start and end apart: 19 -> 19, of which waited for: 9 -> 9; matrix products, arithmetic and copies ran while one was open for 5% -> 6% of each run, Pallas kernels for 3% -> 3%
where the time goes in v5:
time: 151 us
  starting transfers between devices  71.4 us (47%)
  waiting for transfers between devices  62.6 us (41%)
  other arithmetic  9.43 us (6%)
  Pallas kernels  4.3 us (3%)
  local copies, waits for them, and re-layouts  2.4 us (2%)
    ppermute x10, starting transfers between devices, across(): return lax.ppermute(field, 'grid', far)  48 us
    ppermute x10, waiting for transfers between devices, across(): return lax.ppermute(field, 'grid', far)  44.3 us
    ppermute x7, starting transfers between devices, beside(): return lax.ppermute(field, 'grid', near)  13.7 us
    all_to_all x1, waiting for transfers between devices, local(): lax.all_to_all(value, ('scen', 'grid'), 0, 0, axis_index_groups=groups, t...  10.5 us
    ppermute x1, waiting for transfers between devices, local(): other = lax.ppermute(other, 'scen', [(s, s ^ 1) for s in range(scens)])  7.82 us
    all_to_all x1, starting transfers between devices, local(): lax.all_to_all(value, ('scen', 'grid'), 0, 0, axis_index_groups=groups, t...  7.71 us
    pallas_call x1, Pallas kernels, weight_field(): pl.pallas_call(weight_kernel, grid=(count // chunk,), in_specs=[pl.BlockS...  4.3 us
  transfers between devices with their start and end apart: 19, of which 9 were waited for; matrix products, arithmetic and copies ran while one was open for 6% of the time, Pallas kernels for 3%

profile of v5, /device:TPU:40, one launch (start us, length us, event | category | flops | bytes accessed | tf_op | source)
XLA Modules:
  0.0 150.7 jit_solution(3083850644867482753)
XLA Ops:
  0.0 2.2 %collective-permute-start = (f32[4,256,512]{2,1,0:T(8,128)}, f32[4,256,512]{2,1,0:T(8,128)S(1)}, u32[]{:S(2)}, u32[]{:S(2)}) collective-permute-start(f32[4,256,512]{2,1,0:T(8,128)} %bitcast.78), channel_id=1, source_target_pairs={{0,1},{1,0},{2,3},{3,2},{4,5},{5,4},{6,7},{7,6},{8,9},{9,8},{10,11... | collective-permute-start | bytes 6291464 | tf_op jit(solution)/shard_map/ppermute | solution.py:83
  2.2 1.1 slice_bitcast_fusion.7
  3.3 11.8 %collective-permute-start.1 = (f32[256,512]{1,0:T(8,128)S(1)}, f32[256,512]{1,0:T(8,128)S(1)}, u32[]{:S(2)}, u32[]{:S(2)}) collective-permute-start(f32[256,512]{1,0:T(8,128)S(1)} %slice_bitcast_fusion.7), channel_id=1, source_target_pairs={{1,2},{2,1},{3,4},{4,3},{5,6},{6,5},{7,8},{8,7},{9,10},{10,9},{11,... | collective-permute-start | bytes 1572872 | tf_op jit(solution)/shard_map/ppermute | solution.py:80
  15.1 1.1 slice_bitcast_fusion.5
  16.2 1.9 %collective-permute-start.3 = (f32[256,512]{1,0:T(8,128)S(1)}, f32[256,512]{1,0:T(8,128)S(1)}, u32[]{:S(2)}, u32[]{:S(2)}) collective-permute-start(f32[256,512]{1,0:T(8,128)S(1)} %slice_bitcast_fusion.5), channel_id=1, source_target_pairs={{1,2},{2,1},{3,4},{4,3},{5,6},{6,5},{7,8},{8,7},{9,10},{10,9},{11,... | collective-permute-start | bytes 1572872 | tf_op jit(solution)/shard_map/ppermute | solution.py:80
  18.2 0.0 collective-permute-done
  18.2 0.3 fusion.4
  18.5 0.0 copy-start.3
  18.5 0.0 copy-start.4
  18.6 3.4 %collective-permute-done.1 = f32[256,512]{1,0:T(8,128)S(1)} collective-permute-done((f32[256,512]{1,0:T(8,128)S(1)}, f32[256,512]{1,0:T(8,128)S(1)}, u32[]{:S(2)}, u32[]{:S(2)}) %collective-permute-start.1) | collective-permute-done | bytes 524320 | tf_op jit(solution)/shard_map/ppermute | solution.py:80
  22.0 0.2 bitcast_multiply_fusion.9
  22.1 1.9 %collective-permute-start.4 = (f32[256,512]{1,0:T(8,128)S(1)}, f32[256,512]{1,0:T(8,128)S(1)}, u32[]{:S(2)}, u32[]{:S(2)}) collective-permute-start(f32[256,512]{1,0:T(8,128)S(1)} %get-tuple-element.34), channel_id=1, source_target_pairs={{0,1},{1,0},{2,3},{3,2},{4,5},{5,4},{6,7},{7,6},{8,9},{9,8},{10,11... | collective-permute-start | bytes 1572872 | tf_op jit(solution)/shard_map/ppermute | solution.py:83
  24.1 5.8 %collective-permute-start.6 = (f32[288,512]{1,0:T(8,128)S(1)}, f32[288,512]{1,0:T(8,128)S(1)}, u32[]{:S(2)}, u32[]{:S(2)}) collective-permute-start(f32[288,512]{1,0:T(8,128)S(1)} %pad_maximum_fusion.1), channel_id=1, source_target_pairs={{1,2},{2,1},{3,4},{4,3},{5,6},{6,5},{7,8},{8,7},{9,10},{10,9},{11,... | collective-permute-start | bytes 1769480 | tf_op jit(solution)/shard_map/ppermute | solution.py:80
  29.9 1.9 %collective-permute-start.5 = (f32[256,512]{1,0:T(8,128)S(1)}, f32[256,512]{1,0:T(8,128)S(1)}, u32[]{:S(2)}, u32[]{:S(2)}) collective-permute-start(f32[256,512]{1,0:T(8,128)S(1)} %get-tuple-element.34), channel_id=1, source_target_pairs={{1,2},{2,1},{3,4},{4,3},{5,6},{6,5},{7,8},{8,7},{9,10},{10,9},{11,... | collective-permute-start | bytes 1572872 | tf_op jit(solution)/shard_map/ppermute | solution.py:80
  31.8 0.9 fusion.12
  32.8 0.1 multiply_add_fusion.7
  32.9 10.1 %collective-permute-done.5 = f32[256,512]{1,0:T(8,128)S(1)} collective-permute-done((f32[256,512]{1,0:T(8,128)S(1)}, f32[256,512]{1,0:T(8,128)S(1)}, u32[]{:S(2)}, u32[]{:S(2)}) %collective-permute-start.5) | collective-permute-done | bytes 524320 | tf_op jit(solution)/shard_map/ppermute | solution.py:80
  43.1 0.1 multiply_add_fusion.6
  43.3 1.9 %collective-permute-start.7 = (f32[288,512]{1,0:T(8,128)S(1)}, f32[288,512]{1,0:T(8,128)S(1)}, u32[]{:S(2)}, u32[]{:S(2)}) collective-permute-start(f32[288,512]{1,0:T(8,128)S(1)} %pad_maximum_fusion.2), channel_id=1, source_target_pairs={{0,1},{1,0},{2,3},{3,2},{4,5},{5,4},{6,7},{7,6},{8,9},{9,8},{10,11... | collective-permute-start | bytes 1769480 | tf_op jit(solution)/shard_map/ppermute | solution.py:83
  45.2 5.8 %collective-permute-start.9 = (f32[256,512]{1,0:T(8,128)S(1)}, f32[256,512]{1,0:T(8,128)S(1)}, u32[]{:S(2)}, u32[]{:S(2)}) collective-permute-start(f32[256,512]{1,0:T(8,128)S(1)} %slice_bitcast_fusion.1), channel_id=1, source_target_pairs={{1,2},{2,1},{3,4},{4,3},{5,6},{6,5},{7,8},{8,7},{9,10},{10,9},{11,... | collective-permute-start | bytes 1572872 | tf_op jit(solution)/shard_map/ppermute | solution.py:80
  51.0 1.9 %collective-permute-start.8 = (f32[256,512]{1,0:T(8,128)S(1)}, f32[256,512]{1,0:T(8,128)S(1)}, u32[]{:S(2)}, u32[]{:S(2)}) collective-permute-start(f32[256,512]{1,0:T(8,128)S(1)} %multiply_add_fusion.6), channel_id=1, source_target_pairs={{1,2},{2,1},{3,4},{4,3},{5,6},{6,5},{7,8},{8,7},{9,10},{10,9},{11,... | collective-permute-start | bytes 1572872 | tf_op jit(solution)/shard_map/ppermute | solution.py:80
  52.9 0.8 fusion.26
  53.7 0.0 copy-start
  53.8 0.0 copy-start.1
  53.8 0.2 fusion.66
  53.9 9.7 %collective-permute-done.8 = f32[256,512]{1,0:T(8,128)S(1)} collective-permute-done((f32[256,512]{1,0:T(8,128)S(1)}, f32[256,512]{1,0:T(8,128)S(1)}, u32[]{:S(2)}, u32[]{:S(2)}) %collective-permute-start.8) | collective-permute-done | bytes 524320 | tf_op jit(solution)/shard_map/ppermute | solution.py:80
  63.6 0.2 multiply_add_fusion.5
  63.8 1.9 %collective-permute-start.10 = (f32[256,512]{1,0:T(8,128)S(1)}, f32[256,512]{1,0:T(8,128)S(1)}, u32[]{:S(2)}, u32[]{:S(2)}) collective-permute-start(f32[256,512]{1,0:T(8,128)S(1)} %multiply_add_fusion.5), channel_id=1, source_target_pairs={{0,1},{1,0},{2,3},{3,2},{4,5},{5,4},{6,7},{7,6},{8,9},{9,8},{10,11... | collective-permute-start | bytes 1572872 | tf_op jit(solution)/shard_map/ppermute | solution.py:83
  65.7 4.3 %weight_field.1 = f32[256,512]{1,0:T(8,128)S(1)} custom-call(s32[1,4096]{1,0:T(1,128)S(1)} %copy-done, f32[1,4096]{1,0:T(1,128)S(1)} %copy-done.1), custom_call_target="tpu_custom_call" | custom-call | flops 3221225472 | bytes 524288 | tf_op jit(solution)/shard_map/weight_field/pallas_call | solution.py:41
  70.0 5.6 %collective-permute-start.11 = (f32[256,512]{1,0:T(8,128)S(1)}, f32[256,512]{1,0:T(8,128)S(1)}, u32[]{:S(2)}, u32[]{:S(2)}) collective-permute-start(f32[256,512]{1,0:T(8,128)S(1)} %multiply_add_fusion.5), channel_id=1, source_target_pairs={{1,2},{2,1},{3,4},{4,3},{5,6},{6,5},{7,8},{8,7},{9,10},{10,9},{11,... | collective-permute-start | bytes 1572872 | tf_op jit(solution)/shard_map/ppermute | solution.py:80
  75.7 0.8 fusion.40
  76.5 0.2 multiply_add_fusion.4
  76.7 6.0 %collective-permute-done.11 = f32[256,512]{1,0:T(8,128)S(1)} collective-permute-done((f32[256,512]{1,0:T(8,128)S(1)}, f32[256,512]{1,0:T(8,128)S(1)}, u32[]{:S(2)}, u32[]{:S(2)}) %collective-permute-start.11) | collective-permute-done | bytes 524320 | tf_op jit(solution)/shard_map/ppermute | solution.py:80
  82.6 0.2 fusion.77
  82.9 0.1 bitcast_multiply_fusion.7
  83.0 0.4 fusion.82
  83.4 1.9 %collective-permute-start.12 = (f32[256,512]{1,0:T(8,128)S(1)}, f32[256,512]{1,0:T(8,128)S(1)}, u32[]{:S(2)}, u32[]{:S(2)}) collective-permute-start(f32[256,512]{1,0:T(8,128)S(1)} %get-tuple-element.79), channel_id=1, source_target_pairs={{0,1},{1,0},{2,3},{3,2},{4,5},{5,4},{6,7},{7,6},{8,9},{9,8},{10,11... | collective-permute-start | bytes 1572872 | tf_op jit(solution)/shard_map/ppermute | solution.py:83
  85.3 5.6 %collective-permute-start.13 = (f32[256,512]{1,0:T(8,128)S(1)}, f32[256,512]{1,0:T(8,128)S(1)}, u32[]{:S(2)}, u32[]{:S(2)}) collective-permute-start(f32[256,512]{1,0:T(8,128)S(1)} %get-tuple-element.59), channel_id=1, source_target_pairs={{1,2},{2,1},{3,4},{4,3},{5,6},{6,5},{7,8},{8,7},{9,10},{10,9},{11,... | collective-permute-start | bytes 1572872 | tf_op jit(solution)/shard_map/ppermute | solution.py:80
  90.9 0.1 add.278
  91.0 6.9 %collective-permute-done.13 = f32[256,512]{1,0:T(8,128)S(1)} collective-permute-done((f32[256,512]{1,0:T(8,128)S(1)}, f32[256,512]{1,0:T(8,128)S(1)}, u32[]{:S(2)}, u32[]{:S(2)}) %collective-permute-start.13) | collective-permute-done | bytes 524320 | tf_op jit(solution)/shard_map/ppermute | solution.py:80
  97.9 0.1 fusion.76
  98.1 0.1 bitcast_multiply_fusion.6
  98.2 0.5 fusion.81
  98.7 1.9 %collective-permute-start.14 = (f32[256,512]{1,0:T(8,128)S(1)}, f32[256,512]{1,0:T(8,128)S(1)}, u32[]{:S(2)}, u32[]{:S(2)}) collective-permute-start(f32[256,512]{1,0:T(8,128)S(1)} %get-tuple-element.76), channel_id=1, source_target_pairs={{0,1},{1,0},{2,3},{3,2},{4,5},{5,4},{6,7},{7,6},{8,9},{9,8},{10,11... | collective-permute-start | bytes 1572872 | tf_op jit(solution)/shard_map/ppermute | solution.py:83
  100.6 5.6 %collective-permute-start.15 = (f32[256,512]{1,0:T(8,128)S(1)}, f32[256,512]{1,0:T(8,128)S(1)}, u32[]{:S(2)}, u32[]{:S(2)}) collective-permute-start(f32[256,512]{1,0:T(8,128)S(1)} %get-tuple-element.57), channel_id=1, source_target_pairs={{1,2},{2,1},{3,4},{4,3},{5,6},{6,5},{7,8},{8,7},{9,10},{10,9},{11,... | collective-permute-start | bytes 1572872 | tf_op jit(solution)/shard_map/ppermute | solution.py:80
  106.2 2.1 %collective-permute-start.2 = (f32[256,512]{1,0:T(8,128)S(1)}, f32[256,512]{1,0:T(8,128)S(1)}, u32[]{:S(2)}, u32[]{:S(2)}) collective-permute-start(f32[256,512]{1,0:T(8,128)S(1)} %get-tuple-element.32), channel_id=1, source_target_pairs={{1,2},{2,1},{3,4},{4,3},{5,6},{6,5},{7,8},{8,7},{9,10},{10,9},{11,... | collective-permute-start | bytes 1572872 | tf_op jit(solution)/shard_map/ppermute | solution.py:80
  108.3 0.1 add.285
  108.4 4.8 %collective-permute-done.15 = f32[256,512]{1,0:T(8,128)S(1)} collective-permute-done((f32[256,512]{1,0:T(8,128)S(1)}, f32[256,512]{1,0:T(8,128)S(1)}, u32[]{:S(2)}, u32[]{:S(2)}) %collective-permute-start.15) | collective-permute-done | bytes 524320 | tf_op jit(solution)/shard_map/ppermute | solution.py:80
  113.2 0.1 fusion.75
  113.4 1.9 %collective-permute-start.16 = (f32[256,512]{1,0:T(8,128)S(1)}, f32[256,512]{1,0:T(8,128)S(1)}, u32[]{:S(2)}, u32[]{:S(2)}) collective-permute-start(f32[256,512]{1,0:T(8,128)S(1)} %get-tuple-element.55), channel_id=1, source_target_pairs={{0,1},{1,0},{2,3},{3,2},{4,5},{5,4},{6,7},{7,6},{8,9},{9,8},{10,11... | collective-permute-start | bytes 1572872 | tf_op jit(solution)/shard_map/ppermute | solution.py:83
  115.3 0.1 bitcast_multiply_fusion.8
  115.4 3.5 %collective-permute-done.2 = f32[256,512]{1,0:T(8,128)S(1)} collective-permute-done((f32[256,512]{1,0:T(8,128)S(1)}, f32[256,512]{1,0:T(8,128)S(1)}, u32[]{:S(2)}, u32[]{:S(2)}) %collective-permute-start.2) | collective-permute-done | bytes 524320 | tf_op jit(solution)/shard_map/ppermute | solution.py:80
  118.8 0.6 multiply_add_fusion.2
  119.4 0.1 multiply_add_fusion.1
  119.6 0.2 broadcast_select_fusion.1
  119.8 1.1 pad_maximum_fusion
  120.9 7.7 %all-to-all-start = ((f32[8,64,512]{2,1,0:T(8,128)}), f32[8,64,512]{2,1,0:T(8,128)S(1)}, u32[]{:S(2)}, u32[]{:S(2)}) async-start(f32[8,64,512]{2,1,0:T(8,128)} %bitcast.13), calls=%async_computation | async-start | bytes 2097152 | tf_op jit(solution)/shard_map/all_to_all | solution.py:155
  128.6 0.1 pad_slice_fusion.43
  128.7 10.5 %all-to-all-done = f32[8,64,512]{2,1,0:T(8,128)S(1)} async-done(((f32[8,64,512]{2,1,0:T(8,128)}), f32[8,64,512]{2,1,0:T(8,128)S(1)}, u32[]{:S(2)}, u32[]{:S(2)}) %all-to-all-start) | async-done | bytes 1048608 | tf_op jit(solution)/shard_map/all_to_all | solution.py:155
  139.2 0.1 select_reduce_fusion
  139.3 2.0 %collective-permute-start.17 = (f32[32,512]{1,0:T(8,128)S(1)}, f32[32,512]{1,0:T(8,128)S(1)}, u32[]{:S(2)}, u32[]{:S(2)}) collective-permute-start(f32[32,512]{1,0:T(8,128)S(1)} %get-tuple-element.53), channel_id=1, source_target_pairs={{0,64},{64,0},{128,192},{192,128},{256,320},{320,256},{384,448},{4... | collective-permute-start | bytes 196616 | tf_op jit(solution)/shard_map/ppermute | solution.py:167
  141.3 0.9 fusion.74
  142.3 7.8 %collective-permute-done.17 = f32[32,512]{1,0:T(8,128)S(1)} collective-permute-done((f32[32,512]{1,0:T(8,128)S(1)}, f32[32,512]{1,0:T(8,128)S(1)}, u32[]{:S(2)}, u32[]{:S(2)}) %collective-permute-start.17) | collective-permute-done | bytes 65568 | tf_op jit(solution)/shard_map/ppermute | solution.py:167
  150.1 0.6 add_bitcast_fusion
  (26 shorter events, 0.2 us)
Async XLA Ops:
  0.0 18.1 %copy-start.5 = (f32[1,4,1,256,512]{4,3,2,1,0:T(8,128)S(1)}, f32[1,4,1,256,512]{4,3,2,1,0:T(8,128)}, u32[]{:S(2)}) copy-start(f32[1,4,1,256,512]{4,3,2,1,0:T(8,128)} %param.6) | copy-start | bytes 6291460
  0.0 22.0 %copy-start.2 = (f32[1,256,512]{2,1,0:T(8,128)S(1)}, f32[1,256,512]{2,1,0:T(8,128)}, u32[]{:S(2)}) copy-start(f32[1,256,512]{2,1,0:T(8,128)} %param.9) | copy-start | bytes 1572868
  0.0 18.2 %collective-permute-start = (f32[4,256,512]{2,1,0:T(8,128)}, f32[4,256,512]{2,1,0:T(8,128)S(1)}, u32[]{:S(2)}, u32[]{:S(2)}) collective-permute-start(f32[4,256,512]{2,1,0:T(8,128)} %bitcast.78), channel_id=1, source_target_pairs={{0,1},{1,0},{2,3},{3,2},{4,5},{5,4},{6,7},{7,6},{8,9},{9,8},{10,11... | collective-permute-start | bytes 6291464 | tf_op jit(solution)/shard_map/ppermute | solution.py:83
  3.3 18.7 %collective-permute-start.1 = (f32[256,512]{1,0:T(8,128)S(1)}, f32[256,512]{1,0:T(8,128)S(1)}, u32[]{:S(2)}, u32[]{:S(2)}) collective-permute-start(f32[256,512]{1,0:T(8,128)S(1)} %slice_bitcast_fusion.7), channel_id=1, source_target_pairs={{1,2},{2,1},{3,4},{4,3},{5,6},{6,5},{7,8},{8,7},{9,10},{10,9},{11,... | collective-permute-start | bytes 1572872 | tf_op jit(solution)/shard_map/ppermute | solution.py:80
  16.2 15.6 %collective-permute-start.3 = (f32[256,512]{1,0:T(8,128)S(1)}, f32[256,512]{1,0:T(8,128)S(1)}, u32[]{:S(2)}, u32[]{:S(2)}) collective-permute-start(f32[256,512]{1,0:T(8,128)S(1)} %slice_bitcast_fusion.5), channel_id=1, source_target_pairs={{1,2},{2,1},{3,4},{4,3},{5,6},{6,5},{7,8},{8,7},{9,10},{10,9},{11,... | collective-permute-start | bytes 1572872 | tf_op jit(solution)/shard_map/ppermute | solution.py:80
  18.5 13.3 %copy-start.3 = (f32[1,256,512]{2,1,0:T(8,128)S(1)}, f32[1,256,512]{2,1,0:T(8,128)}, u32[]{:S(2)}) copy-start(f32[1,256,512]{2,1,0:T(8,128)} %param.7) | copy-start | bytes 1572868
  18.5 13.3 %copy-start.4 = (f32[1,256,512]{2,1,0:T(8,128)S(1)}, f32[1,256,512]{2,1,0:T(8,128)}, u32[]{:S(2)}) copy-start(f32[1,256,512]{2,1,0:T(8,128)} %param.8) | copy-start | bytes 1572868
  22.1 10.6 %collective-permute-start.4 = (f32[256,512]{1,0:T(8,128)S(1)}, f32[256,512]{1,0:T(8,128)S(1)}, u32[]{:S(2)}, u32[]{:S(2)}) collective-permute-start(f32[256,512]{1,0:T(8,128)S(1)} %get-tuple-element.34), channel_id=1, source_target_pairs={{0,1},{1,0},{2,3},{3,2},{4,5},{5,4},{6,7},{7,6},{8,9},{9,8},{10,11... | collective-permute-start | bytes 1572872 | tf_op jit(solution)/shard_map/ppermute | solution.py:83
  24.1 28.8 %collective-permute-start.6 = (f32[288,512]{1,0:T(8,128)S(1)}, f32[288,512]{1,0:T(8,128)S(1)}, u32[]{:S(2)}, u32[]{:S(2)}) collective-permute-start(f32[288,512]{1,0:T(8,128)S(1)} %pad_maximum_fusion.1), channel_id=1, source_target_pairs={{1,2},{2,1},{3,4},{4,3},{5,6},{6,5},{7,8},{8,7},{9,10},{10,9},{11,... | collective-permute-start | bytes 1769480 | tf_op jit(solution)/shard_map/ppermute | solution.py:80
  29.9 13.2 %collective-permute-start.5 = (f32[256,512]{1,0:T(8,128)S(1)}, f32[256,512]{1,0:T(8,128)S(1)}, u32[]{:S(2)}, u32[]{:S(2)}) collective-permute-start(f32[256,512]{1,0:T(8,128)S(1)} %get-tuple-element.34), channel_id=1, source_target_pairs={{1,2},{2,1},{3,4},{4,3},{5,6},{6,5},{7,8},{8,7},{9,10},{10,9},{11,... | collective-permute-start | bytes 1572872 | tf_op jit(solution)/shard_map/ppermute | solution.py:80
  43.3 10.5 %collective-permute-start.7 = (f32[288,512]{1,0:T(8,128)S(1)}, f32[288,512]{1,0:T(8,128)S(1)}, u32[]{:S(2)}, u32[]{:S(2)}) collective-permute-start(f32[288,512]{1,0:T(8,128)S(1)} %pad_maximum_fusion.2), channel_id=1, source_target_pairs={{0,1},{1,0},{2,3},{3,2},{4,5},{5,4},{6,7},{7,6},{8,9},{9,8},{10,11... | collective-permute-start | bytes 1769480 | tf_op jit(solution)/shard_map/ppermute | solution.py:83
  45.2 30.4 %collective-permute-start.9 = (f32[256,512]{1,0:T(8,128)S(1)}, f32[256,512]{1,0:T(8,128)S(1)}, u32[]{:S(2)}, u32[]{:S(2)}) collective-permute-start(f32[256,512]{1,0:T(8,128)S(1)} %slice_bitcast_fusion.1), channel_id=1, source_target_pairs={{1,2},{2,1},{3,4},{4,3},{5,6},{6,5},{7,8},{8,7},{9,10},{10,9},{11,... | collective-permute-start | bytes 1572872 | tf_op jit(solution)/shard_map/ppermute | solution.py:80
  51.0 12.6 %collective-permute-start.8 = (f32[256,512]{1,0:T(8,128)S(1)}, f32[256,512]{1,0:T(8,128)S(1)}, u32[]{:S(2)}, u32[]{:S(2)}) collective-permute-start(f32[256,512]{1,0:T(8,128)S(1)} %multiply_add_fusion.6), channel_id=1, source_target_pairs={{1,2},{2,1},{3,4},{4,3},{5,6},{6,5},{7,8},{8,7},{9,10},{10,9},{11,... | collective-permute-start | bytes 1572872 | tf_op jit(solution)/shard_map/ppermute | solution.py:80
  53.7 10.0 %copy-start.6 = (f32[288,512]{1,0:T(8,128)}, f32[288,512]{1,0:T(8,128)S(1)}, u32[]{:S(2)}) copy-start(f32[288,512]{1,0:T(8,128)S(1)} %collective-permute-done.7) | copy-start | bytes 1769476
  53.7 12.0 %copy-start = (s32[1,4096]{1,0:T(1,128)S(1)}, s32[1,4096]{1,0:T(1,128)}, u32[]{:S(2)}) copy-start(s32[1,4096]{1,0:T(1,128)} %index_ref.1) | copy-start | bytes 49156
  53.8 12.0 %copy-start.1 = (f32[1,4096]{1,0:T(1,128)S(1)}, f32[1,4096]{1,0:T(1,128)}, u32[]{:S(2)}) copy-start(f32[1,4096]{1,0:T(1,128)} %weight_ref.1) | copy-start | bytes 49156
  63.8 12.7 %collective-permute-start.10 = (f32[256,512]{1,0:T(8,128)S(1)}, f32[256,512]{1,0:T(8,128)S(1)}, u32[]{:S(2)}, u32[]{:S(2)}) collective-permute-start(f32[256,512]{1,0:T(8,128)S(1)} %multiply_add_fusion.5), channel_id=1, source_target_pairs={{0,1},{1,0},{2,3},{3,2},{4,5},{5,4},{6,7},{7,6},{8,9},{9,8},{10,11... | collective-permute-start | bytes 1572872 | tf_op jit(solution)/shard_map/ppermute | solution.py:83
  70.0 12.6 %collective-permute-start.11 = (f32[256,512]{1,0:T(8,128)S(1)}, f32[256,512]{1,0:T(8,128)S(1)}, u32[]{:S(2)}, u32[]{:S(2)}) collective-permute-start(f32[256,512]{1,0:T(8,128)S(1)} %multiply_add_fusion.5), channel_id=1, source_target_pairs={{1,2},{2,1},{3,4},{4,3},{5,6},{6,5},{7,8},{8,7},{9,10},{10,9},{11,... | collective-permute-start | bytes 1572872 | tf_op jit(solution)/shard_map/ppermute | solution.py:80
  83.4 7.6 %collective-permute-start.12 = (f32[256,512]{1,0:T(8,128)S(1)}, f32[256,512]{1,0:T(8,128)S(1)}, u32[]{:S(2)}, u32[]{:S(2)}) collective-permute-start(f32[256,512]{1,0:T(8,128)S(1)} %get-tuple-element.79), channel_id=1, source_target_pairs={{0,1},{1,0},{2,3},{3,2},{4,5},{5,4},{6,7},{7,6},{8,9},{9,8},{10,11... | collective-permute-start | bytes 1572872 | tf_op jit(solution)/shard_map/ppermute | solution.py:83
  85.3 12.6 %collective-permute-start.13 = (f32[256,512]{1,0:T(8,128)S(1)}, f32[256,512]{1,0:T(8,128)S(1)}, u32[]{:S(2)}, u32[]{:S(2)}) collective-permute-start(f32[256,512]{1,0:T(8,128)S(1)} %get-tuple-element.59), channel_id=1, source_target_pairs={{1,2},{2,1},{3,4},{4,3},{5,6},{6,5},{7,8},{8,7},{9,10},{10,9},{11,... | collective-permute-start | bytes 1572872 | tf_op jit(solution)/shard_map/ppermute | solution.py:80
  98.7 9.6 %collective-permute-start.14 = (f32[256,512]{1,0:T(8,128)S(1)}, f32[256,512]{1,0:T(8,128)S(1)}, u32[]{:S(2)}, u32[]{:S(2)}) collective-permute-start(f32[256,512]{1,0:T(8,128)S(1)} %get-tuple-element.76), channel_id=1, source_target_pairs={{0,1},{1,0},{2,3},{3,2},{4,5},{5,4},{6,7},{7,6},{8,9},{9,8},{10,11... | collective-permute-start | bytes 1572872 | tf_op jit(solution)/shard_map/ppermute | solution.py:83
  100.6 12.6 %collective-permute-start.15 = (f32[256,512]{1,0:T(8,128)S(1)}, f32[256,512]{1,0:T(8,128)S(1)}, u32[]{:S(2)}, u32[]{:S(2)}) collective-permute-start(f32[256,512]{1,0:T(8,128)S(1)} %get-tuple-element.57), channel_id=1, source_target_pairs={{1,2},{2,1},{3,4},{4,3},{5,6},{6,5},{7,8},{8,7},{9,10},{10,9},{11,... | collective-permute-start | bytes 1572872 | tf_op jit(solution)/shard_map/ppermute | solution.py:80
  106.2 12.6 %collective-permute-start.2 = (f32[256,512]{1,0:T(8,128)S(1)}, f32[256,512]{1,0:T(8,128)S(1)}, u32[]{:S(2)}, u32[]{:S(2)}) collective-permute-start(f32[256,512]{1,0:T(8,128)S(1)} %get-tuple-element.32), channel_id=1, source_target_pairs={{1,2},{2,1},{3,4},{4,3},{5,6},{6,5},{7,8},{8,7},{9,10},{10,9},{11,... | collective-permute-start | bytes 1572872 | tf_op jit(solution)/shard_map/ppermute | solution.py:80
  113.4 6.2 %collective-permute-start.16 = (f32[256,512]{1,0:T(8,128)S(1)}, f32[256,512]{1,0:T(8,128)S(1)}, u32[]{:S(2)}, u32[]{:S(2)}) collective-permute-start(f32[256,512]{1,0:T(8,128)S(1)} %get-tuple-element.55), channel_id=1, source_target_pairs={{0,1},{1,0},{2,3},{3,2},{4,5},{5,4},{6,7},{7,6},{8,9},{9,8},{10,11... | collective-permute-start | bytes 1572872 | tf_op jit(solution)/shard_map/ppermute | solution.py:83
  120.9 18.3 %all-to-all-start = ((f32[8,64,512]{2,1,0:T(8,128)}), f32[8,64,512]{2,1,0:T(8,128)S(1)}, u32[]{:S(2)}, u32[]{:S(2)}) async-start(f32[8,64,512]{2,1,0:T(8,128)} %bitcast.13), calls=%async_computation | async-start | bytes 2097152 | tf_op jit(solution)/shard_map/all_to_all | solution.py:155
  139.3 10.8 %collective-permute-start.17 = (f32[32,512]{1,0:T(8,128)S(1)}, f32[32,512]{1,0:T(8,128)S(1)}, u32[]{:S(2)}, u32[]{:S(2)}) collective-permute-start(f32[32,512]{1,0:T(8,128)S(1)} %get-tuple-element.53), channel_id=1, source_target_pairs={{0,64},{64,0},{128,192},{192,128},{256,320},{320,256},{384,448},{4... | collective-permute-start | bytes 196616 | tf_op jit(solution)/shard_map/ppermute | solution.py:167

commit v6 on v4

--- a/solution.py
+++ b/solution.py
@@ -105,6 +105,8 @@
     def lap_of(step):
         return source_gain * (overs[step] + nears[step] + side_sum(fields[step]))
 
+    gain_pair = far_gain * across(far_gain)
+
     weights = weight_field(obs_index, obs_weight, rows, columns)
 
     (inner,) = hold(nears[0] + side_sum(fields[0]))
@@ -125,20 +127,29 @@
         (base,) = hold(base + near_gain * side)
         tangent = base + far_gain * over
 
-    adjoint = tangent * weights
-    partial_value = None
-    for step in range(steps - 2, -1, -1):
-        over = across(far_gain * adjoint)
-        side = beside(near_gain * adjoint)
-        term = laps[step + 1] * adjoint
-        partial_value = term if partial_value is None else partial_value + term
-        base = adjoint + side_sum(kappa * adjoint) - courant * adjoint
-        base, partial_value = hold(base, partial_value)
-        (base,) = hold(base + side)
-        if step:
-            adjoint = base + over
-    (rest,) = hold(partial_value + laps[0] * base)
-    partial_value = rest + laps[0] * over
+    def settled(field):
+        side = beside(near_gain * field)
+        base = field + side_sum(kappa * field) - courant * field
+        (base,) = hold(base)
+        return hold(base + side)[0]
+
+    adjoint, sent = hold(tangent * weights, far_gain * (tangent * weights))
+    over = across(sent)
+    ready = settled(adjoint)
+    sent, ready, before = hold(far_gain * ready, ready, adjoint)
+    early = across(sent)
+    echo, partial_value = hold(gain_pair * before, laps[3] * before)
+    (adjoint,) = hold(ready + over)
+    ready = settled(adjoint)
+    sent, ready, before = hold(far_gain * ready, ready, adjoint)
+    later = across(sent)
+    ready, echo, partial_value = hold(
+        ready + echo, gain_pair * before, partial_value + laps[2] * before
+    )
+    (adjoint,) = hold(ready + early)
+    ready = settled(adjoint)
+    (rest,) = hold(partial_value + laps[1] * adjoint + laps[0] * (ready + echo))
+    partial_value = rest + laps[0] * later
 
     groups = [list(range(side, scens, 2)) for side in range(2)]
     pieces = lax.all_to_all(

time: 154 us -> 159 us (1.032)
  waiting for transfers between devices: 65.7 us -> 68.3 us
  starting transfers between devices: 71.6 us -> 73.6 us
    ppermute x10 -> x11, waiting for transfers between devices: 49.7 us -> 52.3 us  [across(): return lax.ppermute(field, 'grid', far)]
    ppermute x10 -> x11, starting transfers between devices: 51.6 us -> 53.6 us  [across(): return lax.ppermute(field, 'grid', far)]
  transfers between devices with their start and end apart: 19 -> 20, of which waited for: 9 -> 10; matrix products, arithmetic and copies ran while one was open for 5% -> 5% of each run, Pallas kernels for 3% -> 3%
where the time goes in v6:
time: 159 us
  starting transfers between devices  73.6 us (46%)
  waiting for transfers between devices  68.3 us (43%)
  other arithmetic  9.48 us (6%)
  Pallas kernels  4.3 us (3%)
  local copies, waits for them, and re-layouts  2.4 us (2%)
    ppermute x11, starting transfers between devices, across(): return lax.ppermute(field, 'grid', far)  53.6 us
    ppermute x11, waiting for transfers between devices, across(): return lax.ppermute(field, 'grid', far)  52.3 us
    ppermute x7, starting transfers between devices, beside(): return lax.ppermute(field, 'grid', near)  13.7 us
    all_to_all x1, waiting for transfers between devices, local(): lax.all_to_all(partial_value, 'scen', 0, 0, axis_index_groups=groups, til...  8.2 us
    ppermute x1, waiting for transfers between devices, local(): other = lax.ppermute(other, 'scen', [(s, s ^ 1) for s in range(scens)])  7.82 us
    pallas_call x1, Pallas kernels, weight_field(): pl.pallas_call(weight_kernel, grid=(count // chunk,), in_specs=[pl.BlockS...  4.3 us
    all_to_all x1, starting transfers between devices, local(): lax.all_to_all(partial_value, 'scen', 0, 0, axis_index_groups=groups, til...  4.29 us
  transfers between devices with their start and end apart: 20, of which 10 were waited for; matrix products, arithmetic and copies ran while one was open for 5% of the time, Pallas kernels for 3%

profile of v6, /device:TPU:40, one launch (start us, length us, event | category | flops | bytes accessed | tf_op | source)
XLA Modules:
  0.0 158.7 jit_solution(1675667457338555221)
XLA Ops:
  0.0 2.2 %collective-permute-start = (f32[4,256,512]{2,1,0:T(8,128)}, f32[4,256,512]{2,1,0:T(8,128)S(1)}, u32[]{:S(2)}, u32[]{:S(2)}) collective-permute-start(f32[4,256,512]{2,1,0:T(8,128)} %bitcast.77), channel_id=1, source_target_pairs={{0,1},{1,0},{2,3},{3,2},{4,5},{5,4},{6,7},{7,6},{8,9},{9,8},{10,11... | collective-permute-start | bytes 6291464 | tf_op jit(solution)/shard_map/ppermute | solution.py:83
  2.2 1.1 slice_bitcast_fusion.7
  3.3 11.8 %collective-permute-start.1 = (f32[256,512]{1,0:T(8,128)S(1)}, f32[256,512]{1,0:T(8,128)S(1)}, u32[]{:S(2)}, u32[]{:S(2)}) collective-permute-start(f32[256,512]{1,0:T(8,128)S(1)} %slice_bitcast_fusion.7), channel_id=1, source_target_pairs={{1,2},{2,1},{3,4},{4,3},{5,6},{6,5},{7,8},{8,7},{9,10},{10,9},{11,... | collective-permute-start | bytes 1572872 | tf_op jit(solution)/shard_map/ppermute | solution.py:80
  15.1 1.1 slice_bitcast_fusion.5
  16.2 1.9 %collective-permute-start.2 = (f32[256,512]{1,0:T(8,128)S(1)}, f32[256,512]{1,0:T(8,128)S(1)}, u32[]{:S(2)}, u32[]{:S(2)}) collective-permute-start(f32[256,512]{1,0:T(8,128)S(1)} %slice_bitcast_fusion.5), channel_id=1, source_target_pairs={{1,2},{2,1},{3,4},{4,3},{5,6},{6,5},{7,8},{8,7},{9,10},{10,9},{11,... | collective-permute-start | bytes 1572872 | tf_op jit(solution)/shard_map/ppermute | solution.py:80
  18.2 0.3 fusion.4
  18.6 3.4 %collective-permute-done.1 = f32[256,512]{1,0:T(8,128)S(1)} collective-permute-done((f32[256,512]{1,0:T(8,128)S(1)}, f32[256,512]{1,0:T(8,128)S(1)}, u32[]{:S(2)}, u32[]{:S(2)}) %collective-permute-start.1) | collective-permute-done | bytes 524320 | tf_op jit(solution)/shard_map/ppermute | solution.py:80
  22.0 0.2 bitcast_multiply_fusion.9
  22.1 1.9 %collective-permute-start.3 = (f32[256,512]{1,0:T(8,128)S(1)}, f32[256,512]{1,0:T(8,128)S(1)}, u32[]{:S(2)}, u32[]{:S(2)}) collective-permute-start(f32[256,512]{1,0:T(8,128)S(1)} %get-tuple-element.38), channel_id=1, source_target_pairs={{0,1},{1,0},{2,3},{3,2},{4,5},{5,4},{6,7},{7,6},{8,9},{9,8},{10,11... | collective-permute-start | bytes 1572872 | tf_op jit(solution)/shard_map/ppermute | solution.py:83
  24.1 5.8 %collective-permute-start.5 = (f32[288,512]{1,0:T(8,128)S(1)}, f32[288,512]{1,0:T(8,128)S(1)}, u32[]{:S(2)}, u32[]{:S(2)}) collective-permute-start(f32[288,512]{1,0:T(8,128)S(1)} %pad_maximum_fusion), channel_id=1, source_target_pairs={{1,2},{2,1},{3,4},{4,3},{5,6},{6,5},{7,8},{8,7},{9,10},{10,9},{11,... | collective-permute-start | bytes 1769480 | tf_op jit(solution)/shard_map/ppermute | solution.py:80
  29.9 1.9 %collective-permute-start.4 = (f32[256,512]{1,0:T(8,128)S(1)}, f32[256,512]{1,0:T(8,128)S(1)}, u32[]{:S(2)}, u32[]{:S(2)}) collective-permute-start(f32[256,512]{1,0:T(8,128)S(1)} %get-tuple-element.38), channel_id=1, source_target_pairs={{1,2},{2,1},{3,4},{4,3},{5,6},{6,5},{7,8},{8,7},{9,10},{10,9},{11,... | collective-permute-start | bytes 1572872 | tf_op jit(solution)/shard_map/ppermute | solution.py:80
  31.8 0.9 fusion.12
  32.8 0.1 multiply_add_fusion.6
  32.9 10.1 %collective-permute-done.4 = f32[256,512]{1,0:T(8,128)S(1)} collective-permute-done((f32[256,512]{1,0:T(8,128)S(1)}, f32[256,512]{1,0:T(8,128)S(1)}, u32[]{:S(2)}, u32[]{:S(2)}) %collective-permute-start.4) | collective-permute-done | bytes 524320 | tf_op jit(solution)/shard_map/ppermute | solution.py:80
  43.1 0.1 multiply_add_fusion.5
  43.3 1.9 %collective-permute-start.6 = (f32[288,512]{1,0:T(8,128)S(1)}, f32[288,512]{1,0:T(8,128)S(1)}, u32[]{:S(2)}, u32[]{:S(2)}) collective-permute-start(f32[288,512]{1,0:T(8,128)S(1)} %pad_maximum_fusion.1), channel_id=1, source_target_pairs={{0,1},{1,0},{2,3},{3,2},{4,5},{5,4},{6,7},{7,6},{8,9},{9,8},{10,11... | collective-permute-start | bytes 1769480 | tf_op jit(solution)/shard_map/ppermute | solution.py:83
  45.2 5.8 %collective-permute-start.8 = (f32[256,512]{1,0:T(8,128)S(1)}, f32[256,512]{1,0:T(8,128)S(1)}, u32[]{:S(2)}, u32[]{:S(2)}) collective-permute-start(f32[256,512]{1,0:T(8,128)S(1)} %slice_bitcast_fusion.1), channel_id=1, source_target_pairs={{1,2},{2,1},{3,4},{4,3},{5,6},{6,5},{7,8},{8,7},{9,10},{10,9},{11,... | collective-permute-start | bytes 1572872 | tf_op jit(solution)/shard_map/ppermute | solution.py:80
  51.0 1.9 %collective-permute-start.7 = (f32[256,512]{1,0:T(8,128)S(1)}, f32[256,512]{1,0:T(8,128)S(1)}, u32[]{:S(2)}, u32[]{:S(2)}) collective-permute-start(f32[256,512]{1,0:T(8,128)S(1)} %multiply_add_fusion.5), channel_id=1, source_target_pairs={{1,2},{2,1},{3,4},{4,3},{5,6},{6,5},{7,8},{8,7},{9,10},{10,9},{11,... | collective-permute-start | bytes 1572872 | tf_op jit(solution)/shard_map/ppermute | solution.py:80
  52.9 0.8 fusion.26
  53.8 0.2 fusion.66
  53.9 9.7 %collective-permute-done.7 = f32[256,512]{1,0:T(8,128)S(1)} collective-permute-done((f32[256,512]{1,0:T(8,128)S(1)}, f32[256,512]{1,0:T(8,128)S(1)}, u32[]{:S(2)}, u32[]{:S(2)}) %collective-permute-start.7) | collective-permute-done | bytes 524320 | tf_op jit(solution)/shard_map/ppermute | solution.py:80
  63.6 0.2 multiply_add_fusion.4
  63.8 1.9 %collective-permute-start.9 = (f32[256,512]{1,0:T(8,128)S(1)}, f32[256,512]{1,0:T(8,128)S(1)}, u32[]{:S(2)}, u32[]{:S(2)}) collective-permute-start(f32[256,512]{1,0:T(8,128)S(1)} %multiply_add_fusion.4), channel_id=1, source_target_pairs={{0,1},{1,0},{2,3},{3,2},{4,5},{5,4},{6,7},{7,6},{8,9},{9,8},{10,11... | collective-permute-start | bytes 1572872 | tf_op jit(solution)/shard_map/ppermute | solution.py:83
  65.7 4.3 %weight_field.1 = f32[256,512]{1,0:T(8,128)S(1)} custom-call(s32[1,4096]{1,0:T(1,128)S(1)} %copy-done, f32[1,4096]{1,0:T(1,128)S(1)} %copy-done.1), custom_call_target="tpu_custom_call" | custom-call | flops 3221225472 | bytes 524288 | tf_op jit(solution)/shard_map/weight_field/pallas_call | solution.py:41
  70.0 5.6 %collective-permute-start.10 = (f32[256,512]{1,0:T(8,128)S(1)}, f32[256,512]{1,0:T(8,128)S(1)}, u32[]{:S(2)}, u32[]{:S(2)}) collective-permute-start(f32[256,512]{1,0:T(8,128)S(1)} %multiply_add_fusion.4), channel_id=1, source_target_pairs={{1,2},{2,1},{3,4},{4,3},{5,6},{6,5},{7,8},{8,7},{9,10},{10,9},{11,... | collective-permute-start | bytes 1572872 | tf_op jit(solution)/shard_map/ppermute | solution.py:80
  75.7 0.8 fusion.40
  76.5 0.2 multiply_add_fusion.3
  76.7 6.0 %collective-permute-done.10 = f32[256,512]{1,0:T(8,128)S(1)} collective-permute-done((f32[256,512]{1,0:T(8,128)S(1)}, f32[256,512]{1,0:T(8,128)S(1)}, u32[]{:S(2)}, u32[]{:S(2)}) %collective-permute-start.10) | collective-permute-done | bytes 524320 | tf_op jit(solution)/shard_map/ppermute | solution.py:80
  82.6 0.2 fusion.75
  82.9 0.1 bitcast_multiply_fusion.7
  83.0 0.4 fusion.81
  83.3 1.9 %collective-permute-start.11 = (f32[256,512]{1,0:T(8,128)S(1)}, f32[256,512]{1,0:T(8,128)S(1)}, u32[]{:S(2)}, u32[]{:S(2)}) collective-permute-start(f32[256,512]{1,0:T(8,128)S(1)} %get-tuple-element.84), channel_id=1, source_target_pairs={{0,1},{1,0},{2,3},{3,2},{4,5},{5,4},{6,7},{7,6},{8,9},{9,8},{10,11... | collective-permute-start | bytes 1572872 | tf_op jit(solution)/shard_map/ppermute | solution.py:83
  85.3 5.6 %collective-permute-start.12 = (f32[256,512]{1,0:T(8,128)S(1)}, f32[256,512]{1,0:T(8,128)S(1)}, u32[]{:S(2)}, u32[]{:S(2)}) collective-permute-start(f32[256,512]{1,0:T(8,128)S(1)} %get-tuple-element.48), channel_id=1, source_target_pairs={{1,2},{2,1},{3,4},{4,3},{5,6},{6,5},{7,8},{8,7},{9,10},{10,9},{11,... | collective-permute-start | bytes 1572872 | tf_op jit(solution)/shard_map/ppermute | solution.py:80
  90.9 0.1 add.287
  91.0 0.1 mul.209
  91.1 6.8 %collective-permute-done.12 = f32[256,512]{1,0:T(8,128)S(1)} collective-permute-done((f32[256,512]{1,0:T(8,128)S(1)}, f32[256,512]{1,0:T(8,128)S(1)}, u32[]{:S(2)}, u32[]{:S(2)}) %collective-permute-start.12) | collective-permute-done | bytes 524320 | tf_op jit(solution)/shard_map/ppermute | solution.py:80
  97.9 0.1 add.288
  98.0 0.1 bitcast_multiply_fusion.6
  98.1 0.4 fusion.80
  98.4 1.9 %collective-permute-start.13 = (f32[256,512]{1,0:T(8,128)S(1)}, f32[256,512]{1,0:T(8,128)S(1)}, u32[]{:S(2)}, u32[]{:S(2)}) collective-permute-start(f32[256,512]{1,0:T(8,128)S(1)} %get-tuple-element.82), channel_id=1, source_target_pairs={{0,1},{1,0},{2,3},{3,2},{4,5},{5,4},{6,7},{7,6},{8,9},{9,8},{10,11... | collective-permute-start | bytes 1572872 | tf_op jit(solution)/shard_map/ppermute | solution.py:83
  100.4 5.6 %collective-permute-start.14 = (f32[256,512]{1,0:T(8,128)S(1)}, f32[256,512]{1,0:T(8,128)S(1)}, u32[]{:S(2)}, u32[]{:S(2)}) collective-permute-start(f32[256,512]{1,0:T(8,128)S(1)} %get-tuple-element.36), channel_id=1, source_target_pairs={{1,2},{2,1},{3,4},{4,3},{5,6},{6,5},{7,8},{8,7},{9,10},{10,9},{11,... | collective-permute-start | bytes 1572872 | tf_op jit(solution)/shard_map/ppermute | solution.py:80
  106.0 2.1 %collective-permute-start.15 = (f32[256,512]{1,0:T(8,128)S(1)}, f32[256,512]{1,0:T(8,128)S(1)}, u32[]{:S(2)}, u32[]{:S(2)}) collective-permute-start(f32[256,512]{1,0:T(8,128)S(1)} %mul.209), channel_id=1, source_target_pairs={{1,2},{2,1},{3,4},{4,3},{5,6},{6,5},{7,8},{8,7},{9,10},{10,9},{11,... | collective-permute-start | bytes 1572872 | tf_op jit(solution)/shard_map/ppermute | solution.py:80
  108.1 0.1 add.293
  108.1 0.1 mul.214
  108.2 4.7 %collective-permute-done.14 = f32[256,512]{1,0:T(8,128)S(1)} collective-permute-done((f32[256,512]{1,0:T(8,128)S(1)}, f32[256,512]{1,0:T(8,128)S(1)}, u32[]{:S(2)}, u32[]{:S(2)}) %collective-permute-start.14) | collective-permute-done | bytes 524320 | tf_op jit(solution)/shard_map/ppermute | solution.py:80
  113.0 0.3 multiply_multiply_fusion
  113.3 0.1 add.294
  113.4 0.2 multiply_add_fusion.2
  113.5 5.1 %collective-permute-done.15 = f32[256,512]{1,0:T(8,128)S(1)} collective-permute-done((f32[256,512]{1,0:T(8,128)S(1)}, f32[256,512]{1,0:T(8,128)S(1)}, u32[]{:S(2)}, u32[]{:S(2)}) %collective-permute-start.15) | collective-permute-done | bytes 524320 | tf_op jit(solution)/shard_map/ppermute | solution.py:80
  118.7 0.1 bitcast_multiply_fusion.8
  118.8 0.3 fusion.79
  119.1 1.9 %collective-permute-start.16 = (f32[256,512]{1,0:T(8,128)S(1)}, f32[256,512]{1,0:T(8,128)S(1)}, u32[]{:S(2)}, u32[]{:S(2)}) collective-permute-start(f32[256,512]{1,0:T(8,128)S(1)} %get-tuple-element.80), channel_id=1, source_target_pairs={{0,1},{1,0},{2,3},{3,2},{4,5},{5,4},{6,7},{7,6},{8,9},{9,8},{10,11... | collective-permute-start | bytes 1572872 | tf_op jit(solution)/shard_map/ppermute | solution.py:83
  121.0 5.6 %collective-permute-start.17 = (f32[256,512]{1,0:T(8,128)S(1)}, f32[256,512]{1,0:T(8,128)S(1)}, u32[]{:S(2)}, u32[]{:S(2)}) collective-permute-start(f32[256,512]{1,0:T(8,128)S(1)} %mul.214), channel_id=1, source_target_pairs={{1,2},{2,1},{3,4},{4,3},{5,6},{6,5},{7,8},{8,7},{9,10},{10,9},{11,... | collective-permute-start | bytes 1572872 | tf_op jit(solution)/shard_map/ppermute | solution.py:80
  126.7 0.1 add.302
  126.8 0.4 multiply_add_fusion.1
  127.1 6.5 %collective-permute-done.17 = f32[256,512]{1,0:T(8,128)S(1)} collective-permute-done((f32[256,512]{1,0:T(8,128)S(1)}, f32[256,512]{1,0:T(8,128)S(1)}, u32[]{:S(2)}, u32[]{:S(2)}) %collective-permute-start.17) | collective-permute-done | bytes 524320 | tf_op jit(solution)/shard_map/ppermute | solution.py:80
  133.7 0.9 multiply_add_fusion
  134.6 4.3 %all-to-all-start = ((f32[4,64,512]{2,1,0:T(8,128)}), f32[4,64,512]{2,1,0:T(8,128)S(1)}, u32[]{:S(2)}, u32[]{:S(2)}) async-start(f32[4,64,512]{2,1,0:T(8,128)} %bitcast.13), calls=%async_computation | async-start | bytes 1048576 | tf_op jit(solution)/shard_map/all_to_all | solution.py:155
  138.9 0.1 pad_slice_fusion.43
  139.0 8.2 %all-to-all-done = f32[4,64,512]{2,1,0:T(8,128)S(1)} async-done(((f32[4,64,512]{2,1,0:T(8,128)}), f32[4,64,512]{2,1,0:T(8,128)S(1)}, u32[]{:S(2)}, u32[]{:S(2)}) %all-to-all-start) | async-done | bytes 524320 | tf_op jit(solution)/shard_map/all_to_all | solution.py:155
  147.3 2.0 %collective-permute-start.18 = (f32[32,512]{1,0:T(8,128)S(1)}, f32[32,512]{1,0:T(8,128)S(1)}, u32[]{:S(2)}, u32[]{:S(2)}) collective-permute-start(f32[32,512]{1,0:T(8,128)S(1)} %get-tuple-element.63), channel_id=1, source_target_pairs={{0,64},{64,0},{128,192},{192,128},{256,320},{320,256},{384,448},{4... | collective-permute-start | bytes 196616 | tf_op jit(solution)/shard_map/ppermute | solution.py:167
  149.3 0.9 fusion.74
  150.2 7.8 %collective-permute-done.18 = f32[32,512]{1,0:T(8,128)S(1)} collective-permute-done((f32[32,512]{1,0:T(8,128)S(1)}, f32[32,512]{1,0:T(8,128)S(1)}, u32[]{:S(2)}, u32[]{:S(2)}) %collective-permute-start.18) | collective-permute-done | bytes 65568 | tf_op jit(solution)/shard_map/ppermute | solution.py:167
  158.0 0.6 add_bitcast_fusion
  (33 shorter events, 0.4 us)
Async XLA Ops:
  0.0 18.1 %copy-start.5 = (f32[1,4,1,256,512]{4,3,2,1,0:T(8,128)S(1)}, f32[1,4,1,256,512]{4,3,2,1,0:T(8,128)}, u32[]{:S(2)}) copy-start(f32[1,4,1,256,512]{4,3,2,1,0:T(8,128)} %param.6) | copy-start | bytes 6291460
  0.0 22.0 %copy-start.2 = (f32[1,256,512]{2,1,0:T(8,128)S(1)}, f32[1,256,512]{2,1,0:T(8,128)}, u32[]{:S(2)}) copy-start(f32[1,256,512]{2,1,0:T(8,128)} %param.9) | copy-start | bytes 1572868
  0.0 18.2 %collective-permute-start = (f32[4,256,512]{2,1,0:T(8,128)}, f32[4,256,512]{2,1,0:T(8,128)S(1)}, u32[]{:S(2)}, u32[]{:S(2)}) collective-permute-start(f32[4,256,512]{2,1,0:T(8,128)} %bitcast.77), channel_id=1, source_target_pairs={{0,1},{1,0},{2,3},{3,2},{4,5},{5,4},{6,7},{7,6},{8,9},{9,8},{10,11... | collective-permute-start | bytes 6291464 | tf_op jit(solution)/shard_map/ppermute | solution.py:83
  3.3 18.7 %collective-permute-start.1 = (f32[256,512]{1,0:T(8,128)S(1)}, f32[256,512]{1,0:T(8,128)S(1)}, u32[]{:S(2)}, u32[]{:S(2)}) collective-permute-start(f32[256,512]{1,0:T(8,128)S(1)} %slice_bitcast_fusion.7), channel_id=1, source_target_pairs={{1,2},{2,1},{3,4},{4,3},{5,6},{6,5},{7,8},{8,7},{9,10},{10,9},{11,... | collective-permute-start | bytes 1572872 | tf_op jit(solution)/shard_map/ppermute | solution.py:80
  16.2 15.6 %collective-permute-start.2 = (f32[256,512]{1,0:T(8,128)S(1)}, f32[256,512]{1,0:T(8,128)S(1)}, u32[]{:S(2)}, u32[]{:S(2)}) collective-permute-start(f32[256,512]{1,0:T(8,128)S(1)} %slice_bitcast_fusion.5), channel_id=1, source_target_pairs={{1,2},{2,1},{3,4},{4,3},{5,6},{6,5},{7,8},{8,7},{9,10},{10,9},{11,... | collective-permute-start | bytes 1572872 | tf_op jit(solution)/shard_map/ppermute | solution.py:80
  18.5 13.3 %copy-start.3 = (f32[1,256,512]{2,1,0:T(8,128)S(1)}, f32[1,256,512]{2,1,0:T(8,128)}, u32[]{:S(2)}) copy-start(f32[1,256,512]{2,1,0:T(8,128)} %param.7) | copy-start | bytes 1572868
  18.5 13.3 %copy-start.4 = (f32[1,256,512]{2,1,0:T(8,128)S(1)}, f32[1,256,512]{2,1,0:T(8,128)}, u32[]{:S(2)}) copy-start(f32[1,256,512]{2,1,0:T(8,128)} %param.8) | copy-start | bytes 1572868
  22.1 10.7 %collective-permute-start.3 = (f32[256,512]{1,0:T(8,128)S(1)}, f32[256,512]{1,0:T(8,128)S(1)}, u32[]{:S(2)}, u32[]{:S(2)}) collective-permute-start(f32[256,512]{1,0:T(8,128)S(1)} %get-tuple-element.38), channel_id=1, source_target_pairs={{0,1},{1,0},{2,3},{3,2},{4,5},{5,4},{6,7},{7,6},{8,9},{9,8},{10,11... | collective-permute-start | bytes 1572872 | tf_op jit(solution)/shard_map/ppermute | solution.py:83
  24.1 28.8 %collective-permute-start.5 = (f32[288,512]{1,0:T(8,128)S(1)}, f32[288,512]{1,0:T(8,128)S(1)}, u32[]{:S(2)}, u32[]{:S(2)}) collective-permute-start(f32[288,512]{1,0:T(8,128)S(1)} %pad_maximum_fusion), channel_id=1, source_target_pairs={{1,2},{2,1},{3,4},{4,3},{5,6},{6,5},{7,8},{8,7},{9,10},{10,9},{11,... | collective-permute-start | bytes 1769480 | tf_op jit(solution)/shard_map/ppermute | solution.py:80
  29.9 13.2 %collective-permute-start.4 = (f32[256,512]{1,0:T(8,128)S(1)}, f32[256,512]{1,0:T(8,128)S(1)}, u32[]{:S(2)}, u32[]{:S(2)}) collective-permute-start(f32[256,512]{1,0:T(8,128)S(1)} %get-tuple-element.38), channel_id=1, source_target_pairs={{1,2},{2,1},{3,4},{4,3},{5,6},{6,5},{7,8},{8,7},{9,10},{10,9},{11,... | collective-permute-start | bytes 1572872 | tf_op jit(solution)/shard_map/ppermute | solution.py:80
  43.3 10.5 %collective-permute-start.6 = (f32[288,512]{1,0:T(8,128)S(1)}, f32[288,512]{1,0:T(8,128)S(1)}, u32[]{:S(2)}, u32[]{:S(2)}) collective-permute-start(f32[288,512]{1,0:T(8,128)S(1)} %pad_maximum_fusion.1), channel_id=1, source_target_pairs={{0,1},{1,0},{2,3},{3,2},{4,5},{5,4},{6,7},{7,6},{8,9},{9,8},{10,11... | collective-permute-start | bytes 1769480 | tf_op jit(solution)/shard_map/ppermute | solution.py:83
  45.2 30.4 %collective-permute-start.8 = (f32[256,512]{1,0:T(8,128)S(1)}, f32[256,512]{1,0:T(8,128)S(1)}, u32[]{:S(2)}, u32[]{:S(2)}) collective-permute-start(f32[256,512]{1,0:T(8,128)S(1)} %slice_bitcast_fusion.1), channel_id=1, source_target_pairs={{1,2},{2,1},{3,4},{4,3},{5,6},{6,5},{7,8},{8,7},{9,10},{10,9},{11,... | collective-permute-start | bytes 1572872 | tf_op jit(solution)/shard_map/ppermute | solution.py:80
  51.0 12.6 %collective-permute-start.7 = (f32[256,512]{1,0:T(8,128)S(1)}, f32[256,512]{1,0:T(8,128)S(1)}, u32[]{:S(2)}, u32[]{:S(2)}) collective-permute-start(f32[256,512]{1,0:T(8,128)S(1)} %multiply_add_fusion.5), channel_id=1, source_target_pairs={{1,2},{2,1},{3,4},{4,3},{5,6},{6,5},{7,8},{8,7},{9,10},{10,9},{11,... | collective-permute-start | bytes 1572872 | tf_op jit(solution)/shard_map/ppermute | solution.py:80
  53.7 10.0 %copy-start.6 = (f32[288,512]{1,0:T(8,128)}, f32[288,512]{1,0:T(8,128)S(1)}, u32[]{:S(2)}) copy-start(f32[288,512]{1,0:T(8,128)S(1)} %collective-permute-done.6) | copy-start | bytes 1769476
  53.7 12.0 %copy-start = (s32[1,4096]{1,0:T(1,128)S(1)}, s32[1,4096]{1,0:T(1,128)}, u32[]{:S(2)}) copy-start(s32[1,4096]{1,0:T(1,128)} %index_ref.1) | copy-start | bytes 49156
  53.8 12.0 %copy-start.1 = (f32[1,4096]{1,0:T(1,128)S(1)}, f32[1,4096]{1,0:T(1,128)}, u32[]{:S(2)}) copy-start(f32[1,4096]{1,0:T(1,128)} %weight_ref.1) | copy-start | bytes 49156
  63.8 12.7 %collective-permute-start.9 = (f32[256,512]{1,0:T(8,128)S(1)}, f32[256,512]{1,0:T(8,128)S(1)}, u32[]{:S(2)}, u32[]{:S(2)}) collective-permute-start(f32[256,512]{1,0:T(8,128)S(1)} %multiply_add_fusion.4), channel_id=1, source_target_pairs={{0,1},{1,0},{2,3},{3,2},{4,5},{5,4},{6,7},{7,6},{8,9},{9,8},{10,11... | collective-permute-start | bytes 1572872 | tf_op jit(solution)/shard_map/ppermute | solution.py:83
  70.0 12.6 %collective-permute-start.10 = (f32[256,512]{1,0:T(8,128)S(1)}, f32[256,512]{1,0:T(8,128)S(1)}, u32[]{:S(2)}, u32[]{:S(2)}) collective-permute-start(f32[256,512]{1,0:T(8,128)S(1)} %multiply_add_fusion.4), channel_id=1, source_target_pairs={{1,2},{2,1},{3,4},{4,3},{5,6},{6,5},{7,8},{8,7},{9,10},{10,9},{11,... | collective-permute-start | bytes 1572872 | tf_op jit(solution)/shard_map/ppermute | solution.py:80
  83.3 7.6 %collective-permute-start.11 = (f32[256,512]{1,0:T(8,128)S(1)}, f32[256,512]{1,0:T(8,128)S(1)}, u32[]{:S(2)}, u32[]{:S(2)}) collective-permute-start(f32[256,512]{1,0:T(8,128)S(1)} %get-tuple-element.84), channel_id=1, source_target_pairs={{0,1},{1,0},{2,3},{3,2},{4,5},{5,4},{6,7},{7,6},{8,9},{9,8},{10,11... | collective-permute-start | bytes 1572872 | tf_op jit(solution)/shard_map/ppermute | solution.py:83
  85.3 12.6 %collective-permute-start.12 = (f32[256,512]{1,0:T(8,128)S(1)}, f32[256,512]{1,0:T(8,128)S(1)}, u32[]{:S(2)}, u32[]{:S(2)}) collective-permute-start(f32[256,512]{1,0:T(8,128)S(1)} %get-tuple-element.48), channel_id=1, source_target_pairs={{1,2},{2,1},{3,4},{4,3},{5,6},{6,5},{7,8},{8,7},{9,10},{10,9},{11,... | collective-permute-start | bytes 1572872 | tf_op jit(solution)/shard_map/ppermute | solution.py:80
  98.4 9.6 %collective-permute-start.13 = (f32[256,512]{1,0:T(8,128)S(1)}, f32[256,512]{1,0:T(8,128)S(1)}, u32[]{:S(2)}, u32[]{:S(2)}) collective-permute-start(f32[256,512]{1,0:T(8,128)S(1)} %get-tuple-element.82), channel_id=1, source_target_pairs={{0,1},{1,0},{2,3},{3,2},{4,5},{5,4},{6,7},{7,6},{8,9},{9,8},{10,11... | collective-permute-start | bytes 1572872 | tf_op jit(solution)/shard_map/ppermute | solution.py:83
  100.4 12.6 %collective-permute-start.14 = (f32[256,512]{1,0:T(8,128)S(1)}, f32[256,512]{1,0:T(8,128)S(1)}, u32[]{:S(2)}, u32[]{:S(2)}) collective-permute-start(f32[256,512]{1,0:T(8,128)S(1)} %get-tuple-element.36), channel_id=1, source_target_pairs={{1,2},{2,1},{3,4},{4,3},{5,6},{6,5},{7,8},{8,7},{9,10},{10,9},{11,... | collective-permute-start | bytes 1572872 | tf_op jit(solution)/shard_map/ppermute | solution.py:80
  106.0 12.6 %collective-permute-start.15 = (f32[256,512]{1,0:T(8,128)S(1)}, f32[256,512]{1,0:T(8,128)S(1)}, u32[]{:S(2)}, u32[]{:S(2)}) collective-permute-start(f32[256,512]{1,0:T(8,128)S(1)} %mul.209), channel_id=1, source_target_pairs={{1,2},{2,1},{3,4},{4,3},{5,6},{6,5},{7,8},{8,7},{9,10},{10,9},{11,... | collective-permute-start | bytes 1572872 | tf_op jit(solution)/shard_map/ppermute | solution.py:80
  119.1 7.5 %collective-permute-start.16 = (f32[256,512]{1,0:T(8,128)S(1)}, f32[256,512]{1,0:T(8,128)S(1)}, u32[]{:S(2)}, u32[]{:S(2)}) collective-permute-start(f32[256,512]{1,0:T(8,128)S(1)} %get-tuple-element.80), channel_id=1, source_target_pairs={{0,1},{1,0},{2,3},{3,2},{4,5},{5,4},{6,7},{7,6},{8,9},{9,8},{10,11... | collective-permute-start | bytes 1572872 | tf_op jit(solution)/shard_map/ppermute | solution.py:83
  121.0 12.6 %collective-permute-start.17 = (f32[256,512]{1,0:T(8,128)S(1)}, f32[256,512]{1,0:T(8,128)S(1)}, u32[]{:S(2)}, u32[]{:S(2)}) collective-permute-start(f32[256,512]{1,0:T(8,128)S(1)} %mul.214), channel_id=1, source_target_pairs={{1,2},{2,1},{3,4},{4,3},{5,6},{6,5},{7,8},{8,7},{9,10},{10,9},{11,... | collective-permute-start | bytes 1572872 | tf_op jit(solution)/shard_map/ppermute | solution.py:80
  134.6 12.6 %all-to-all-start = ((f32[4,64,512]{2,1,0:T(8,128)}), f32[4,64,512]{2,1,0:T(8,128)S(1)}, u32[]{:S(2)}, u32[]{:S(2)}) async-start(f32[4,64,512]{2,1,0:T(8,128)} %bitcast.13), calls=%async_computation | async-start | bytes 1048576 | tf_op jit(solution)/shard_map/all_to_all | solution.py:155
  147.3 10.8 %collective-permute-start.18 = (f32[32,512]{1,0:T(8,128)S(1)}, f32[32,512]{1,0:T(8,128)S(1)}, u32[]{:S(2)}, u32[]{:S(2)}) collective-permute-start(f32[32,512]{1,0:T(8,128)S(1)} %get-tuple-element.63), channel_id=1, source_target_pairs={{0,64},{64,0},{128,192},{192,128},{256,320},{320,256},{384,448},{4... | collective-permute-start | bytes 196616 | tf_op jit(solution)/shard_map/ppermute | solution.py:167

commit v7 on v6

--- a/solution.py
+++ b/solution.py
@@ -35,13 +35,13 @@
         )
 
 
-def weight_field(index, weight, rows, columns):
-    count = index.shape[1]
-    chunk = 1024
+def weight_field(index, weight, rows, columns, part, parts):
+    count = index.shape[1] // parts
+    chunk = count // 2
     return pl.pallas_call(
         weight_kernel,
-        grid=(count // chunk,),
-        in_specs=[pl.BlockSpec((1, chunk), lambda i: (0, i))] * 2,
+        grid=(2,),
+        in_specs=[pl.BlockSpec((1, chunk), lambda i: (0, 2 * part + i))] * 2,
         out_specs=pl.BlockSpec((rows, columns), lambda i: (0, 0)),
         out_shape=jax.ShapeDtypeStruct((rows, columns), jnp.float32),
         compiler_params=pltpu.CompilerParams(vmem_limit_bytes=24 << 20),
@@ -107,7 +107,8 @@
 
     gain_pair = far_gain * across(far_gain)
 
-    weights = weight_field(obs_index, obs_weight, rows, columns)
+    weights = weight_field(obs_index, obs_weight, rows, columns, 0, 2)
+    more_weights = weight_field(obs_index, obs_weight, rows, columns, 1, 2)
 
     (inner,) = hold(nears[0] + side_sum(fields[0]))
     laps = [source_gain * (inner + over)]
@@ -133,7 +134,8 @@
         (base,) = hold(base)
         return hold(base + side)[0]
 
-    adjoint, sent = hold(tangent * weights, far_gain * (tangent * weights))
+    adjoint = tangent * (weights + more_weights)
+    adjoint, sent = hold(adjoint, far_gain * adjoint)
     over = across(sent)
     ready = settled(adjoint)
     sent, ready, before = hold(far_gain * ready, ready, adjoint)

time: 159 us -> 160 us (level)
    pallas_call x1 -> x2, Pallas kernels: 4.3 us -> 4.36 us  [weight_field(): pl.pallas_call(weight_kernel, grid=(2,), in_specs=[pl.BlockSpec((1, chunk...]
where the time goes in v7:
time: 160 us; the launch traced here: 159 us
  starting transfers between devices  73.6 us (46%)
  waiting for transfers between devices  68.3 us (43%)
  other arithmetic  9.58 us (6%)
  Pallas kernels  4.36 us (3%)
  local copies, waits for them, and re-layouts  2.4 us (2%)
    ppermute x11, starting transfers between devices, across(): return lax.ppermute(field, 'grid', far)  53.6 us
    ppermute x11, waiting for transfers between devices, across(): return lax.ppermute(field, 'grid', far)  52.3 us
    ppermute x7, starting transfers between devices, beside(): return lax.ppermute(field, 'grid', near)  13.7 us
    all_to_all x1, waiting for transfers between devices, local(): lax.all_to_all(partial_value, 'scen', 0, 0, axis_index_groups=groups, til...  8.2 us
    ppermute x1, waiting for transfers between devices, local(): other = lax.ppermute(other, 'scen', [(s, s ^ 1) for s in range(scens)])  7.82 us
    pallas_call x2, Pallas kernels, weight_field(): pl.pallas_call(weight_kernel, grid=(2,), in_specs=[pl.BlockSpec((1, chunk...  4.36 us
    all_to_all x1, starting transfers between devices, local(): lax.all_to_all(partial_value, 'scen', 0, 0, axis_index_groups=groups, til...  4.28 us
  transfers between devices with their start and end apart: 20, of which 10 were waited for; matrix products, arithmetic and copies ran while one was open for 5% of the time, Pallas kernels for 3%

profile of v7, /device:TPU:40, one launch (start us, length us, event | category | flops | bytes accessed | tf_op | source)
XLA Modules:
  0.0 158.8 jit_solution(3539774274671841625)
XLA Ops:
  0.0 2.2 %collective-permute-start = (f32[4,256,512]{2,1,0:T(8,128)}, f32[4,256,512]{2,1,0:T(8,128)S(1)}, u32[]{:S(2)}, u32[]{:S(2)}) collective-permute-start(f32[4,256,512]{2,1,0:T(8,128)} %bitcast.77), channel_id=1, source_target_pairs={{0,1},{1,0},{2,3},{3,2},{4,5},{5,4},{6,7},{7,6},{8,9},{9,8},{10,11... | collective-permute-start | bytes 6291464 | tf_op jit(solution)/shard_map/ppermute | solution.py:83
  2.2 1.1 slice_bitcast_fusion.7
  3.3 11.8 %collective-permute-start.1 = (f32[256,512]{1,0:T(8,128)S(1)}, f32[256,512]{1,0:T(8,128)S(1)}, u32[]{:S(2)}, u32[]{:S(2)}) collective-permute-start(f32[256,512]{1,0:T(8,128)S(1)} %slice_bitcast_fusion.7), channel_id=1, source_target_pairs={{1,2},{2,1},{3,4},{4,3},{5,6},{6,5},{7,8},{8,7},{9,10},{10,9},{11,... | collective-permute-start | bytes 1572872 | tf_op jit(solution)/shard_map/ppermute | solution.py:80
  15.1 1.1 slice_bitcast_fusion.5
  16.2 1.9 %collective-permute-start.2 = (f32[256,512]{1,0:T(8,128)S(1)}, f32[256,512]{1,0:T(8,128)S(1)}, u32[]{:S(2)}, u32[]{:S(2)}) collective-permute-start(f32[256,512]{1,0:T(8,128)S(1)} %slice_bitcast_fusion.5), channel_id=1, source_target_pairs={{1,2},{2,1},{3,4},{4,3},{5,6},{6,5},{7,8},{8,7},{9,10},{10,9},{11,... | collective-permute-start | bytes 1572872 | tf_op jit(solution)/shard_map/ppermute | solution.py:80
  18.2 0.3 fusion.4
  18.6 3.4 %collective-permute-done.1 = f32[256,512]{1,0:T(8,128)S(1)} collective-permute-done((f32[256,512]{1,0:T(8,128)S(1)}, f32[256,512]{1,0:T(8,128)S(1)}, u32[]{:S(2)}, u32[]{:S(2)}) %collective-permute-start.1) | collective-permute-done | bytes 524320 | tf_op jit(solution)/shard_map/ppermute | solution.py:80
  22.0 0.2 bitcast_multiply_fusion.9
  22.1 1.9 %collective-permute-start.3 = (f32[256,512]{1,0:T(8,128)S(1)}, f32[256,512]{1,0:T(8,128)S(1)}, u32[]{:S(2)}, u32[]{:S(2)}) collective-permute-start(f32[256,512]{1,0:T(8,128)S(1)} %get-tuple-element.38), channel_id=1, source_target_pairs={{0,1},{1,0},{2,3},{3,2},{4,5},{5,4},{6,7},{7,6},{8,9},{9,8},{10,11... | collective-permute-start | bytes 1572872 | tf_op jit(solution)/shard_map/ppermute | solution.py:83
  24.1 5.8 %collective-permute-start.5 = (f32[288,512]{1,0:T(8,128)S(1)}, f32[288,512]{1,0:T(8,128)S(1)}, u32[]{:S(2)}, u32[]{:S(2)}) collective-permute-start(f32[288,512]{1,0:T(8,128)S(1)} %pad_maximum_fusion), channel_id=1, source_target_pairs={{1,2},{2,1},{3,4},{4,3},{5,6},{6,5},{7,8},{8,7},{9,10},{10,9},{11,... | collective-permute-start | bytes 1769480 | tf_op jit(solution)/shard_map/ppermute | solution.py:80
  29.9 1.9 %collective-permute-start.4 = (f32[256,512]{1,0:T(8,128)S(1)}, f32[256,512]{1,0:T(8,128)S(1)}, u32[]{:S(2)}, u32[]{:S(2)}) collective-permute-start(f32[256,512]{1,0:T(8,128)S(1)} %get-tuple-element.38), channel_id=1, source_target_pairs={{1,2},{2,1},{3,4},{4,3},{5,6},{6,5},{7,8},{8,7},{9,10},{10,9},{11,... | collective-permute-start | bytes 1572872 | tf_op jit(solution)/shard_map/ppermute | solution.py:80
  31.8 0.9 fusion.12
  32.8 0.1 multiply_add_fusion.6
  32.9 10.1 %collective-permute-done.4 = f32[256,512]{1,0:T(8,128)S(1)} collective-permute-done((f32[256,512]{1,0:T(8,128)S(1)}, f32[256,512]{1,0:T(8,128)S(1)}, u32[]{:S(2)}, u32[]{:S(2)}) %collective-permute-start.4) | collective-permute-done | bytes 524320 | tf_op jit(solution)/shard_map/ppermute | solution.py:80
  43.1 0.1 multiply_add_fusion.5
  43.3 1.9 %collective-permute-start.6 = (f32[288,512]{1,0:T(8,128)S(1)}, f32[288,512]{1,0:T(8,128)S(1)}, u32[]{:S(2)}, u32[]{:S(2)}) collective-permute-start(f32[288,512]{1,0:T(8,128)S(1)} %pad_maximum_fusion.1), channel_id=1, source_target_pairs={{0,1},{1,0},{2,3},{3,2},{4,5},{5,4},{6,7},{7,6},{8,9},{9,8},{10,11... | collective-permute-start | bytes 1769480 | tf_op jit(solution)/shard_map/ppermute | solution.py:83
  45.2 5.8 %collective-permute-start.8 = (f32[256,512]{1,0:T(8,128)S(1)}, f32[256,512]{1,0:T(8,128)S(1)}, u32[]{:S(2)}, u32[]{:S(2)}) collective-permute-start(f32[256,512]{1,0:T(8,128)S(1)} %slice_bitcast_fusion.1), channel_id=1, source_target_pairs={{1,2},{2,1},{3,4},{4,3},{5,6},{6,5},{7,8},{8,7},{9,10},{10,9},{11,... | collective-permute-start | bytes 1572872 | tf_op jit(solution)/shard_map/ppermute | solution.py:80
  51.0 1.9 %collective-permute-start.7 = (f32[256,512]{1,0:T(8,128)S(1)}, f32[256,512]{1,0:T(8,128)S(1)}, u32[]{:S(2)}, u32[]{:S(2)}) collective-permute-start(f32[256,512]{1,0:T(8,128)S(1)} %multiply_add_fusion.5), channel_id=1, source_target_pairs={{1,2},{2,1},{3,4},{4,3},{5,6},{6,5},{7,8},{8,7},{9,10},{10,9},{11,... | collective-permute-start | bytes 1572872 | tf_op jit(solution)/shard_map/ppermute | solution.py:80
  52.9 0.8 fusion.26
  53.8 0.2 fusion.66
  53.9 9.7 %collective-permute-done.7 = f32[256,512]{1,0:T(8,128)S(1)} collective-permute-done((f32[256,512]{1,0:T(8,128)S(1)}, f32[256,512]{1,0:T(8,128)S(1)}, u32[]{:S(2)}, u32[]{:S(2)}) %collective-permute-start.7) | collective-permute-done | bytes 524320 | tf_op jit(solution)/shard_map/ppermute | solution.py:80
  63.6 0.2 multiply_add_fusion.4
  63.8 1.9 %collective-permute-start.9 = (f32[256,512]{1,0:T(8,128)S(1)}, f32[256,512]{1,0:T(8,128)S(1)}, u32[]{:S(2)}, u32[]{:S(2)}) collective-permute-start(f32[256,512]{1,0:T(8,128)S(1)} %multiply_add_fusion.4), channel_id=1, source_target_pairs={{0,1},{1,0},{2,3},{3,2},{4,5},{5,4},{6,7},{7,6},{8,9},{9,8},{10,11... | collective-permute-start | bytes 1572872 | tf_op jit(solution)/shard_map/ppermute | solution.py:83
  65.7 2.2 %weight_field.2 = f32[256,512]{1,0:T(8,128)S(1)} custom-call(s32[1,4096]{1,0:T(1,128)S(1)} %copy-done, f32[1,4096]{1,0:T(1,128)S(1)} %copy-done.1), custom_call_target="tpu_custom_call" | custom-call | flops 1610612736 | bytes 524288 | tf_op jit(solution)/shard_map/weight_field/pallas_call | solution.py:41
  67.9 2.2 %weight_field.3 = f32[256,512]{1,0:T(8,128)S(1)} custom-call(s32[1,4096]{1,0:T(1,128)S(1)} %copy-done, f32[1,4096]{1,0:T(1,128)S(1)} %copy-done.1), custom_call_target="tpu_custom_call" | custom-call | flops 1610612736 | bytes 524288 | tf_op jit(solution)/shard_map/weight_field/pallas_call | solution.py:41
  70.1 5.6 %collective-permute-start.10 = (f32[256,512]{1,0:T(8,128)S(1)}, f32[256,512]{1,0:T(8,128)S(1)}, u32[]{:S(2)}, u32[]{:S(2)}) collective-permute-start(f32[256,512]{1,0:T(8,128)S(1)} %multiply_add_fusion.4), channel_id=1, source_target_pairs={{1,2},{2,1},{3,4},{4,3},{5,6},{6,5},{7,8},{8,7},{9,10},{10,9},{11,... | collective-permute-start | bytes 1572872 | tf_op jit(solution)/shard_map/ppermute | solution.py:80
  75.7 0.8 fusion.40
  76.6 0.2 multiply_add_fusion.3
  76.7 6.0 %collective-permute-done.10 = f32[256,512]{1,0:T(8,128)S(1)} collective-permute-done((f32[256,512]{1,0:T(8,128)S(1)}, f32[256,512]{1,0:T(8,128)S(1)}, u32[]{:S(2)}, u32[]{:S(2)}) %collective-permute-start.10) | collective-permute-done | bytes 524320 | tf_op jit(solution)/shard_map/ppermute | solution.py:80
  82.7 0.3 fusion.75
  83.0 0.1 bitcast_multiply_fusion.7
  83.1 0.4 fusion.81
  83.5 1.9 %collective-permute-start.11 = (f32[256,512]{1,0:T(8,128)S(1)}, f32[256,512]{1,0:T(8,128)S(1)}, u32[]{:S(2)}, u32[]{:S(2)}) collective-permute-start(f32[256,512]{1,0:T(8,128)S(1)} %get-tuple-element.84), channel_id=1, source_target_pairs={{0,1},{1,0},{2,3},{3,2},{4,5},{5,4},{6,7},{7,6},{8,9},{9,8},{10,11... | collective-permute-start | bytes 1572872 | tf_op jit(solution)/shard_map/ppermute | solution.py:83
  85.4 5.6 %collective-permute-start.12 = (f32[256,512]{1,0:T(8,128)S(1)}, f32[256,512]{1,0:T(8,128)S(1)}, u32[]{:S(2)}, u32[]{:S(2)}) collective-permute-start(f32[256,512]{1,0:T(8,128)S(1)} %get-tuple-element.48), channel_id=1, source_target_pairs={{1,2},{2,1},{3,4},{4,3},{5,6},{6,5},{7,8},{8,7},{9,10},{10,9},{11,... | collective-permute-start | bytes 1572872 | tf_op jit(solution)/shard_map/ppermute | solution.py:80
  91.0 0.1 add.291
  91.1 0.1 mul.208
  91.2 6.8 %collective-permute-done.12 = f32[256,512]{1,0:T(8,128)S(1)} collective-permute-done((f32[256,512]{1,0:T(8,128)S(1)}, f32[256,512]{1,0:T(8,128)S(1)}, u32[]{:S(2)}, u32[]{:S(2)}) %collective-permute-start.12) | collective-permute-done | bytes 524320 | tf_op jit(solution)/shard_map/ppermute | solution.py:80
  98.0 0.1 add.292
  98.1 0.1 bitcast_multiply_fusion.6
  98.2 0.4 fusion.80
  98.6 1.9 %collective-permute-start.13 = (f32[256,512]{1,0:T(8,128)S(1)}, f32[256,512]{1,0:T(8,128)S(1)}, u32[]{:S(2)}, u32[]{:S(2)}) collective-permute-start(f32[256,512]{1,0:T(8,128)S(1)} %get-tuple-element.82), channel_id=1, source_target_pairs={{0,1},{1,0},{2,3},{3,2},{4,5},{5,4},{6,7},{7,6},{8,9},{9,8},{10,11... | collective-permute-start | bytes 1572872 | tf_op jit(solution)/shard_map/ppermute | solution.py:83
  100.5 5.6 %collective-permute-start.14 = (f32[256,512]{1,0:T(8,128)S(1)}, f32[256,512]{1,0:T(8,128)S(1)}, u32[]{:S(2)}, u32[]{:S(2)}) collective-permute-start(f32[256,512]{1,0:T(8,128)S(1)} %get-tuple-element.36), channel_id=1, source_target_pairs={{1,2},{2,1},{3,4},{4,3},{5,6},{6,5},{7,8},{8,7},{9,10},{10,9},{11,... | collective-permute-start | bytes 1572872 | tf_op jit(solution)/shard_map/ppermute | solution.py:80
  106.1 2.1 %collective-permute-start.15 = (f32[256,512]{1,0:T(8,128)S(1)}, f32[256,512]{1,0:T(8,128)S(1)}, u32[]{:S(2)}, u32[]{:S(2)}) collective-permute-start(f32[256,512]{1,0:T(8,128)S(1)} %mul.208), channel_id=1, source_target_pairs={{1,2},{2,1},{3,4},{4,3},{5,6},{6,5},{7,8},{8,7},{9,10},{10,9},{11,... | collective-permute-start | bytes 1572872 | tf_op jit(solution)/shard_map/ppermute | solution.py:80
  108.2 0.1 add.297
  108.3 0.1 mul.213
  108.4 4.7 %collective-permute-done.14 = f32[256,512]{1,0:T(8,128)S(1)} collective-permute-done((f32[256,512]{1,0:T(8,128)S(1)}, f32[256,512]{1,0:T(8,128)S(1)}, u32[]{:S(2)}, u32[]{:S(2)}) %collective-permute-start.14) | collective-permute-done | bytes 524320 | tf_op jit(solution)/shard_map/ppermute | solution.py:80
  113.1 0.3 multiply_multiply_fusion
  113.4 0.1 add.298
  113.5 0.2 multiply_add_fusion.2
  113.7 5.1 %collective-permute-done.15 = f32[256,512]{1,0:T(8,128)S(1)} collective-permute-done((f32[256,512]{1,0:T(8,128)S(1)}, f32[256,512]{1,0:T(8,128)S(1)}, u32[]{:S(2)}, u32[]{:S(2)}) %collective-permute-start.15) | collective-permute-done | bytes 524320 | tf_op jit(solution)/shard_map/ppermute | solution.py:80
  118.7 0.1 add.300
  118.9 0.3 fusion.79
  119.2 1.9 %collective-permute-start.16 = (f32[256,512]{1,0:T(8,128)S(1)}, f32[256,512]{1,0:T(8,128)S(1)}, u32[]{:S(2)}, u32[]{:S(2)}) collective-permute-start(f32[256,512]{1,0:T(8,128)S(1)} %get-tuple-element.80), channel_id=1, source_target_pairs={{0,1},{1,0},{2,3},{3,2},{4,5},{5,4},{6,7},{7,6},{8,9},{9,8},{10,11... | collective-permute-start | bytes 1572872 | tf_op jit(solution)/shard_map/ppermute | solution.py:83
  121.2 5.6 %collective-permute-start.17 = (f32[256,512]{1,0:T(8,128)S(1)}, f32[256,512]{1,0:T(8,128)S(1)}, u32[]{:S(2)}, u32[]{:S(2)}) collective-permute-start(f32[256,512]{1,0:T(8,128)S(1)} %mul.213), channel_id=1, source_target_pairs={{1,2},{2,1},{3,4},{4,3},{5,6},{6,5},{7,8},{8,7},{9,10},{10,9},{11,... | collective-permute-start | bytes 1572872 | tf_op jit(solution)/shard_map/ppermute | solution.py:80
  126.9 0.4 multiply_add_fusion.1
  127.3 6.5 %collective-permute-done.17 = f32[256,512]{1,0:T(8,128)S(1)} collective-permute-done((f32[256,512]{1,0:T(8,128)S(1)}, f32[256,512]{1,0:T(8,128)S(1)}, u32[]{:S(2)}, u32[]{:S(2)}) %collective-permute-start.17) | collective-permute-done | bytes 524320 | tf_op jit(solution)/shard_map/ppermute | solution.py:80
  133.8 1.0 multiply_add_fusion
  134.8 4.3 %all-to-all-start = ((f32[4,64,512]{2,1,0:T(8,128)}), f32[4,64,512]{2,1,0:T(8,128)S(1)}, u32[]{:S(2)}, u32[]{:S(2)}) async-start(f32[4,64,512]{2,1,0:T(8,128)} %bitcast.13), calls=%async_computation | async-start | bytes 1048576 | tf_op jit(solution)/shard_map/all_to_all | solution.py:157
  139.1 0.1 pad_slice_fusion.43
  139.2 8.2 %all-to-all-done = f32[4,64,512]{2,1,0:T(8,128)S(1)} async-done(((f32[4,64,512]{2,1,0:T(8,128)}), f32[4,64,512]{2,1,0:T(8,128)S(1)}, u32[]{:S(2)}, u32[]{:S(2)}) %all-to-all-start) | async-done | bytes 524320 | tf_op jit(solution)/shard_map/all_to_all | solution.py:157
  147.4 2.0 %collective-permute-start.18 = (f32[32,512]{1,0:T(8,128)S(1)}, f32[32,512]{1,0:T(8,128)S(1)}, u32[]{:S(2)}, u32[]{:S(2)}) collective-permute-start(f32[32,512]{1,0:T(8,128)S(1)} %get-tuple-element.63), channel_id=1, source_target_pairs={{0,64},{64,0},{128,192},{192,128},{256,320},{320,256},{384,448},{4... | collective-permute-start | bytes 196616 | tf_op jit(solution)/shard_map/ppermute | solution.py:169
  149.4 0.9 fusion.74
  150.4 7.8 %collective-permute-done.18 = f32[32,512]{1,0:T(8,128)S(1)} collective-permute-done((f32[32,512]{1,0:T(8,128)S(1)}, f32[32,512]{1,0:T(8,128)S(1)}, u32[]{:S(2)}, u32[]{:S(2)}) %collective-permute-start.18) | collective-permute-done | bytes 65568 | tf_op jit(solution)/shard_map/ppermute | solution.py:169
  158.2 0.6 add_bitcast_fusion
  (34 shorter events, 0.5 us)
Async XLA Ops:
  0.0 18.1 %copy-start.5 = (f32[1,4,1,256,512]{4,3,2,1,0:T(8,128)S(1)}, f32[1,4,1,256,512]{4,3,2,1,0:T(8,128)}, u32[]{:S(2)}) copy-start(f32[1,4,1,256,512]{4,3,2,1,0:T(8,128)} %param.6) | copy-start | bytes 6291460
  0.0 22.0 %copy-start.2 = (f32[1,256,512]{2,1,0:T(8,128)S(1)}, f32[1,256,512]{2,1,0:T(8,128)}, u32[]{:S(2)}) copy-start(f32[1,256,512]{2,1,0:T(8,128)} %param.9) | copy-start | bytes 1572868
  0.0 18.2 %collective-permute-start = (f32[4,256,512]{2,1,0:T(8,128)}, f32[4,256,512]{2,1,0:T(8,128)S(1)}, u32[]{:S(2)}, u32[]{:S(2)}) collective-permute-start(f32[4,256,512]{2,1,0:T(8,128)} %bitcast.77), channel_id=1, source_target_pairs={{0,1},{1,0},{2,3},{3,2},{4,5},{5,4},{6,7},{7,6},{8,9},{9,8},{10,11... | collective-permute-start | bytes 6291464 | tf_op jit(solution)/shard_map/ppermute | solution.py:83
  3.3 18.7 %collective-permute-start.1 = (f32[256,512]{1,0:T(8,128)S(1)}, f32[256,512]{1,0:T(8,128)S(1)}, u32[]{:S(2)}, u32[]{:S(2)}) collective-permute-start(f32[256,512]{1,0:T(8,128)S(1)} %slice_bitcast_fusion.7), channel_id=1, source_target_pairs={{1,2},{2,1},{3,4},{4,3},{5,6},{6,5},{7,8},{8,7},{9,10},{10,9},{11,... | collective-permute-start | bytes 1572872 | tf_op jit(solution)/shard_map/ppermute | solution.py:80
  16.2 15.6 %collective-permute-start.2 = (f32[256,512]{1,0:T(8,128)S(1)}, f32[256,512]{1,0:T(8,128)S(1)}, u32[]{:S(2)}, u32[]{:S(2)}) collective-permute-start(f32[256,512]{1,0:T(8,128)S(1)} %slice_bitcast_fusion.5), channel_id=1, source_target_pairs={{1,2},{2,1},{3,4},{4,3},{5,6},{6,5},{7,8},{8,7},{9,10},{10,9},{11,... | collective-permute-start | bytes 1572872 | tf_op jit(solution)/shard_map/ppermute | solution.py:80
  18.5 13.3 %copy-start.3 = (f32[1,256,512]{2,1,0:T(8,128)S(1)}, f32[1,256,512]{2,1,0:T(8,128)}, u32[]{:S(2)}) copy-start(f32[1,256,512]{2,1,0:T(8,128)} %param.7) | copy-start | bytes 1572868
  18.5 13.3 %copy-start.4 = (f32[1,256,512]{2,1,0:T(8,128)S(1)}, f32[1,256,512]{2,1,0:T(8,128)}, u32[]{:S(2)}) copy-start(f32[1,256,512]{2,1,0:T(8,128)} %param.8) | copy-start | bytes 1572868
  22.1 10.7 %collective-permute-start.3 = (f32[256,512]{1,0:T(8,128)S(1)}, f32[256,512]{1,0:T(8,128)S(1)}, u32[]{:S(2)}, u32[]{:S(2)}) collective-permute-start(f32[256,512]{1,0:T(8,128)S(1)} %get-tuple-element.38), channel_id=1, source_target_pairs={{0,1},{1,0},{2,3},{3,2},{4,5},{5,4},{6,7},{7,6},{8,9},{9,8},{10,11... | collective-permute-start | bytes 1572872 | tf_op jit(solution)/shard_map/ppermute | solution.py:83
  24.1 28.8 %collective-permute-start.5 = (f32[288,512]{1,0:T(8,128)S(1)}, f32[288,512]{1,0:T(8,128)S(1)}, u32[]{:S(2)}, u32[]{:S(2)}) collective-permute-start(f32[288,512]{1,0:T(8,128)S(1)} %pad_maximum_fusion), channel_id=1, source_target_pairs={{1,2},{2,1},{3,4},{4,3},{5,6},{6,5},{7,8},{8,7},{9,10},{10,9},{11,... | collective-permute-start | bytes 1769480 | tf_op jit(solution)/shard_map/ppermute | solution.py:80
  29.9 13.2 %collective-permute-start.4 = (f32[256,512]{1,0:T(8,128)S(1)}, f32[256,512]{1,0:T(8,128)S(1)}, u32[]{:S(2)}, u32[]{:S(2)}) collective-permute-start(f32[256,512]{1,0:T(8,128)S(1)} %get-tuple-element.38), channel_id=1, source_target_pairs={{1,2},{2,1},{3,4},{4,3},{5,6},{6,5},{7,8},{8,7},{9,10},{10,9},{11,... | collective-permute-start | bytes 1572872 | tf_op jit(solution)/shard_map/ppermute | solution.py:80
  43.3 10.5 %collective-permute-start.6 = (f32[288,512]{1,0:T(8,128)S(1)}, f32[288,512]{1,0:T(8,128)S(1)}, u32[]{:S(2)}, u32[]{:S(2)}) collective-permute-start(f32[288,512]{1,0:T(8,128)S(1)} %pad_maximum_fusion.1), channel_id=1, source_target_pairs={{0,1},{1,0},{2,3},{3,2},{4,5},{5,4},{6,7},{7,6},{8,9},{9,8},{10,11... | collective-permute-start | bytes 1769480 | tf_op jit(solution)/shard_map/ppermute | solution.py:83
  45.2 30.5 %collective-permute-start.8 = (f32[256,512]{1,0:T(8,128)S(1)}, f32[256,512]{1,0:T(8,128)S(1)}, u32[]{:S(2)}, u32[]{:S(2)}) collective-permute-start(f32[256,512]{1,0:T(8,128)S(1)} %slice_bitcast_fusion.1), channel_id=1, source_target_pairs={{1,2},{2,1},{3,4},{4,3},{5,6},{6,5},{7,8},{8,7},{9,10},{10,9},{11,... | collective-permute-start | bytes 1572872 | tf_op jit(solution)/shard_map/ppermute | solution.py:80
  51.0 12.6 %collective-permute-start.7 = (f32[256,512]{1,0:T(8,128)S(1)}, f32[256,512]{1,0:T(8,128)S(1)}, u32[]{:S(2)}, u32[]{:S(2)}) collective-permute-start(f32[256,512]{1,0:T(8,128)S(1)} %multiply_add_fusion.5), channel_id=1, source_target_pairs={{1,2},{2,1},{3,4},{4,3},{5,6},{6,5},{7,8},{8,7},{9,10},{10,9},{11,... | collective-permute-start | bytes 1572872 | tf_op jit(solution)/shard_map/ppermute | solution.py:80
  53.7 10.0 %copy-start.6 = (f32[288,512]{1,0:T(8,128)}, f32[288,512]{1,0:T(8,128)S(1)}, u32[]{:S(2)}) copy-start(f32[288,512]{1,0:T(8,128)S(1)} %collective-permute-done.6) | copy-start | bytes 1769476
  53.7 12.0 %copy-start = (s32[1,4096]{1,0:T(1,128)S(1)}, s32[1,4096]{1,0:T(1,128)}, u32[]{:S(2)}) copy-start(s32[1,4096]{1,0:T(1,128)} %index_ref.3) | copy-start | bytes 49156
  53.8 12.0 %copy-start.1 = (f32[1,4096]{1,0:T(1,128)S(1)}, f32[1,4096]{1,0:T(1,128)}, u32[]{:S(2)}) copy-start(f32[1,4096]{1,0:T(1,128)} %weight_ref.3) | copy-start | bytes 49156
  63.8 12.8 %collective-permute-start.9 = (f32[256,512]{1,0:T(8,128)S(1)}, f32[256,512]{1,0:T(8,128)S(1)}, u32[]{:S(2)}, u32[]{:S(2)}) collective-permute-start(f32[256,512]{1,0:T(8,128)S(1)} %multiply_add_fusion.4), channel_id=1, source_target_pairs={{0,1},{1,0},{2,3},{3,2},{4,5},{5,4},{6,7},{7,6},{8,9},{9,8},{10,11... | collective-permute-start | bytes 1572872 | tf_op jit(solution)/shard_map/ppermute | solution.py:83
  70.1 12.6 %collective-permute-start.10 = (f32[256,512]{1,0:T(8,128)S(1)}, f32[256,512]{1,0:T(8,128)S(1)}, u32[]{:S(2)}, u32[]{:S(2)}) collective-permute-start(f32[256,512]{1,0:T(8,128)S(1)} %multiply_add_fusion.4), channel_id=1, source_target_pairs={{1,2},{2,1},{3,4},{4,3},{5,6},{6,5},{7,8},{8,7},{9,10},{10,9},{11,... | collective-permute-start | bytes 1572872 | tf_op jit(solution)/shard_map/ppermute | solution.py:80
  83.5 7.6 %collective-permute-start.11 = (f32[256,512]{1,0:T(8,128)S(1)}, f32[256,512]{1,0:T(8,128)S(1)}, u32[]{:S(2)}, u32[]{:S(2)}) collective-permute-start(f32[256,512]{1,0:T(8,128)S(1)} %get-tuple-element.84), channel_id=1, source_target_pairs={{0,1},{1,0},{2,3},{3,2},{4,5},{5,4},{6,7},{7,6},{8,9},{9,8},{10,11... | collective-permute-start | bytes 1572872 | tf_op jit(solution)/shard_map/ppermute | solution.py:83
  85.4 12.6 %collective-permute-start.12 = (f32[256,512]{1,0:T(8,128)S(1)}, f32[256,512]{1,0:T(8,128)S(1)}, u32[]{:S(2)}, u32[]{:S(2)}) collective-permute-start(f32[256,512]{1,0:T(8,128)S(1)} %get-tuple-element.48), channel_id=1, source_target_pairs={{1,2},{2,1},{3,4},{4,3},{5,6},{6,5},{7,8},{8,7},{9,10},{10,9},{11,... | collective-permute-start | bytes 1572872 | tf_op jit(solution)/shard_map/ppermute | solution.py:80
  98.6 9.6 %collective-permute-start.13 = (f32[256,512]{1,0:T(8,128)S(1)}, f32[256,512]{1,0:T(8,128)S(1)}, u32[]{:S(2)}, u32[]{:S(2)}) collective-permute-start(f32[256,512]{1,0:T(8,128)S(1)} %get-tuple-element.82), channel_id=1, source_target_pairs={{0,1},{1,0},{2,3},{3,2},{4,5},{5,4},{6,7},{7,6},{8,9},{9,8},{10,11... | collective-permute-start | bytes 1572872 | tf_op jit(solution)/shard_map/ppermute | solution.py:83
  100.5 12.6 %collective-permute-start.14 = (f32[256,512]{1,0:T(8,128)S(1)}, f32[256,512]{1,0:T(8,128)S(1)}, u32[]{:S(2)}, u32[]{:S(2)}) collective-permute-start(f32[256,512]{1,0:T(8,128)S(1)} %get-tuple-element.36), channel_id=1, source_target_pairs={{1,2},{2,1},{3,4},{4,3},{5,6},{6,5},{7,8},{8,7},{9,10},{10,9},{11,... | collective-permute-start | bytes 1572872 | tf_op jit(solution)/shard_map/ppermute | solution.py:80
  106.1 12.6 %collective-permute-start.15 = (f32[256,512]{1,0:T(8,128)S(1)}, f32[256,512]{1,0:T(8,128)S(1)}, u32[]{:S(2)}, u32[]{:S(2)}) collective-permute-start(f32[256,512]{1,0:T(8,128)S(1)} %mul.208), channel_id=1, source_target_pairs={{1,2},{2,1},{3,4},{4,3},{5,6},{6,5},{7,8},{8,7},{9,10},{10,9},{11,... | collective-permute-start | bytes 1572872 | tf_op jit(solution)/shard_map/ppermute | solution.py:80
  119.2 7.5 %collective-permute-start.16 = (f32[256,512]{1,0:T(8,128)S(1)}, f32[256,512]{1,0:T(8,128)S(1)}, u32[]{:S(2)}, u32[]{:S(2)}) collective-permute-start(f32[256,512]{1,0:T(8,128)S(1)} %get-tuple-element.80), channel_id=1, source_target_pairs={{0,1},{1,0},{2,3},{3,2},{4,5},{5,4},{6,7},{7,6},{8,9},{9,8},{10,11... | collective-permute-start | bytes 1572872 | tf_op jit(solution)/shard_map/ppermute | solution.py:83
  121.2 12.6 %collective-permute-start.17 = (f32[256,512]{1,0:T(8,128)S(1)}, f32[256,512]{1,0:T(8,128)S(1)}, u32[]{:S(2)}, u32[]{:S(2)}) collective-permute-start(f32[256,512]{1,0:T(8,128)S(1)} %mul.213), channel_id=1, source_target_pairs={{1,2},{2,1},{3,4},{4,3},{5,6},{6,5},{7,8},{8,7},{9,10},{10,9},{11,... | collective-permute-start | bytes 1572872 | tf_op jit(solution)/shard_map/ppermute | solution.py:80
  134.8 12.6 %all-to-all-start = ((f32[4,64,512]{2,1,0:T(8,128)}), f32[4,64,512]{2,1,0:T(8,128)S(1)}, u32[]{:S(2)}, u32[]{:S(2)}) async-start(f32[4,64,512]{2,1,0:T(8,128)} %bitcast.13), calls=%async_computation | async-start | bytes 1048576 | tf_op jit(solution)/shard_map/all_to_all | solution.py:157
  147.4 10.8 %collective-permute-start.18 = (f32[32,512]{1,0:T(8,128)S(1)}, f32[32,512]{1,0:T(8,128)S(1)}, u32[]{:S(2)}, u32[]{:S(2)}) collective-permute-start(f32[32,512]{1,0:T(8,128)S(1)} %get-tuple-element.63), channel_id=1, source_target_pairs={{0,64},{64,0},{128,192},{192,128},{256,320},{320,256},{384,448},{4... | collective-permute-start | bytes 196616 | tf_op jit(solution)/shard_map/ppermute | solution.py:169

commit v8 on v7

--- a/solution.py
+++ b/solution.py
@@ -129,10 +129,10 @@
         tangent = base + far_gain * over
 
     def settled(field):
-        side = beside(near_gain * field)
+        weighted = near_gain * field
         base = field + side_sum(kappa * field) - courant * field
-        (base,) = hold(base)
-        return hold(base + side)[0]
+        weighted, base = hold(weighted, base)
+        return hold(base + beside(weighted))[0]
 
     adjoint = tangent * (weights + more_weights)
     adjoint, sent = hold(adjoint, far_gain * adjoint)

time: 160 us -> 160 us (level)
  no operation moved by 1% of the time
where the time goes in v8:
time: 160 us; the launch traced here: 159 us
  starting transfers between devices  73.6 us (46%)
  waiting for transfers between devices  68.3 us (43%)
  other arithmetic  9.57 us (6%)
  Pallas kernels  4.36 us (3%)
  local copies, waits for them, and re-layouts  2.4 us (2%)
    ppermute x11, starting transfers between devices, across(): return lax.ppermute(field, 'grid', far)  53.6 us
    ppermute x11, waiting for transfers between devices, across(): return lax.ppermute(field, 'grid', far)  52.3 us
    ppermute x7, starting transfers between devices, beside(): return lax.ppermute(field, 'grid', near)  13.7 us
    all_to_all x1, waiting for transfers between devices, local(): lax.all_to_all(partial_value, 'scen', 0, 0, axis_index_groups=groups, til...  8.2 us
    ppermute x1, waiting for transfers between devices, local(): other = lax.ppermute(other, 'scen', [(s, s ^ 1) for s in range(scens)])  7.82 us
    pallas_call x2, Pallas kernels, weight_field(): pl.pallas_call(weight_kernel, grid=(2,), in_specs=[pl.BlockSpec((1, chunk...  4.36 us
    all_to_all x1, starting transfers between devices, local(): lax.all_to_all(partial_value, 'scen', 0, 0, axis_index_groups=groups, til...  4.28 us
  transfers between devices with their start and end apart: 20, of which 10 were waited for; matrix products, arithmetic and copies ran while one was open for 5% of the time, Pallas kernels for 3%

profile of v8, /device:TPU:40, one launch (start us, length us, event | category | flops | bytes accessed | tf_op | source)
XLA Modules:
  0.0 158.8 jit_solution(15037311055307790844)
XLA Ops:
  0.0 2.2 %collective-permute-start = (f32[4,256,512]{2,1,0:T(8,128)}, f32[4,256,512]{2,1,0:T(8,128)S(1)}, u32[]{:S(2)}, u32[]{:S(2)}) collective-permute-start(f32[4,256,512]{2,1,0:T(8,128)} %bitcast.77), channel_id=1, source_target_pairs={{0,1},{1,0},{2,3},{3,2},{4,5},{5,4},{6,7},{7,6},{8,9},{9,8},{10,11... | collective-permute-start | bytes 6291464 | tf_op jit(solution)/shard_map/ppermute | solution.py:83
  2.2 1.1 slice_bitcast_fusion.7
  3.3 11.8 %collective-permute-start.1 = (f32[256,512]{1,0:T(8,128)S(1)}, f32[256,512]{1,0:T(8,128)S(1)}, u32[]{:S(2)}, u32[]{:S(2)}) collective-permute-start(f32[256,512]{1,0:T(8,128)S(1)} %slice_bitcast_fusion.7), channel_id=1, source_target_pairs={{1,2},{2,1},{3,4},{4,3},{5,6},{6,5},{7,8},{8,7},{9,10},{10,9},{11,... | collective-permute-start | bytes 1572872 | tf_op jit(solution)/shard_map/ppermute | solution.py:80
  15.1 1.1 slice_bitcast_fusion.5
  16.2 1.9 %collective-permute-start.2 = (f32[256,512]{1,0:T(8,128)S(1)}, f32[256,512]{1,0:T(8,128)S(1)}, u32[]{:S(2)}, u32[]{:S(2)}) collective-permute-start(f32[256,512]{1,0:T(8,128)S(1)} %slice_bitcast_fusion.5), channel_id=1, source_target_pairs={{1,2},{2,1},{3,4},{4,3},{5,6},{6,5},{7,8},{8,7},{9,10},{10,9},{11,... | collective-permute-start | bytes 1572872 | tf_op jit(solution)/shard_map/ppermute | solution.py:80
  18.2 0.3 fusion.4
  18.6 3.4 %collective-permute-done.1 = f32[256,512]{1,0:T(8,128)S(1)} collective-permute-done((f32[256,512]{1,0:T(8,128)S(1)}, f32[256,512]{1,0:T(8,128)S(1)}, u32[]{:S(2)}, u32[]{:S(2)}) %collective-permute-start.1) | collective-permute-done | bytes 524320 | tf_op jit(solution)/shard_map/ppermute | solution.py:80
  22.0 0.2 bitcast_multiply_fusion.9
  22.1 1.9 %collective-permute-start.3 = (f32[256,512]{1,0:T(8,128)S(1)}, f32[256,512]{1,0:T(8,128)S(1)}, u32[]{:S(2)}, u32[]{:S(2)}) collective-permute-start(f32[256,512]{1,0:T(8,128)S(1)} %get-tuple-element.45), channel_id=1, source_target_pairs={{0,1},{1,0},{2,3},{3,2},{4,5},{5,4},{6,7},{7,6},{8,9},{9,8},{10,11... | collective-permute-start | bytes 1572872 | tf_op jit(solution)/shard_map/ppermute | solution.py:83
  24.1 5.8 %collective-permute-start.5 = (f32[288,512]{1,0:T(8,128)S(1)}, f32[288,512]{1,0:T(8,128)S(1)}, u32[]{:S(2)}, u32[]{:S(2)}) collective-permute-start(f32[288,512]{1,0:T(8,128)S(1)} %pad_maximum_fusion), channel_id=1, source_target_pairs={{1,2},{2,1},{3,4},{4,3},{5,6},{6,5},{7,8},{8,7},{9,10},{10,9},{11,... | collective-permute-start | bytes 1769480 | tf_op jit(solution)/shard_map/ppermute | solution.py:80
  29.9 1.9 %collective-permute-start.4 = (f32[256,512]{1,0:T(8,128)S(1)}, f32[256,512]{1,0:T(8,128)S(1)}, u32[]{:S(2)}, u32[]{:S(2)}) collective-permute-start(f32[256,512]{1,0:T(8,128)S(1)} %get-tuple-element.45), channel_id=1, source_target_pairs={{1,2},{2,1},{3,4},{4,3},{5,6},{6,5},{7,8},{8,7},{9,10},{10,9},{11,... | collective-permute-start | bytes 1572872 | tf_op jit(solution)/shard_map/ppermute | solution.py:80
  31.8 0.9 fusion.12
  32.8 0.1 multiply_add_fusion.6
  32.9 10.1 %collective-permute-done.4 = f32[256,512]{1,0:T(8,128)S(1)} collective-permute-done((f32[256,512]{1,0:T(8,128)S(1)}, f32[256,512]{1,0:T(8,128)S(1)}, u32[]{:S(2)}, u32[]{:S(2)}) %collective-permute-start.4) | collective-permute-done | bytes 524320 | tf_op jit(solution)/shard_map/ppermute | solution.py:80
  43.1 0.1 multiply_add_fusion.5
  43.3 1.9 %collective-permute-start.6 = (f32[288,512]{1,0:T(8,128)S(1)}, f32[288,512]{1,0:T(8,128)S(1)}, u32[]{:S(2)}, u32[]{:S(2)}) collective-permute-start(f32[288,512]{1,0:T(8,128)S(1)} %pad_maximum_fusion.1), channel_id=1, source_target_pairs={{0,1},{1,0},{2,3},{3,2},{4,5},{5,4},{6,7},{7,6},{8,9},{9,8},{10,11... | collective-permute-start | bytes 1769480 | tf_op jit(solution)/shard_map/ppermute | solution.py:83
  45.2 5.8 %collective-permute-start.8 = (f32[256,512]{1,0:T(8,128)S(1)}, f32[256,512]{1,0:T(8,128)S(1)}, u32[]{:S(2)}, u32[]{:S(2)}) collective-permute-start(f32[256,512]{1,0:T(8,128)S(1)} %slice_bitcast_fusion.1), channel_id=1, source_target_pairs={{1,2},{2,1},{3,4},{4,3},{5,6},{6,5},{7,8},{8,7},{9,10},{10,9},{11,... | collective-permute-start | bytes 1572872 | tf_op jit(solution)/shard_map/ppermute | solution.py:80
  51.0 1.9 %collective-permute-start.7 = (f32[256,512]{1,0:T(8,128)S(1)}, f32[256,512]{1,0:T(8,128)S(1)}, u32[]{:S(2)}, u32[]{:S(2)}) collective-permute-start(f32[256,512]{1,0:T(8,128)S(1)} %multiply_add_fusion.5), channel_id=1, source_target_pairs={{1,2},{2,1},{3,4},{4,3},{5,6},{6,5},{7,8},{8,7},{9,10},{10,9},{11,... | collective-permute-start | bytes 1572872 | tf_op jit(solution)/shard_map/ppermute | solution.py:80
  52.9 0.8 fusion.26
  53.8 0.2 fusion.66
  53.9 9.7 %collective-permute-done.7 = f32[256,512]{1,0:T(8,128)S(1)} collective-permute-done((f32[256,512]{1,0:T(8,128)S(1)}, f32[256,512]{1,0:T(8,128)S(1)}, u32[]{:S(2)}, u32[]{:S(2)}) %collective-permute-start.7) | collective-permute-done | bytes 524320 | tf_op jit(solution)/shard_map/ppermute | solution.py:80
  63.6 0.2 multiply_add_fusion.4
  63.8 1.9 %collective-permute-start.9 = (f32[256,512]{1,0:T(8,128)S(1)}, f32[256,512]{1,0:T(8,128)S(1)}, u32[]{:S(2)}, u32[]{:S(2)}) collective-permute-start(f32[256,512]{1,0:T(8,128)S(1)} %multiply_add_fusion.4), channel_id=1, source_target_pairs={{0,1},{1,0},{2,3},{3,2},{4,5},{5,4},{6,7},{7,6},{8,9},{9,8},{10,11... | collective-permute-start | bytes 1572872 | tf_op jit(solution)/shard_map/ppermute | solution.py:83
  65.7 2.2 %weight_field.2 = f32[256,512]{1,0:T(8,128)S(1)} custom-call(s32[1,4096]{1,0:T(1,128)S(1)} %copy-done, f32[1,4096]{1,0:T(1,128)S(1)} %copy-done.1), custom_call_target="tpu_custom_call" | custom-call | flops 1610612736 | bytes 524288 | tf_op jit(solution)/shard_map/weight_field/pallas_call | solution.py:41
  67.9 2.2 %weight_field.3 = f32[256,512]{1,0:T(8,128)S(1)} custom-call(s32[1,4096]{1,0:T(1,128)S(1)} %copy-done, f32[1,4096]{1,0:T(1,128)S(1)} %copy-done.1), custom_call_target="tpu_custom_call" | custom-call | flops 1610612736 | bytes 524288 | tf_op jit(solution)/shard_map/weight_field/pallas_call | solution.py:41
  70.1 5.6 %collective-permute-start.10 = (f32[256,512]{1,0:T(8,128)S(1)}, f32[256,512]{1,0:T(8,128)S(1)}, u32[]{:S(2)}, u32[]{:S(2)}) collective-permute-start(f32[256,512]{1,0:T(8,128)S(1)} %multiply_add_fusion.4), channel_id=1, source_target_pairs={{1,2},{2,1},{3,4},{4,3},{5,6},{6,5},{7,8},{8,7},{9,10},{10,9},{11,... | collective-permute-start | bytes 1572872 | tf_op jit(solution)/shard_map/ppermute | solution.py:80
  75.7 0.8 fusion.40
  76.6 0.2 multiply_add_fusion.3
  76.7 6.0 %collective-permute-done.10 = f32[256,512]{1,0:T(8,128)S(1)} collective-permute-done((f32[256,512]{1,0:T(8,128)S(1)}, f32[256,512]{1,0:T(8,128)S(1)}, u32[]{:S(2)}, u32[]{:S(2)}) %collective-permute-start.10) | collective-permute-done | bytes 524320 | tf_op jit(solution)/shard_map/ppermute | solution.py:80
  82.7 0.3 fusion.75
  83.0 0.1 bitcast_multiply_fusion.7
  83.1 0.4 fusion.52
  83.5 1.9 %collective-permute-start.11 = (f32[256,512]{1,0:T(8,128)S(1)}, f32[256,512]{1,0:T(8,128)S(1)}, u32[]{:S(2)}, u32[]{:S(2)}) collective-permute-start(f32[256,512]{1,0:T(8,128)S(1)} %get-tuple-element.54), channel_id=1, source_target_pairs={{0,1},{1,0},{2,3},{3,2},{4,5},{5,4},{6,7},{7,6},{8,9},{9,8},{10,11... | collective-permute-start | bytes 1572872 | tf_op jit(solution)/shard_map/ppermute | solution.py:83
  85.4 5.6 %collective-permute-start.12 = (f32[256,512]{1,0:T(8,128)S(1)}, f32[256,512]{1,0:T(8,128)S(1)}, u32[]{:S(2)}, u32[]{:S(2)}) collective-permute-start(f32[256,512]{1,0:T(8,128)S(1)} %get-tuple-element.56), channel_id=1, source_target_pairs={{1,2},{2,1},{3,4},{4,3},{5,6},{6,5},{7,8},{8,7},{9,10},{10,9},{11,... | collective-permute-start | bytes 1572872 | tf_op jit(solution)/shard_map/ppermute | solution.py:80
  91.0 0.1 add.291
  91.1 0.1 mul.208
  91.2 6.8 %collective-permute-done.12 = f32[256,512]{1,0:T(8,128)S(1)} collective-permute-done((f32[256,512]{1,0:T(8,128)S(1)}, f32[256,512]{1,0:T(8,128)S(1)}, u32[]{:S(2)}, u32[]{:S(2)}) %collective-permute-start.12) | collective-permute-done | bytes 524320 | tf_op jit(solution)/shard_map/ppermute | solution.py:80
  98.0 0.1 add.292
  98.2 0.4 fusion.58
  98.6 1.9 %collective-permute-start.13 = (f32[256,512]{1,0:T(8,128)S(1)}, f32[256,512]{1,0:T(8,128)S(1)}, u32[]{:S(2)}, u32[]{:S(2)}) collective-permute-start(f32[256,512]{1,0:T(8,128)S(1)} %get-tuple-element.58), channel_id=1, source_target_pairs={{0,1},{1,0},{2,3},{3,2},{4,5},{5,4},{6,7},{7,6},{8,9},{9,8},{10,11... | collective-permute-start | bytes 1572872 | tf_op jit(solution)/shard_map/ppermute | solution.py:83
  100.5 5.6 %collective-permute-start.14 = (f32[256,512]{1,0:T(8,128)S(1)}, f32[256,512]{1,0:T(8,128)S(1)}, u32[]{:S(2)}, u32[]{:S(2)}) collective-permute-start(f32[256,512]{1,0:T(8,128)S(1)} %get-tuple-element.42), channel_id=1, source_target_pairs={{1,2},{2,1},{3,4},{4,3},{5,6},{6,5},{7,8},{8,7},{9,10},{10,9},{11,... | collective-permute-start | bytes 1572872 | tf_op jit(solution)/shard_map/ppermute | solution.py:80
  106.1 2.1 %collective-permute-start.15 = (f32[256,512]{1,0:T(8,128)S(1)}, f32[256,512]{1,0:T(8,128)S(1)}, u32[]{:S(2)}, u32[]{:S(2)}) collective-permute-start(f32[256,512]{1,0:T(8,128)S(1)} %mul.208), channel_id=1, source_target_pairs={{1,2},{2,1},{3,4},{4,3},{5,6},{6,5},{7,8},{8,7},{9,10},{10,9},{11,... | collective-permute-start | bytes 1572872 | tf_op jit(solution)/shard_map/ppermute | solution.py:80
  108.2 0.1 add.297
  108.3 0.1 mul.213
  108.4 4.7 %collective-permute-done.14 = f32[256,512]{1,0:T(8,128)S(1)} collective-permute-done((f32[256,512]{1,0:T(8,128)S(1)}, f32[256,512]{1,0:T(8,128)S(1)}, u32[]{:S(2)}, u32[]{:S(2)}) %collective-permute-start.14) | collective-permute-done | bytes 524320 | tf_op jit(solution)/shard_map/ppermute | solution.py:80
  113.1 0.3 multiply_multiply_fusion
  113.4 0.1 add.298
  113.5 0.2 multiply_add_fusion.2
  113.7 5.1 %collective-permute-done.15 = f32[256,512]{1,0:T(8,128)S(1)} collective-permute-done((f32[256,512]{1,0:T(8,128)S(1)}, f32[256,512]{1,0:T(8,128)S(1)}, u32[]{:S(2)}, u32[]{:S(2)}) %collective-permute-start.15) | collective-permute-done | bytes 524320 | tf_op jit(solution)/shard_map/ppermute | solution.py:80
  118.7 0.1 add.300
  118.8 0.1 bitcast_multiply_fusion.8
  118.9 0.3 fusion.64
  119.2 1.9 %collective-permute-start.16 = (f32[256,512]{1,0:T(8,128)S(1)}, f32[256,512]{1,0:T(8,128)S(1)}, u32[]{:S(2)}, u32[]{:S(2)}) collective-permute-start(f32[256,512]{1,0:T(8,128)S(1)} %get-tuple-element.72), channel_id=1, source_target_pairs={{0,1},{1,0},{2,3},{3,2},{4,5},{5,4},{6,7},{7,6},{8,9},{9,8},{10,11... | collective-permute-start | bytes 1572872 | tf_op jit(solution)/shard_map/ppermute | solution.py:83
  121.2 5.6 %collective-permute-start.17 = (f32[256,512]{1,0:T(8,128)S(1)}, f32[256,512]{1,0:T(8,128)S(1)}, u32[]{:S(2)}, u32[]{:S(2)}) collective-permute-start(f32[256,512]{1,0:T(8,128)S(1)} %mul.213), channel_id=1, source_target_pairs={{1,2},{2,1},{3,4},{4,3},{5,6},{6,5},{7,8},{8,7},{9,10},{10,9},{11,... | collective-permute-start | bytes 1572872 | tf_op jit(solution)/shard_map/ppermute | solution.py:80
  126.9 0.4 multiply_add_fusion.1
  127.3 6.5 %collective-permute-done.17 = f32[256,512]{1,0:T(8,128)S(1)} collective-permute-done((f32[256,512]{1,0:T(8,128)S(1)}, f32[256,512]{1,0:T(8,128)S(1)}, u32[]{:S(2)}, u32[]{:S(2)}) %collective-permute-start.17) | collective-permute-done | bytes 524320 | tf_op jit(solution)/shard_map/ppermute | solution.py:80
  133.8 1.0 multiply_add_fusion
  134.8 4.3 %all-to-all-start = ((f32[4,64,512]{2,1,0:T(8,128)}), f32[4,64,512]{2,1,0:T(8,128)S(1)}, u32[]{:S(2)}, u32[]{:S(2)}) async-start(f32[4,64,512]{2,1,0:T(8,128)} %bitcast.13), calls=%async_computation | async-start | bytes 1048576 | tf_op jit(solution)/shard_map/all_to_all | solution.py:157
  139.1 0.1 pad_slice_fusion.43
  139.2 8.2 %all-to-all-done = f32[4,64,512]{2,1,0:T(8,128)S(1)} async-done(((f32[4,64,512]{2,1,0:T(8,128)}), f32[4,64,512]{2,1,0:T(8,128)S(1)}, u32[]{:S(2)}, u32[]{:S(2)}) %all-to-all-start) | async-done | bytes 524320 | tf_op jit(solution)/shard_map/all_to_all | solution.py:157
  147.4 2.0 %collective-permute-start.18 = (f32[32,512]{1,0:T(8,128)S(1)}, f32[32,512]{1,0:T(8,128)S(1)}, u32[]{:S(2)}, u32[]{:S(2)}) collective-permute-start(f32[32,512]{1,0:T(8,128)S(1)} %get-tuple-element.75), channel_id=1, source_target_pairs={{0,64},{64,0},{128,192},{192,128},{256,320},{320,256},{384,448},{4... | collective-permute-start | bytes 196616 | tf_op jit(solution)/shard_map/ppermute | solution.py:169
  149.4 0.9 fusion.74
  150.4 7.8 %collective-permute-done.18 = f32[32,512]{1,0:T(8,128)S(1)} collective-permute-done((f32[32,512]{1,0:T(8,128)S(1)}, f32[32,512]{1,0:T(8,128)S(1)}, u32[]{:S(2)}, u32[]{:S(2)}) %collective-permute-start.18) | collective-permute-done | bytes 65568 | tf_op jit(solution)/shard_map/ppermute | solution.py:169
  158.2 0.6 add_bitcast_fusion
  (34 shorter events, 0.5 us)
Async XLA Ops:
  0.0 18.1 %copy-start.5 = (f32[1,4,1,256,512]{4,3,2,1,0:T(8,128)S(1)}, f32[1,4,1,256,512]{4,3,2,1,0:T(8,128)}, u32[]{:S(2)}) copy-start(f32[1,4,1,256,512]{4,3,2,1,0:T(8,128)} %param.6) | copy-start | bytes 6291460
  0.0 22.0 %copy-start.2 = (f32[1,256,512]{2,1,0:T(8,128)S(1)}, f32[1,256,512]{2,1,0:T(8,128)}, u32[]{:S(2)}) copy-start(f32[1,256,512]{2,1,0:T(8,128)} %param.9) | copy-start | bytes 1572868
  0.0 18.2 %collective-permute-start = (f32[4,256,512]{2,1,0:T(8,128)}, f32[4,256,512]{2,1,0:T(8,128)S(1)}, u32[]{:S(2)}, u32[]{:S(2)}) collective-permute-start(f32[4,256,512]{2,1,0:T(8,128)} %bitcast.77), channel_id=1, source_target_pairs={{0,1},{1,0},{2,3},{3,2},{4,5},{5,4},{6,7},{7,6},{8,9},{9,8},{10,11... | collective-permute-start | bytes 6291464 | tf_op jit(solution)/shard_map/ppermute | solution.py:83
  3.3 18.7 %collective-permute-start.1 = (f32[256,512]{1,0:T(8,128)S(1)}, f32[256,512]{1,0:T(8,128)S(1)}, u32[]{:S(2)}, u32[]{:S(2)}) collective-permute-start(f32[256,512]{1,0:T(8,128)S(1)} %slice_bitcast_fusion.7), channel_id=1, source_target_pairs={{1,2},{2,1},{3,4},{4,3},{5,6},{6,5},{7,8},{8,7},{9,10},{10,9},{11,... | collective-permute-start | bytes 1572872 | tf_op jit(solution)/shard_map/ppermute | solution.py:80
  16.2 15.6 %collective-permute-start.2 = (f32[256,512]{1,0:T(8,128)S(1)}, f32[256,512]{1,0:T(8,128)S(1)}, u32[]{:S(2)}, u32[]{:S(2)}) collective-permute-start(f32[256,512]{1,0:T(8,128)S(1)} %slice_bitcast_fusion.5), channel_id=1, source_target_pairs={{1,2},{2,1},{3,4},{4,3},{5,6},{6,5},{7,8},{8,7},{9,10},{10,9},{11,... | collective-permute-start | bytes 1572872 | tf_op jit(solution)/shard_map/ppermute | solution.py:80
  18.5 13.3 %copy-start.3 = (f32[1,256,512]{2,1,0:T(8,128)S(1)}, f32[1,256,512]{2,1,0:T(8,128)}, u32[]{:S(2)}) copy-start(f32[1,256,512]{2,1,0:T(8,128)} %param.7) | copy-start | bytes 1572868
  18.5 13.3 %copy-start.4 = (f32[1,256,512]{2,1,0:T(8,128)S(1)}, f32[1,256,512]{2,1,0:T(8,128)}, u32[]{:S(2)}) copy-start(f32[1,256,512]{2,1,0:T(8,128)} %param.8) | copy-start | bytes 1572868
  22.1 10.7 %collective-permute-start.3 = (f32[256,512]{1,0:T(8,128)S(1)}, f32[256,512]{1,0:T(8,128)S(1)}, u32[]{:S(2)}, u32[]{:S(2)}) collective-permute-start(f32[256,512]{1,0:T(8,128)S(1)} %get-tuple-element.45), channel_id=1, source_target_pairs={{0,1},{1,0},{2,3},{3,2},{4,5},{5,4},{6,7},{7,6},{8,9},{9,8},{10,11... | collective-permute-start | bytes 1572872 | tf_op jit(solution)/shard_map/ppermute | solution.py:83
  24.1 28.8 %collective-permute-start.5 = (f32[288,512]{1,0:T(8,128)S(1)}, f32[288,512]{1,0:T(8,128)S(1)}, u32[]{:S(2)}, u32[]{:S(2)}) collective-permute-start(f32[288,512]{1,0:T(8,128)S(1)} %pad_maximum_fusion), channel_id=1, source_target_pairs={{1,2},{2,1},{3,4},{4,3},{5,6},{6,5},{7,8},{8,7},{9,10},{10,9},{11,... | collective-permute-start | bytes 1769480 | tf_op jit(solution)/shard_map/ppermute | solution.py:80
  29.9 13.2 %collective-permute-start.4 = (f32[256,512]{1,0:T(8,128)S(1)}, f32[256,512]{1,0:T(8,128)S(1)}, u32[]{:S(2)}, u32[]{:S(2)}) collective-permute-start(f32[256,512]{1,0:T(8,128)S(1)} %get-tuple-element.45), channel_id=1, source_target_pairs={{1,2},{2,1},{3,4},{4,3},{5,6},{6,5},{7,8},{8,7},{9,10},{10,9},{11,... | collective-permute-start | bytes 1572872 | tf_op jit(solution)/shard_map/ppermute | solution.py:80
  43.3 10.5 %collective-permute-start.6 = (f32[288,512]{1,0:T(8,128)S(1)}, f32[288,512]{1,0:T(8,128)S(1)}, u32[]{:S(2)}, u32[]{:S(2)}) collective-permute-start(f32[288,512]{1,0:T(8,128)S(1)} %pad_maximum_fusion.1), channel_id=1, source_target_pairs={{0,1},{1,0},{2,3},{3,2},{4,5},{5,4},{6,7},{7,6},{8,9},{9,8},{10,11... | collective-permute-start | bytes 1769480 | tf_op jit(solution)/shard_map/ppermute | solution.py:83
  45.2 30.5 %collective-permute-start.8 = (f32[256,512]{1,0:T(8,128)S(1)}, f32[256,512]{1,0:T(8,128)S(1)}, u32[]{:S(2)}, u32[]{:S(2)}) collective-permute-start(f32[256,512]{1,0:T(8,128)S(1)} %slice_bitcast_fusion.1), channel_id=1, source_target_pairs={{1,2},{2,1},{3,4},{4,3},{5,6},{6,5},{7,8},{8,7},{9,10},{10,9},{11,... | collective-permute-start | bytes 1572872 | tf_op jit(solution)/shard_map/ppermute | solution.py:80
  51.0 12.6 %collective-permute-start.7 = (f32[256,512]{1,0:T(8,128)S(1)}, f32[256,512]{1,0:T(8,128)S(1)}, u32[]{:S(2)}, u32[]{:S(2)}) collective-permute-start(f32[256,512]{1,0:T(8,128)S(1)} %multiply_add_fusion.5), channel_id=1, source_target_pairs={{1,2},{2,1},{3,4},{4,3},{5,6},{6,5},{7,8},{8,7},{9,10},{10,9},{11,... | collective-permute-start | bytes 1572872 | tf_op jit(solution)/shard_map/ppermute | solution.py:80
  53.7 10.0 %copy-start.6 = (f32[288,512]{1,0:T(8,128)}, f32[288,512]{1,0:T(8,128)S(1)}, u32[]{:S(2)}) copy-start(f32[288,512]{1,0:T(8,128)S(1)} %collective-permute-done.6) | copy-start | bytes 1769476
  53.7 12.0 %copy-start = (s32[1,4096]{1,0:T(1,128)S(1)}, s32[1,4096]{1,0:T(1,128)}, u32[]{:S(2)}) copy-start(s32[1,4096]{1,0:T(1,128)} %index_ref.3) | copy-start | bytes 49156
  53.8 12.0 %copy-start.1 = (f32[1,4096]{1,0:T(1,128)S(1)}, f32[1,4096]{1,0:T(1,128)}, u32[]{:S(2)}) copy-start(f32[1,4096]{1,0:T(1,128)} %weight_ref.3) | copy-start | bytes 49156
  63.8 12.8 %collective-permute-start.9 = (f32[256,512]{1,0:T(8,128)S(1)}, f32[256,512]{1,0:T(8,128)S(1)}, u32[]{:S(2)}, u32[]{:S(2)}) collective-permute-start(f32[256,512]{1,0:T(8,128)S(1)} %multiply_add_fusion.4), channel_id=1, source_target_pairs={{0,1},{1,0},{2,3},{3,2},{4,5},{5,4},{6,7},{7,6},{8,9},{9,8},{10,11... | collective-permute-start | bytes 1572872 | tf_op jit(solution)/shard_map/ppermute | solution.py:83
  70.1 12.6 %collective-permute-start.10 = (f32[256,512]{1,0:T(8,128)S(1)}, f32[256,512]{1,0:T(8,128)S(1)}, u32[]{:S(2)}, u32[]{:S(2)}) collective-permute-start(f32[256,512]{1,0:T(8,128)S(1)} %multiply_add_fusion.4), channel_id=1, source_target_pairs={{1,2},{2,1},{3,4},{4,3},{5,6},{6,5},{7,8},{8,7},{9,10},{10,9},{11,... | collective-permute-start | bytes 1572872 | tf_op jit(solution)/shard_map/ppermute | solution.py:80
  83.5 7.6 %collective-permute-start.11 = (f32[256,512]{1,0:T(8,128)S(1)}, f32[256,512]{1,0:T(8,128)S(1)}, u32[]{:S(2)}, u32[]{:S(2)}) collective-permute-start(f32[256,512]{1,0:T(8,128)S(1)} %get-tuple-element.54), channel_id=1, source_target_pairs={{0,1},{1,0},{2,3},{3,2},{4,5},{5,4},{6,7},{7,6},{8,9},{9,8},{10,11... | collective-permute-start | bytes 1572872 | tf_op jit(solution)/shard_map/ppermute | solution.py:83
  85.4 12.6 %collective-permute-start.12 = (f32[256,512]{1,0:T(8,128)S(1)}, f32[256,512]{1,0:T(8,128)S(1)}, u32[]{:S(2)}, u32[]{:S(2)}) collective-permute-start(f32[256,512]{1,0:T(8,128)S(1)} %get-tuple-element.56), channel_id=1, source_target_pairs={{1,2},{2,1},{3,4},{4,3},{5,6},{6,5},{7,8},{8,7},{9,10},{10,9},{11,... | collective-permute-start | bytes 1572872 | tf_op jit(solution)/shard_map/ppermute | solution.py:80
  98.6 9.6 %collective-permute-start.13 = (f32[256,512]{1,0:T(8,128)S(1)}, f32[256,512]{1,0:T(8,128)S(1)}, u32[]{:S(2)}, u32[]{:S(2)}) collective-permute-start(f32[256,512]{1,0:T(8,128)S(1)} %get-tuple-element.58), channel_id=1, source_target_pairs={{0,1},{1,0},{2,3},{3,2},{4,5},{5,4},{6,7},{7,6},{8,9},{9,8},{10,11... | collective-permute-start | bytes 1572872 | tf_op jit(solution)/shard_map/ppermute | solution.py:83
  100.5 12.6 %collective-permute-start.14 = (f32[256,512]{1,0:T(8,128)S(1)}, f32[256,512]{1,0:T(8,128)S(1)}, u32[]{:S(2)}, u32[]{:S(2)}) collective-permute-start(f32[256,512]{1,0:T(8,128)S(1)} %get-tuple-element.42), channel_id=1, source_target_pairs={{1,2},{2,1},{3,4},{4,3},{5,6},{6,5},{7,8},{8,7},{9,10},{10,9},{11,... | collective-permute-start | bytes 1572872 | tf_op jit(solution)/shard_map/ppermute | solution.py:80
  106.1 12.6 %collective-permute-start.15 = (f32[256,512]{1,0:T(8,128)S(1)}, f32[256,512]{1,0:T(8,128)S(1)}, u32[]{:S(2)}, u32[]{:S(2)}) collective-permute-start(f32[256,512]{1,0:T(8,128)S(1)} %mul.208), channel_id=1, source_target_pairs={{1,2},{2,1},{3,4},{4,3},{5,6},{6,5},{7,8},{8,7},{9,10},{10,9},{11,... | collective-permute-start | bytes 1572872 | tf_op jit(solution)/shard_map/ppermute | solution.py:80
  119.2 7.5 %collective-permute-start.16 = (f32[256,512]{1,0:T(8,128)S(1)}, f32[256,512]{1,0:T(8,128)S(1)}, u32[]{:S(2)}, u32[]{:S(2)}) collective-permute-start(f32[256,512]{1,0:T(8,128)S(1)} %get-tuple-element.72), channel_id=1, source_target_pairs={{0,1},{1,0},{2,3},{3,2},{4,5},{5,4},{6,7},{7,6},{8,9},{9,8},{10,11... | collective-permute-start | bytes 1572872 | tf_op jit(solution)/shard_map/ppermute | solution.py:83
  121.2 12.6 %collective-permute-start.17 = (f32[256,512]{1,0:T(8,128)S(1)}, f32[256,512]{1,0:T(8,128)S(1)}, u32[]{:S(2)}, u32[]{:S(2)}) collective-permute-start(f32[256,512]{1,0:T(8,128)S(1)} %mul.213), channel_id=1, source_target_pairs={{1,2},{2,1},{3,4},{4,3},{5,6},{6,5},{7,8},{8,7},{9,10},{10,9},{11,... | collective-permute-start | bytes 1572872 | tf_op jit(solution)/shard_map/ppermute | solution.py:80
  134.8 12.6 %all-to-all-start = ((f32[4,64,512]{2,1,0:T(8,128)}), f32[4,64,512]{2,1,0:T(8,128)S(1)}, u32[]{:S(2)}, u32[]{:S(2)}) async-start(f32[4,64,512]{2,1,0:T(8,128)} %bitcast.13), calls=%async_computation | async-start | bytes 1048576 | tf_op jit(solution)/shard_map/all_to_all | solution.py:157
  147.4 10.8 %collective-permute-start.18 = (f32[32,512]{1,0:T(8,128)S(1)}, f32[32,512]{1,0:T(8,128)S(1)}, u32[]{:S(2)}, u32[]{:S(2)}) collective-permute-start(f32[32,512]{1,0:T(8,128)S(1)} %get-tuple-element.75), channel_id=1, source_target_pairs={{0,64},{64,0},{128,192},{192,128},{256,320},{320,256},{384,448},{4... | collective-permute-start | bytes 196616 | tf_op jit(solution)/shard_map/ppermute | solution.py:169
